TPU v7x, 256 devices: a whole 4x4x8 slice. The times are simulated.
256 devices in a mesh: hour: 16 (over y, x_lo, core), lat: 2 (over x_hi), lon: 8 (over z).
Axes of the slice: x: 4 (x_hi: 2, x_lo: 2; x = x_hi * 2 + x_lo), y: 4, z: 8, core: 2. Of those that a mesh axis runs over, the one named last changes fastest.
Arguments:
- precip: float32 [16, 1024, 4096], P('hour', 'lat', 'lon'), may hold values from 0.05 to 5
- scaling: float32 [16, 1024, 4096], P('hour', 'lat', 'lon'), may hold values from 0.5 to 2
- hour_weight: float32 [16], P('hour'), may hold values from 0.03 to 0.3
- cotangent: float32 [16, 1024, 4096], P('hour', 'lat', 'lon'), may hold values from -6 to 6
Outputs:
- grad_precip: float32 [16, 1024, 4096], P('hour', 'lat', 'lon')
- grad_scaling: float32 [16, 1024, 4096], P('hour', 'lat', 'lon')
All inputs are finite; a program needn't handle non-finite values.
Results may differ from a plain program's by a relative error of at most 0.00012.
Values sent between devices are 32-bit elements; how exact they have to be, the bound alone decides.
No kernel may reach another device: no remote copies, remote signals or barrier semaphores. Data moves between devices by JAX's collectives and lax.ppermute only.
A program may use at most 64 MiB of HBM per device.

v0:
```python
import numpy as np
import jax
import jax.numpy as jnp
from jax import lax
from jax.experimental import pallas as pl
from jax.experimental.pallas import tpu as pltpu
from jax.sharding import Mesh
from jax.sharding import PartitionSpec as P


RADIUS = 8
HOUR = ("hour_0", "hour_1", "hour_2")
PHI = 0.8
SPREAD = 50.0

ROWS = 512
COLS = 512
WIDE = 640
EDGE = 128
TALL = ROWS + 2 * RADIUS
TALLER = ROWS + 4 * RADIUS
BLOCK = TALL // 3
PIECES = 16
CHIPS = 8
ORDER = (5, 7, 3, 1, 4, 2, 6)
PIECE = ROWS // PIECES
STRIP = 3 * RADIUS
F32 = jnp.float32
BF16 = jnp.bfloat16


def taps_of(spacing):
    offsets = np.arange(-RADIUS, RADIUS + 1).astype(np.float64)
    total = np.sum(np.exp(-offsets * offsets / SPREAD))
    return np.where(np.abs(spacing) <= RADIUS, np.exp(-spacing * spacing / SPREAD) / total, 0.0)


def halves(matrix):
    matrix = matrix.astype(np.float32)
    high = matrix.astype(jnp.bfloat16)
    low = (matrix - high.astype(np.float32)).astype(jnp.bfloat16)
    return jnp.asarray(high), jnp.asarray(low)


def row_band(size):
    outer = np.arange(size)[:, None]
    inner = np.arange(size + 2 * RADIUS)[None, :]
    return halves(taps_of((inner - outer - RADIUS).astype(np.float64)))


def edge_bands():
    outer = np.arange(2 * RADIUS)[:, None]
    inner = np.arange(2 * RADIUS)[None, :]
    low = taps_of((inner - outer - RADIUS).astype(np.float64))
    high = taps_of((inner - outer + RADIUS).astype(np.float64))
    stacks = np.zeros((2, 48, 48))
    for lat, along in enumerate((high, low)):
        for k, band in enumerate((along, low, high)):
            stacks[lat, 16 * k : 16 * (k + 1), 16 * k : 16 * (k + 1)] = band
    return halves(stacks)


def col_band():
    outer = np.arange(2 * EDGE)[None, :]
    inner = np.arange(4 * EDGE)[:, None]
    return halves(taps_of((inner - EDGE - outer).astype(np.float64)))


def split(x):
    high = x.astype(BF16)
    return high, (x - high.astype(F32)).astype(BF16)


def dot(a, b):
    return jnp.dot(a, b, preferred_element_type=F32)


def rows_pass(x, high, low):
    xh, xl = split(x)
    return dot(high[...], xh) + (dot(low[...], xh) + dot(high[...], xl))


def cols_piece(rh, rl, ch, cl, spans, count):
    total = None
    for lo, hi, at in spans:
        high, low = ch[at : at + hi - lo, 0:count], cl[at : at + hi - lo, 0:count]
        part = dot(rh[:, lo:hi], high) + (dot(rl[:, lo:hi], high) + dot(rh[:, lo:hi], low))
        total = part if total is None else total + part
    return total


def cols_pass(r, ch, cl, halo):
    rh, rl = split(r)
    pieces = [
        cols_piece(rh, rl, ch, cl, ((512, 640, 0), (0, 384, 128)), 256),
        cols_piece(rh, rl, ch, cl, ((128, 640, 0),), 256),
    ]
    if halo:
        pieces.append(cols_piece(rh, rl, ch, cl, ((384, 640, 0), (0, 128, 256)), 128))
    return jnp.concatenate(pieces, axis=1)


def valid_part(start, count, lat):
    row = lax.broadcasted_iota(jnp.int32, (count, WIDE), 0) + start
    lane = lax.broadcasted_iota(jnp.int32, (count, WIDE), 1)
    inside = (row >= jnp.where(lat == 0, RADIUS, 0)) & (
        row < jnp.where(lat == 0, TALL, TALL - RADIUS)
    )
    return inside & ((lane < COLS + RADIUS) | (lane >= WIDE - RADIUS))


def my_lat():
    return lax.axis_index("lat")


def my_parity():
    return lax.axis_index("lon") & 1


def fill_edges(ext, reach, rows_in, even, odd, side):
    lat, parity = my_lat(), my_parity()
    side[...] = jnp.zeros((EDGE, WIDE), F32)
    side[0:reach, :] = jnp.where(parity == 0, even, odd)
    side[EDGE - reach : EDGE, :] = jnp.where(parity == 0, odd, even)
    flat = jnp.transpose(side[...])
    corner = flat[ROWS : ROWS + reach]
    ext[reach : reach + ROWS, COLS:WIDE] = flat[0:ROWS]
    ext[0:reach, 0:COLS] = jnp.where(lat == 1, rows_in, 0.0)
    ext[0:reach, COLS:WIDE] = jnp.where(lat == 1, corner, 0.0)
    ext[reach + ROWS : 2 * reach + ROWS, 0:COLS] = jnp.where(lat == 0, rows_in, 0.0)
    ext[reach + ROWS : 2 * reach + ROWS, COLS:WIDE] = jnp.where(lat == 0, corner, 0.0)


def column_strips(reach, first_block, last_block, rows_in, parity):
    spare = jnp.zeros((EDGE - reach, EDGE), F32)
    left = jnp.transpose(jnp.concatenate([first_block, rows_in[:, 0:EDGE], spare], axis=0))
    right = jnp.transpose(
        jnp.concatenate([last_block, rows_in[:, COLS - EDGE : COLS], spare], axis=0)
    )
    left, right = left[0:reach], right[EDGE - reach : EDGE]
    return jnp.where(parity == 0, right, left), jnp.where(parity == 0, left, right)


def lat_kernel(scaling, precip, to_lat, sems):
    wide, narrow = 2 * RADIUS, RADIUS
    keep = 1 - my_lat()
    at = pl.multiple_of(keep * (ROWS - wide), 8)
    near = pl.multiple_of(keep * (ROWS - narrow), 8)
    copies = (
        pltpu.make_async_copy(scaling.at[pl.ds(at, wide), :], to_lat.at[0:wide, :], sems.at[0]),
        pltpu.make_async_copy(
            precip.at[pl.ds(near, narrow), :], to_lat.at[wide:STRIP, :], sems.at[1]
        ),
    )
    for copy in copies:
        copy.start()
    for copy in copies:
        copy.wait()


def in_hbm(x):
    return pltpu.with_memory_space_constraint(x, pltpu.HBM)


def lat_strip(scaling, precip):
    return pl.pallas_call(
        lat_kernel,
        out_shape=jax.ShapeDtypeStruct((STRIP, COLS), F32),
        in_specs=[pl.BlockSpec(memory_space=pltpu.HBM)] * 2,
        out_specs=pl.BlockSpec(memory_space=pltpu.VMEM),
        scratch_shapes=[pltpu.SemaphoreType.DMA((2,))],
        compiler_params=pltpu.CompilerParams(vmem_limit_bytes=2 << 20),
        name="lat_edges",
    )(in_hbm(scaling), in_hbm(precip))


def lon_kernel(scaling, precip, lat_in, to_even, to_odd):
    wide, narrow = 2 * RADIUS, RADIUS
    to_even[0:wide, :], to_odd[0:wide, :] = column_strips(
        wide, scaling[:, 0:EDGE], scaling[:, COLS - EDGE : COLS], lat_in[0:wide, :], my_parity()
    )
    to_even[wide:STRIP, :], to_odd[wide:STRIP, :] = column_strips(
        narrow, precip[:, 0:EDGE], precip[:, COLS - EDGE : COLS], lat_in[wide:STRIP, :], my_parity()
    )


def forward_kernel(
    weight, scaling, precip, upstream, lat_in, even, odd, rh3, rl3, rh4, rl4, ch, cl,
    slope, share, second, logs, keep, give, sx, px, side, lifted,
):
    lat = my_lat()
    core = lax.axis_index("hour_2")
    wide, narrow = 2 * RADIUS, RADIUS
    sx[wide : wide + ROWS, 0:COLS] = scaling[...]
    px[narrow : narrow + ROWS, 0:COLS] = precip[...]
    fill_edges(sx, wide, lat_in[0:wide, :], even[0:wide, :], odd[0:wide, :], side)
    fill_edges(px, narrow, lat_in[wide:STRIP, :], even[wide:STRIP, :], odd[wide:STRIP, :], side)
    for i in range(3):
        at = BLOCK * i
        r = rows_pass(sx[at : at + BLOCK + 2 * RADIUS, :], rh3, rl3)
        a = cols_pass(r, ch, cl, True)
        rain = px[at : at + BLOCK, :]
        inside = valid_part(at, BLOCK, lat)
        u = jnp.where(inside, jnp.exp(PHI * jnp.log(rain / a)), 0.0)
        lifted[at : at + BLOCK, :] = u
        slope[at : at + BLOCK, :] = jnp.where(inside, -PHI * u / a, 0.0)
        lo, hi = max(at, RADIUS), min(at + BLOCK, RADIUS + ROWS)
        here = slice(lo - RADIUS, hi - RADIUS)
        share[here, :] = PHI * u[lo - at : hi - at, 0:COLS] / rain[lo - at : hi - at, 0:COLS]
    for i in range(4):
        at = EDGE * i
        r = rows_pass(lifted[at : at + EDGE + 2 * RADIUS, :], rh4, rl4)
        b = cols_pass(r, ch, cl, False)
        logb = jnp.log(b)
        parts = (weight[0] * logb, upstream[at : at + EDGE, :] * jnp.exp(-PHI * logb))
        for j in range(COLS // EDGE):
            lanes = slice(EDGE * j, EDGE * (j + 1))
            for q in range(EDGE // PIECE):
                rows = slice(PIECE * q, PIECE * (q + 1))
                to = slice(PIECE * j, PIECE * (j + 1))
                second[i * (EDGE // PIECE) + q, to, :] = b[rows, lanes]
                logs[i * (EDGE // PIECE) + q, to, :] = logb[rows, lanes]
            for c in range(2):
                first = slice(2 * PIECE * c, 2 * PIECE * c + PIECE)
                other = slice(2 * PIECE * c + PIECE, 2 * PIECE * (c + 1))
                for k, part in enumerate(parts):
                    to = slice(EDGE * k + PIECE * j, EDGE * k + PIECE * (j + 1))
                    x, y = part[first, lanes], part[other, lanes]
                    keep[2 * i + c, to, :] = jnp.where(core == 0, x, y)
                    give[2 * i + c, to, :] = jnp.where(core == 0, y, x)


def my_chip():
    return lax.axis_index("hour_0") * 2 + lax.axis_index("hour_1")


def pair_kernel(keep, given, *outs):
    chip = my_chip()
    for k, out in enumerate(outs):
        out[...] = keep[chip ^ k] + given[chip ^ k]


def owner_kernel(*refs):
    sums, out = refs[:CHIPS], refs[CHIPS]

    def total(start):
        x = sums[0][start : start + EDGE, :]
        for part in sums[1:]:
            x = x + part[start : start + EDGE, :]
        return x

    logq = total(0)
    out[0:EDGE, :] = logq
    out[EDGE : 2 * EDGE, :] = PHI * jnp.exp(PHI * logq) * total(EDGE)


def gather_kernel(*refs):
    chip = my_chip()
    out = refs[CHIPS]
    for k in range(CHIPS):
        out[chip ^ k] = refs[k][...]


def db_kernel(weight, mine, theirs, upstream, second, logs, pieces):
    core = lax.axis_index("hour_2")
    for p in range(PIECES):
        here = core == p % 2
        for j in range(COLS // EDGE):
            rows = slice(PIECE * j, PIECE * (j + 1))
            low = slice(EDGE + PIECE * j, EDGE + PIECE * (j + 1))
            logq = jnp.where(here, mine[p // 2, rows, :], theirs[p // 2, rows, :])
            dlogq = jnp.where(here, mine[p // 2, low, :], theirs[p // 2, low, :])
            own = upstream[PIECE * p : PIECE * (p + 1), EDGE * j : EDGE * (j + 1)]
            term = PHI * own * jnp.exp(PHI * (logq - logs[p, rows, :]))
            pieces[p, rows, :] = (weight[0] * dlogq - term) / second[p, rows, :]


def tile_column(pieces, j):
    return jnp.concatenate(
        [pieces[p, PIECE * j : PIECE * (j + 1), :] for p in range(PIECES)], axis=0
    )


def back_lat_kernel(pieces, to_lat):
    wide = 2 * RADIUS
    for j in range(COLS // EDGE):
        to_lat[:, EDGE * j : EDGE * (j + 1)] = jnp.where(
            my_lat() == 0,
            pieces[PIECES - 1, PIECE * (j + 1) - wide : PIECE * (j + 1), :],
            pieces[0, PIECE * j : PIECE * j + wide, :],
        )


def back_lon_kernel(pieces, lat_in, to_even, to_odd):
    to_even[...], to_odd[...] = column_strips(
        2 * RADIUS, tile_column(pieces, 0), tile_column(pieces, COLS // EDGE - 1), lat_in[...],
        my_parity(),
    )


def coefficient_strips(slope, share, slope_edge, share_edge):
    wide = 2 * RADIUS
    top = my_lat() == 1
    nothing = jnp.zeros((RADIUS, COLS), F32)
    first, last = slice(0, EDGE), slice(COLS - EDGE, COLS)

    def turned(block):
        gap = jnp.zeros((WIDE - TALL, EDGE), F32)
        return jnp.transpose(jnp.concatenate([block[RADIUS:TALL], gap, block[0:RADIUS]], axis=0))

    near = lax.broadcasted_iota(jnp.int32, (TALL, EDGE), 1) < EDGE // 2
    tile = turned(jnp.where(near, slope[:, first], slope[:, last]))
    halo = turned(slope[:, COLS:WIDE])
    slope_edge[0:wide, :] = jnp.where(top, slope[0:wide, :], slope[TALL - wide : TALL, :])
    slope_edge[16:24, :] = halo[EDGE - RADIUS : EDGE]
    slope_edge[24:32, :] = tile[0:RADIUS]
    slope_edge[32:40, :] = tile[EDGE - RADIUS : EDGE]
    slope_edge[40:48, :] = halo[0:RADIUS]
    tile = jnp.transpose(jnp.where(near[0:ROWS], share[:, first], share[:, last]))
    share_edge[...] = jnp.zeros((48, WIDE), F32)
    share_edge[0:RADIUS, 0:COLS] = jnp.where(top, nothing, share[ROWS - RADIUS : ROWS, :])
    share_edge[RADIUS:wide, 0:COLS] = jnp.where(top, share[0:RADIUS, :], nothing)
    share_edge[24:32, 0:COLS] = tile[0:RADIUS]
    share_edge[32:40, 0:COLS] = tile[EDGE - RADIUS : EDGE]


def back_first_kernel(
    pieces, slope, share, rh3, rl3, ch, cl, grad_precip, sloped, slope_edge, share_edge, dx
):
    coefficient_strips(slope, share, slope_edge, share_edge)
    wide = 2 * RADIUS
    dx[0:wide, :] = jnp.zeros((wide, COLS), F32)
    dx[wide + ROWS : TALLER, :] = jnp.zeros((wide, COLS), F32)
    for p in range(PIECES):
        for j in range(COLS // EDGE):
            dx[wide + PIECE * p : wide + PIECE * (p + 1), EDGE * j : EDGE * (j + 1)] = pieces[
                p, PIECE * j : PIECE * (j + 1), :
            ]
    for i in range(3):
        at = BLOCK * i
        rh, rl = split(rows_pass(dx[at : at + BLOCK + 2 * RADIUS, :], rh3, rl3))
        du = jnp.concatenate(
            [
                cols_piece(rh, rl, ch, cl, ((0, 384, 128),), 256),
                cols_piece(rh, rl, ch, cl, ((128, 512, 0),), 256),
                cols_piece(rh, rl, ch, cl, ((384, 512, 0), (0, 128, 256)), 128),
            ],
            axis=1,
        )
        sloped[at : at + BLOCK, :] = slope[at : at + BLOCK, :] * du
        lo, hi = max(at, RADIUS), min(at + BLOCK, RADIUS + ROWS)
        here = slice(lo - RADIUS, hi - RADIUS)
        grad_precip[here, :] = share[here, :] * du[lo - at : hi - at, 0:COLS]


def back_second_kernel(sloped, rh4, rl4, ch, cl, grad_scaling):
    for i in range(4):
        at = EDGE * i
        r = rows_pass(sloped[at : at + EDGE + 2 * RADIUS, :], rh4, rl4)
        grad_scaling[at : at + EDGE, :] = cols_pass(r, ch, cl, False)


def around_pass(x):
    taps = taps_of(np.arange(RADIUS + 1).astype(np.float64))
    total = float(taps[0]) * x
    for d in range(1, RADIUS + 1):
        total += float(taps[d]) * (pltpu.roll(x, d, 1) + pltpu.roll(x, WIDE - d, 1))
    return total


def back_halo_kernel(
    lat_in, even, odd, slope_edge, share_edge, precip_part, scaling_part, dh, dl,
    precip_out, scaling_out, strips, square, flat, precip_edge, scaling_edge, middle, sems,
):
    wide = 2 * RADIUS
    lat, parity = my_lat(), my_parity()
    top = lat == 1
    inner = slice(EDGE, COLS - EDGE)
    last = slice(COLS - EDGE, COLS)
    copies = []

    def sent(src, dst):
        copies.append(pltpu.make_async_copy(src, dst, sems.at[len(copies)]))
        copies[-1].start()

    for part, out in ((precip_part, precip_out), (scaling_part, scaling_out)):
        sent(part.at[wide : ROWS - wide, inner], out.at[wide : ROWS - wide, inner])

    right = jnp.where(parity == 0, even[...], odd[...])
    left = jnp.where(parity == 0, odd[...], even[...])
    square[...] = jnp.zeros((EDGE, EDGE), F32)
    square[0:wide, :] = right[:, COLS:WIDE]
    square[EDGE - wide : EDGE, :] = left[:, COLS:WIDE]
    strips[...] = jnp.zeros((48, WIDE), F32)
    strips[0:16, 0:COLS] = lat_in[...]
    strips[0:16, COLS:WIDE] = jnp.transpose(square[...])[0:wide]
    strips[16:32, 0:COLS] = left[:, 0:COLS]
    strips[32:48, 0:COLS] = right[:, 0:COLS]
    band_h, band_l = dh[lat], dl[lat]

    def smoothed(x):
        xh, xl = split(x)
        return around_pass(dot(band_h, xh) + (dot(band_l, xh) + dot(band_h, xl)))

    du = smoothed(strips[...])
    precip_more = share_edge[...] * du
    scaling_more = smoothed(slope_edge[...] * du)
    nothing = jnp.zeros((RADIUS, COLS), F32)
    near = lax.broadcasted_iota(jnp.int32, (ROWS, EDGE), 1) < EDGE // 2

    def finished(k, part, out, edges, reach, low, high, first, final):
        flat[...] = jnp.zeros((EDGE, ROWS), F32)
        flat[0:reach, :] = low
        flat[EDGE - reach : EDGE, :] = high
        turned = jnp.transpose(flat[...])
        middle[2 * k] = part[0:wide, inner] + first[:, inner]
        middle[2 * k + 1] = part[ROWS - wide : ROWS, inner] + final[:, inner]
        sent(middle.at[2 * k], out.at[0:wide, inner])
        sent(middle.at[2 * k + 1], out.at[ROWS - wide : ROWS, inner])
        edges[:, 0:EDGE] = part[:, 0:EDGE] + jnp.where(near, turned, 0.0)
        edges[:, EDGE : 2 * EDGE] = part[:, last] + jnp.where(near, 0.0, turned)
        for q, lanes in enumerate((slice(0, EDGE), last)):
            mine = slice(EDGE * q, EDGE * (q + 1))
            edges[0:wide, mine] += first[:, lanes]
            edges[ROWS - wide : ROWS, mine] += final[:, lanes]
            sent(edges.at[:, mine], out.at[:, lanes])

    finished(
        0, precip_part, precip_out, precip_edge, RADIUS,
        precip_more[24:32, 0:COLS], precip_more[32:40, 0:COLS],
        jnp.concatenate([precip_more[RADIUS:wide, 0:COLS], nothing], axis=0),
        jnp.concatenate([nothing, precip_more[0:RADIUS, 0:COLS]], axis=0),
    )
    added = scaling_more[0:wide, 0:COLS]
    finished(
        1, scaling_part, scaling_out, scaling_edge, wide,
        scaling_more[16:32, 0:COLS], scaling_more[32:48, 0:COLS],
        jnp.where(top, added, 0.0), jnp.where(top, 0.0, added),
    )
    for copy in copies:
        copy.wait()


def in_vmem(*shapes):
    return [pltpu.VMEM(shape, F32) for shape in shapes]


def call(
    kernel, args, outs, scratch=(), scalars=0, flops=0, room=4 << 20, copies=0,
    out_hbm=False,
):
    size = sum(4 * a.size for a in args) + sum(4 * int(np.prod(o)) for o in outs)
    where = pltpu.HBM if out_hbm else pltpu.VMEM
    spaces = [
        pltpu.SMEM if k < scalars else pltpu.VMEM
        for k in range(len(args))
    ]
    sems = [pltpu.SemaphoreType.DMA((copies,))] if copies else []
    return pl.pallas_call(
        kernel,
        out_shape=[pltpu.HBM(o, F32) if out_hbm else jax.ShapeDtypeStruct(o, F32) for o in outs],
        in_specs=[pl.BlockSpec(memory_space=space) for space in spaces],
        out_specs=[pl.BlockSpec(memory_space=where)] * len(outs),
        scratch_shapes=in_vmem(*scratch) + sems,
        cost_estimate=pl.CostEstimate(flops=flops, bytes_accessed=size, transcendentals=0),
        compiler_params=pltpu.CompilerParams(vmem_limit_bytes=room),
    )(*args)


def lat_swapped(strip):
    return lax.ppermute(strip, "lat", [(0, 1), (1, 0)])


def lon_swapped(to_even, to_odd):
    count = lax.axis_size("lon")
    even = [(i, i ^ 1) for i in range(count)]
    odd = [(i, (((i - 1) % count ^ 1) + 1) % count) for i in range(count)]
    return lax.ppermute(to_even, "lon", even), lax.ppermute(to_odd, "lon", odd)


def chips_swapped(parts):
    moved = {0: parts[0]}
    for k in ORDER:
        pairs = [(i, i ^ k) for i in range(CHIPS)]
        moved[k] = lax.ppermute(parts[k], ("hour_0", "hour_1"), pairs)
    return [moved[k] for k in range(CHIPS)]


def cores_swapped(parts):
    return lax.ppermute(parts, "hour_2", [(0, 1), (1, 0)])


def per_device(precip, scaling, hour_weight, cotangent):
    rainfall = precip[0]
    incoming = scaling[0]
    upstream = cotangent[0]
    band3, band4, around = row_band(BLOCK), row_band(EDGE), col_band()
    bands = (*band3, *band4, *around)
    to_lat = lat_strip(incoming, rainfall)
    lat_in = lat_swapped(to_lat)
    even, odd = lon_swapped(
        *call(lon_kernel, (incoming, rainfall, lat_in), ((STRIP, WIDE), (STRIP, WIDE)))
    )
    shared = (CHIPS, 2 * EDGE, EDGE)
    whole = (PIECES, EDGE, EDGE)
    slope, share, second, logs, keep, give = call(
        forward_kernel,
        (hour_weight, incoming, rainfall, upstream, lat_in, even, odd, *bands),
        ((TALL, WIDE), (ROWS, COLS), whole, whole, shared, shared),
        scratch=((TALLER, WIDE), (TALL, WIDE), (EDGE, WIDE), (TALL, WIDE)),
        scalars=1,
        flops=4 * 10**9,
        room=14 << 20,
    )
    one = shared[1:]
    sums = call(pair_kernel, (keep, cores_swapped(give)), (one,) * CHIPS)
    (owned,) = call(owner_kernel, chips_swapped(sums), (one,))
    (mine,) = call(gather_kernel, chips_swapped([owned] * CHIPS), (shared,))
    (pieces,) = call(
        db_kernel, (hour_weight, mine, cores_swapped(mine), upstream, second, logs), (whole,),
        scalars=1,
    )
    (to_lat,) = call(back_lat_kernel, (pieces,), ((2 * RADIUS, COLS),))
    lat_in = lat_swapped(to_lat)
    even, odd = lon_swapped(
        *call(back_lon_kernel, (pieces, lat_in), ((2 * RADIUS, WIDE), (2 * RADIUS, WIDE)))
    )
    precip_part, sloped, slope_edge, share_edge = call(
        back_first_kernel,
        (pieces, slope, share, *band3, *around),
        ((ROWS, COLS), (TALL, WIDE), (48, WIDE), (48, WIDE)),
        scratch=((TALLER, COLS),),
        flops=2 * 10**9,
        room=14 << 20,
    )
    (scaling_part,) = call(
        back_second_kernel, (sloped, *band4, *around), ((ROWS, COLS),),
        flops=2 * 10**9, room=14 << 20,
    )
    grad_precip, grad_scaling = call(
        back_halo_kernel,
        (lat_in, even, odd, slope_edge, share_edge, precip_part, scaling_part, *edge_bands()),
        ((ROWS, COLS), (ROWS, COLS)),
        scratch=(
            (48, WIDE), (EDGE, EDGE), (EDGE, ROWS), (ROWS, 2 * EDGE), (ROWS, 2 * EDGE),
            (4, 2 * RADIUS, 2 * EDGE),
        ),
        flops=10**9,
        room=14 << 20,
        copies=10,
        out_hbm=True,
    )
    return (grad_precip[None], grad_scaling[None])


def solution(mesh):
    split_mesh = Mesh(
        mesh.devices.reshape(4, 2, 2, mesh.shape["lat"], mesh.shape["lon"]),
        ("hour_0", "hour_1", "hour_2", "lat", "lon"),
    )
    return jax.shard_map(
        per_device,
        mesh=split_mesh,
        in_specs=(P(HOUR, "lat", "lon"), P(HOUR, "lat", "lon"), P(HOUR), P(HOUR, "lat", "lon")),
        out_specs=(P(HOUR, "lat", "lon"), P(HOUR, "lat", "lon")),
        check_vma=False,
    )
```

profile of v0, /device:TPU:4, one launch (start us, length us, event | category | flops | bytes accessed | tf_op | source)
XLA Modules:
  0.0 83.5 jit_solution(14718133447270902991)
XLA Ops:
  0.6 0.0 copy-start
  0.6 0.0 copy-start.1
  0.6 0.9 %lat_edges.1 = f32[24,512]{1,0:T(8,128)S(1)} custom-call(f32[512,512]{1,0:T(8,128)} %bitcast.5, f32[512,512]{1,0:T(8,128)} %bitcast.8), custom_call_target="tpu_custom_call" | custom-call | tf_op jit(solution)/shard_map/lat_edges/pallas_call | solution.py:166
  1.6 0.0 copy-start.2
  1.6 0.0 copy-start.3
  1.6 0.0 copy-start.4
  1.6 0.0 copy-start.5
  1.6 0.0 copy-start.6
  1.7 0.0 copy-start.7
  1.7 0.0 copy-start.8
  1.7 2.3 %collective-permute-start = (f32[24,512]{1,0:T(8,128)S(1)}, f32[24,512]{1,0:T(8,128)S(1)}, u32[]{:S(2)}, u32[]{:S(2)}) collective-permute-start(f32[24,512]{1,0:T(8,128)S(1)} %lat_edges.1), channel_id=1, source_target_pairs={{0,8},{8,0},{1,9},{9,1},{2,10},{10,2},{3,11},{11,3},{4,12},{12,4},... | collective-permute-start | bytes 147464 | tf_op jit(solution)/shard_map/ppermute | solution.py:471
  4.0 3.4 %collective-permute-done.lat_in = f32[24,512]{1,0:T(8,128)S(1)} collective-permute-done((f32[24,512]{1,0:T(8,128)S(1)}, f32[24,512]{1,0:T(8,128)S(1)}, u32[]{:S(2)}, u32[]{:S(2)}) %collective-permute-start) | collective-permute-done | bytes 49184 | tf_op jit(solution)/shard_map/ppermute | solution.py:471
  7.4 0.4 shard_map.131
  7.7 2.0 %collective-permute-start.1 = (f32[24,640]{1,0:T(8,128)S(1)}, f32[24,640]{1,0:T(8,128)S(1)}, u32[]{:S(2)}, u32[]{:S(2)}) collective-permute-start(f32[24,640]{1,0:T(8,128)S(1)} %get-tuple-element.26), channel_id=1, source_target_pairs={{0,1},{1,0},{2,3},{3,2},{4,5},{5,4},{6,7},{7,6},{8,9},{9,8},{10,11... | collective-permute-start | bytes 184328 | tf_op jit(solution)/shard_map/ppermute | solution.py:478
  9.7 4.9 %collective-permute-start.2 = (f32[24,640]{1,0:T(8,128)S(1)}, f32[24,640]{1,0:T(8,128)S(1)}, u32[]{:S(2)}, u32[]{:S(2)}) collective-permute-start(f32[24,640]{1,0:T(8,128)S(1)} %get-tuple-element.27), channel_id=1, source_target_pairs={{0,7},{1,2},{2,1},{3,4},{4,3},{5,6},{6,5},{7,0},{8,15},{9,10},{10,... | collective-permute-start | bytes 184328 | tf_op jit(solution)/shard_map/ppermute | solution.py:478
  15.3 0.0 collective-permute-done.1.even
  15.3 1.5 %collective-permute-done.2.odd = f32[24,640]{1,0:T(8,128)S(1)} collective-permute-done((f32[24,640]{1,0:T(8,128)S(1)}, f32[24,640]{1,0:T(8,128)S(1)}, u32[]{:S(2)}, u32[]{:S(2)}) %collective-permute-start.2) | collective-permute-done | bytes 61472 | tf_op jit(solution)/shard_map/ppermute | solution.py:478
  16.9 4.9 %shard_map.132 = (f32[528,640]{1,0:T(8,128)S(1)}, f32[512,512]{1,0:T(8,128)S(1)}, f32[16,128,128]{2,1,0:T(8,128)S(1)}, f32[16,128,128]{2,1,0:T(8,128)S(1)}, f32[...) custom-call(f32[1]{0:T(128)S(6)} %copy.14.weight, f32[512,512]{1,0:T(8,128)S(1)} %bitcast.7, f32[512,512]{1,0:T(8,128)S(1)} %bitcast.10, ...), custom_call_target="tpu_custom_call" | custom-call | flops 4000000000 | bytes 11378692 | tf_op jit(solution)/shard_map/pallas_call | solution.py:459
  21.8 0.1 collective-permute-start.3
  21.9 2.6 %collective-permute-done.3.given = f32[8,256,128]{2,1,0:T(8,128)S(1)} collective-permute-done((f32[8,256,128]{2,1,0:T(8,128)S(1)}, f32[8,256,128]{2,1,0:T(8,128)S(1)}, u32[]{:S(2)}, u32[]{:S(2)}) %collective-permute-start.3) | collective-permute-done | bytes 1048608 | tf_op jit(solution)/shard_map/ppermute | solution.py:490
  24.6 0.1 shard_map.133
  24.7 1.3 %collective-permute-start.4 = (f32[256,128]{1,0:T(8,128)S(1)}, f32[256,128]{1,0:T(8,128)S(1)}, u32[]{:S(2)}, u32[]{:S(2)}) collective-permute-start(f32[256,128]{1,0:T(8,128)S(1)} %get-tuple-element.31), channel_id=1, source_target_pairs={{0,32},{32,0},{64,96},{96,64},{128,160},{160,128},{192,224},{224,1... | collective-permute-start | bytes 393224 | tf_op jit(solution)/shard_map/ppermute | solution.py:485
  26.0 1.6 %collective-permute-start.5 = (f32[256,128]{1,0:T(8,128)S(1)}, f32[256,128]{1,0:T(8,128)S(1)}, u32[]{:S(2)}, u32[]{:S(2)}) collective-permute-start(f32[256,128]{1,0:T(8,128)S(1)} %get-tuple-element.32), channel_id=1, source_target_pairs={{0,64},{32,96},{64,0},{96,32},{128,192},{160,224},{192,128},{224,1... | collective-permute-start | bytes 393224 | tf_op jit(solution)/shard_map/ppermute | solution.py:485
  27.5 0.7 collective-permute-start.6
  28.2 3.2 %collective-permute-start.7 = (f32[256,128]{1,0:T(8,128)S(1)}, f32[256,128]{1,0:T(8,128)S(1)}, u32[]{:S(2)}, u32[]{:S(2)}) collective-permute-start(f32[256,128]{1,0:T(8,128)S(1)} %get-tuple-element.34), channel_id=1, source_target_pairs={{0,128},{32,160},{64,192},{96,224},{128,0},{160,32},{192,64},{224,... | collective-permute-start | bytes 393224 | tf_op jit(solution)/shard_map/ppermute | solution.py:485
  31.4 1.0 %collective-permute-start.8 = (f32[256,128]{1,0:T(8,128)S(1)}, f32[256,128]{1,0:T(8,128)S(1)}, u32[]{:S(2)}, u32[]{:S(2)}) collective-permute-start(f32[256,128]{1,0:T(8,128)S(1)} %get-tuple-element.35), channel_id=1, source_target_pairs={{0,160},{32,128},{64,224},{96,192},{128,32},{160,0},{192,96},{224,... | collective-permute-start | bytes 393224 | tf_op jit(solution)/shard_map/ppermute | solution.py:485
  32.4 0.0 collective-permute-done.4.refs_1_
  32.4 3.0 %collective-permute-start.9 = (f32[256,128]{1,0:T(8,128)S(1)}, f32[256,128]{1,0:T(8,128)S(1)}, u32[]{:S(2)}, u32[]{:S(2)}) collective-permute-start(f32[256,128]{1,0:T(8,128)S(1)} %get-tuple-element.36), channel_id=1, source_target_pairs={{0,192},{32,224},{64,128},{96,160},{128,64},{160,96},{192,0},{224,... | collective-permute-start | bytes 393224 | tf_op jit(solution)/shard_map/ppermute | solution.py:485
  35.4 1.5 %collective-permute-done.5.refs_2_ = f32[256,128]{1,0:T(8,128)S(1)} collective-permute-done((f32[256,128]{1,0:T(8,128)S(1)}, f32[256,128]{1,0:T(8,128)S(1)}, u32[]{:S(2)}, u32[]{:S(2)}) %collective-permute-start.5) | collective-permute-done | bytes 131104 | tf_op jit(solution)/shard_map/ppermute | solution.py:485
  36.9 4.3 %collective-permute-start.10 = (f32[256,128]{1,0:T(8,128)S(1)}, f32[256,128]{1,0:T(8,128)S(1)}, u32[]{:S(2)}, u32[]{:S(2)}) collective-permute-start(f32[256,128]{1,0:T(8,128)S(1)} %get-tuple-element.37), channel_id=1, source_target_pairs={{0,224},{32,192},{64,160},{96,128},{128,96},{160,64},{192,32},{224... | collective-permute-start | bytes 393224 | tf_op jit(solution)/shard_map/ppermute | solution.py:485
  41.3 0.0 collective-permute-done.6.refs_3_
  41.3 1.8 %collective-permute-done.7.refs_4_ = f32[256,128]{1,0:T(8,128)S(1)} collective-permute-done((f32[256,128]{1,0:T(8,128)S(1)}, f32[256,128]{1,0:T(8,128)S(1)}, u32[]{:S(2)}, u32[]{:S(2)}) %collective-permute-start.7) | collective-permute-done | bytes 131104 | tf_op jit(solution)/shard_map/ppermute | solution.py:485
  43.1 0.0 collective-permute-done.8.refs_5_
  43.1 2.9 %collective-permute-done.9.refs_6_ = f32[256,128]{1,0:T(8,128)S(1)} collective-permute-done((f32[256,128]{1,0:T(8,128)S(1)}, f32[256,128]{1,0:T(8,128)S(1)}, u32[]{:S(2)}, u32[]{:S(2)}) %collective-permute-start.9) | collective-permute-done | bytes 131104 | tf_op jit(solution)/shard_map/ppermute | solution.py:485
  46.0 0.0 collective-permute-done.10.refs_7_
  46.0 0.1 shard_map.134.refs_0_
  46.1 2.7 %collective-permute-start.17 = (f32[256,128]{1,0:T(8,128)S(1)}, f32[256,128]{1,0:T(8,128)S(1)}, u32[]{:S(2)}, u32[]{:S(2)}) collective-permute-start(f32[256,128]{1,0:T(8,128)S(1)} %shard_map.134.refs_0_), channel_id=1, source_target_pairs={{0,224},{32,192},{64,160},{96,128},{128,96},{160,64},{192,32},{224... | collective-permute-start | bytes 393224 | tf_op jit(solution)/shard_map/ppermute | solution.py:485
  48.7 0.7 collective-permute-start.16
  49.5 1.0 %collective-permute-start.15 = (f32[256,128]{1,0:T(8,128)S(1)}, f32[256,128]{1,0:T(8,128)S(1)}, u32[]{:S(2)}, u32[]{:S(2)}) collective-permute-start(f32[256,128]{1,0:T(8,128)S(1)} %shard_map.134.refs_0_), channel_id=1, source_target_pairs={{0,160},{32,128},{64,224},{96,192},{128,32},{160,0},{192,96},{224,... | collective-permute-start | bytes 393224 | tf_op jit(solution)/shard_map/ppermute | solution.py:485
  50.5 3.4 %collective-permute-start.14 = (f32[256,128]{1,0:T(8,128)S(1)}, f32[256,128]{1,0:T(8,128)S(1)}, u32[]{:S(2)}, u32[]{:S(2)}) collective-permute-start(f32[256,128]{1,0:T(8,128)S(1)} %shard_map.134.refs_0_), channel_id=1, source_target_pairs={{0,128},{32,160},{64,192},{96,224},{128,0},{160,32},{192,64},{224,... | collective-permute-start | bytes 393224 | tf_op jit(solution)/shard_map/ppermute | solution.py:485
  53.8 0.0 collective-permute-start.13
  53.8 1.2 %collective-permute-done.17.refs_7_ = f32[256,128]{1,0:T(8,128)S(1)} collective-permute-done((f32[256,128]{1,0:T(8,128)S(1)}, f32[256,128]{1,0:T(8,128)S(1)}, u32[]{:S(2)}, u32[]{:S(2)}) %collective-permute-start.17) | collective-permute-done | bytes 131104 | tf_op jit(solution)/shard_map/ppermute | solution.py:485
  55.1 0.9 %collective-permute-start.12 = (f32[256,128]{1,0:T(8,128)S(1)}, f32[256,128]{1,0:T(8,128)S(1)}, u32[]{:S(2)}, u32[]{:S(2)}) collective-permute-start(f32[256,128]{1,0:T(8,128)S(1)} %shard_map.134.refs_0_), channel_id=1, source_target_pairs={{0,64},{32,96},{64,0},{96,32},{128,192},{160,224},{192,128},{224,1... | collective-permute-start | bytes 393224 | tf_op jit(solution)/shard_map/ppermute | solution.py:485
  55.9 4.7 %collective-permute-done.16.refs_6_ = f32[256,128]{1,0:T(8,128)S(1)} collective-permute-done((f32[256,128]{1,0:T(8,128)S(1)}, f32[256,128]{1,0:T(8,128)S(1)}, u32[]{:S(2)}, u32[]{:S(2)}) %collective-permute-start.16) | collective-permute-done | bytes 131104 | tf_op jit(solution)/shard_map/ppermute | solution.py:485
  60.7 0.0 collective-permute-start.11
  60.7 0.0 collective-permute-done.15.refs_5_
  60.7 2.0 %collective-permute-done.14.refs_4_ = f32[256,128]{1,0:T(8,128)S(1)} collective-permute-done((f32[256,128]{1,0:T(8,128)S(1)}, f32[256,128]{1,0:T(8,128)S(1)}, u32[]{:S(2)}, u32[]{:S(2)}) %collective-permute-start.14) | collective-permute-done | bytes 131104 | tf_op jit(solution)/shard_map/ppermute | solution.py:485
  62.6 0.0 collective-permute-done.13.refs_3_
  62.6 1.8 %collective-permute-done.12.refs_2_ = f32[256,128]{1,0:T(8,128)S(1)} collective-permute-done((f32[256,128]{1,0:T(8,128)S(1)}, f32[256,128]{1,0:T(8,128)S(1)}, u32[]{:S(2)}, u32[]{:S(2)}) %collective-permute-start.12) | collective-permute-done | bytes 131104 | tf_op jit(solution)/shard_map/ppermute | solution.py:485
  64.4 1.2 %collective-permute-done.11.refs_1_ = f32[256,128]{1,0:T(8,128)S(1)} collective-permute-done((f32[256,128]{1,0:T(8,128)S(1)}, f32[256,128]{1,0:T(8,128)S(1)}, u32[]{:S(2)}, u32[]{:S(2)}) %collective-permute-start.11) | collective-permute-done | bytes 131104 | tf_op jit(solution)/shard_map/ppermute | solution.py:485
  65.6 0.1 shard_map.135.mine
  65.7 0.1 collective-permute-start.18
  65.8 2.6 %collective-permute-done.18.theirs = f32[8,256,128]{2,1,0:T(8,128)S(1)} collective-permute-done((f32[8,256,128]{2,1,0:T(8,128)S(1)}, f32[8,256,128]{2,1,0:T(8,128)S(1)}, u32[]{:S(2)}, u32[]{:S(2)}) %collective-permute-start.18) | collective-permute-done | bytes 1048608 | tf_op jit(solution)/shard_map/ppermute | solution.py:490
  68.5 0.4 shard_map.136.pieces
  68.9 1.1 %collective-permute-start.19 = (f32[16,512]{1,0:T(8,128)S(1)}, f32[16,512]{1,0:T(8,128)S(1)}, u32[]{:S(2)}, u32[]{:S(2)}) collective-permute-start(f32[16,512]{1,0:T(8,128)S(1)} %shard_map.137), channel_id=1, source_target_pairs={{0,8},{8,0},{1,9},{9,1},{2,10},{10,2},{3,11},{11,3},{4,12},{12,4},... | collective-permute-start | bytes 98312 | tf_op jit(solution)/shard_map/ppermute | solution.py:471
  70.0 2.3 %shard_map.139 = (f32[512,512]{1,0:T(8,128)S(1)}, f32[528,640]{1,0:T(8,128)S(1)}, f32[48,640]{1,0:T(8,128)S(1)}, f32[48,640]{1,0:T(8,128)S(1)}) custom-call(f32[16,128,128]{2,1,0:T(8,128)S(1)} %shard_map.136.pieces, f32[528,640]{1,0:T(8,128)S(1)} %get-tuple-element.42.slope, f32[512,512]{1,0:T(8,128)S(1)} %get-tuple-element.43.share, ...), custom_call_target="tpu_custom_call" | custom-call | flops 2000000000 | bytes 7413760 | tf_op jit(solution)/shard_map/pallas_call | solution.py:459
  72.3 2.1 %collective-permute-done.19.lat_in = f32[16,512]{1,0:T(8,128)S(1)} collective-permute-done((f32[16,512]{1,0:T(8,128)S(1)}, f32[16,512]{1,0:T(8,128)S(1)}, u32[]{:S(2)}, u32[]{:S(2)}) %collective-permute-start.19) | collective-permute-done | bytes 32800 | tf_op jit(solution)/shard_map/ppermute | solution.py:471
  74.4 0.2 shard_map.138
  74.6 0.1 collective-permute-start.20
  74.7 3.3 %collective-permute-start.21 = (f32[16,640]{1,0:T(8,128)S(1)}, f32[16,640]{1,0:T(8,128)S(1)}, u32[]{:S(2)}, u32[]{:S(2)}) collective-permute-start(f32[16,640]{1,0:T(8,128)S(1)} %get-tuple-element.41), channel_id=1, source_target_pairs={{0,7},{1,2},{2,1},{3,4},{4,3},{5,6},{6,5},{7,0},{8,15},{9,10},{10,... | collective-permute-start | bytes 122888 | tf_op jit(solution)/shard_map/ppermute | solution.py:478
  78.1 2.3 %shard_map.140.scaling_part = f32[512,512]{1,0:T(8,128)S(1)} custom-call(f32[528,640]{1,0:T(8,128)S(1)} %get-tuple-element.47.sloped, bf16[128,144]{1,0:T(8,128)(2,1)S(1)} %copy-done.8, bf16[128,144]{1,0:T(8,128)(2,1)S(1)} %copy-done.7, bf16[512,256]{1,0:T(8,128)(2,1)S(1)} %copy-done.4, bf16[512,256]{1,0:T(8,128)(2,1)S(1)} %copy-done.3), custom_call_target="tpu_custom_call" | custom-call | flops 2000000000 | bytes 3596288 | tf_op jit(solution)/shard_map/pallas_call | solution.py:459
  80.3 0.0 collective-permute-done.20.even
  80.3 0.0 collective-permute-done.21.odd
  80.4 2.9 %shard_map.141 = (f32[512,512]{1,0:T(8,128)}, f32[512,512]{1,0:T(8,128)}) custom-call(f32[16,512]{1,0:T(8,128)S(1)} %collective-permute-done.19.lat_in, f32[16,640]{1,0:T(8,128)S(1)} %collective-permute-done.20.even, f32[16,640]{1,0:T(8,128)S(1)} %collective-permute-done.21.odd, f32[48,640]{1,0:T(8,128)S(1)} %get-tuple-element.44.slope_edge, ...), custom_call_target="tpu_custom_call" | custom-call | flops 1000000000 | bytes 4591616 | tf_op jit(solution)/shard_map/pallas_call | solution.py:459
  (14 shorter events, 0.0 us)
Async XLA Ops:
  0.6 6.7 %copy-start = (f32[1,512,512]{2,1,0:T(8,128)S(1)}, f32[1,512,512]{2,1,0:T(8,128)}, u32[]{:S(2)}) copy-start(f32[1,512,512]{2,1,0:T(8,128)} %param.13) | copy-start | bytes 3145732
  0.6 6.7 %copy-start.1 = (f32[1,512,512]{2,1,0:T(8,128)S(1)}, f32[1,512,512]{2,1,0:T(8,128)}, u32[]{:S(2)}) copy-start(f32[1,512,512]{2,1,0:T(8,128)} %param.12) | copy-start | bytes 3145732
  1.6 15.3 %copy-start.2 = (f32[1,512,512]{2,1,0:T(8,128)S(1)}, f32[1,512,512]{2,1,0:T(8,128)}, u32[]{:S(2)}) copy-start(f32[1,512,512]{2,1,0:T(8,128)} %param.15) | copy-start | bytes 3145732
  1.6 15.3 %copy-start.3 = (bf16[512,256]{1,0:T(8,128)(2,1)S(1)}, bf16[512,256]{1,0:T(8,128)(2,1)}, u32[]{:S(2)}) copy-start(bf16[512,256]{1,0:T(8,128)(2,1)} %constant.21.clone.cl) | copy-start | bytes 786436
  1.6 15.3 %copy-start.4 = (bf16[512,256]{1,0:T(8,128)(2,1)S(1)}, bf16[512,256]{1,0:T(8,128)(2,1)}, u32[]{:S(2)}) copy-start(bf16[512,256]{1,0:T(8,128)(2,1)} %constant.20.clone.ch) | copy-start | bytes 786436
  1.6 15.3 %copy-start.5 = (bf16[176,192]{1,0:T(8,128)(2,1)S(1)}, bf16[176,192]{1,0:T(8,128)(2,1)}, u32[]{:S(2)}) copy-start(bf16[176,192]{1,0:T(8,128)(2,1)} %constant.17.clone.rl3) | copy-start | bytes 202756
  1.6 15.3 %copy-start.6 = (bf16[176,192]{1,0:T(8,128)(2,1)S(1)}, bf16[176,192]{1,0:T(8,128)(2,1)}, u32[]{:S(2)}) copy-start(bf16[176,192]{1,0:T(8,128)(2,1)} %constant.16.clone.rh3) | copy-start | bytes 202756
  1.7 15.3 %copy-start.7 = (bf16[128,144]{1,0:T(8,128)(2,1)S(1)}, bf16[128,144]{1,0:T(8,128)(2,1)}, u32[]{:S(2)}) copy-start(bf16[128,144]{1,0:T(8,128)(2,1)} %constant.19.clone.rl4) | copy-start | bytes 110596
  1.7 15.3 %copy-start.8 = (bf16[128,144]{1,0:T(8,128)(2,1)S(1)}, bf16[128,144]{1,0:T(8,128)(2,1)}, u32[]{:S(2)}) copy-start(bf16[128,144]{1,0:T(8,128)(2,1)} %constant.18.clone.rh4) | copy-start | bytes 110596
  1.7 5.7 %collective-permute-start = (f32[24,512]{1,0:T(8,128)S(1)}, f32[24,512]{1,0:T(8,128)S(1)}, u32[]{:S(2)}, u32[]{:S(2)}) collective-permute-start(f32[24,512]{1,0:T(8,128)S(1)} %lat_edges.1), channel_id=1, source_target_pairs={{0,8},{8,0},{1,9},{9,1},{2,10},{10,2},{3,11},{11,3},{4,12},{12,4},... | collective-permute-start | bytes 147464 | tf_op jit(solution)/shard_map/ppermute | solution.py:471
  7.7 7.6 %collective-permute-start.1 = (f32[24,640]{1,0:T(8,128)S(1)}, f32[24,640]{1,0:T(8,128)S(1)}, u32[]{:S(2)}, u32[]{:S(2)}) collective-permute-start(f32[24,640]{1,0:T(8,128)S(1)} %get-tuple-element.26), channel_id=1, source_target_pairs={{0,1},{1,0},{2,3},{3,2},{4,5},{5,4},{6,7},{7,6},{8,9},{9,8},{10,11... | collective-permute-start | bytes 184328 | tf_op jit(solution)/shard_map/ppermute | solution.py:478
  9.7 7.1 %collective-permute-start.2 = (f32[24,640]{1,0:T(8,128)S(1)}, f32[24,640]{1,0:T(8,128)S(1)}, u32[]{:S(2)}, u32[]{:S(2)}) collective-permute-start(f32[24,640]{1,0:T(8,128)S(1)} %get-tuple-element.27), channel_id=1, source_target_pairs={{0,7},{1,2},{2,1},{3,4},{4,3},{5,6},{6,5},{7,0},{8,15},{9,10},{10,... | collective-permute-start | bytes 184328 | tf_op jit(solution)/shard_map/ppermute | solution.py:478
  21.8 2.7 %collective-permute-start.3 = (f32[8,256,128]{2,1,0:T(8,128)S(1)}, f32[8,256,128]{2,1,0:T(8,128)S(1)}, u32[]{:S(2)}, u32[]{:S(2)}) collective-permute-start(f32[8,256,128]{2,1,0:T(8,128)S(1)} %get-tuple-element.29), channel_id=1, source_target_pairs={{0,16},{16,0},{1,17},{17,1},{2,18},{18,2},{3,19},{19,3},{4,20},{20... | collective-permute-start | bytes 3145736 | tf_op jit(solution)/shard_map/ppermute | solution.py:490
  24.7 7.8 %collective-permute-start.4 = (f32[256,128]{1,0:T(8,128)S(1)}, f32[256,128]{1,0:T(8,128)S(1)}, u32[]{:S(2)}, u32[]{:S(2)}) collective-permute-start(f32[256,128]{1,0:T(8,128)S(1)} %get-tuple-element.31), channel_id=1, source_target_pairs={{0,32},{32,0},{64,96},{96,64},{128,160},{160,128},{192,224},{224,1... | collective-permute-start | bytes 393224 | tf_op jit(solution)/shard_map/ppermute | solution.py:485
  26.0 11.0 %collective-permute-start.5 = (f32[256,128]{1,0:T(8,128)S(1)}, f32[256,128]{1,0:T(8,128)S(1)}, u32[]{:S(2)}, u32[]{:S(2)}) collective-permute-start(f32[256,128]{1,0:T(8,128)S(1)} %get-tuple-element.32), channel_id=1, source_target_pairs={{0,64},{32,96},{64,0},{96,32},{128,192},{160,224},{192,128},{224,1... | collective-permute-start | bytes 393224 | tf_op jit(solution)/shard_map/ppermute | solution.py:485
  27.5 13.7 %collective-permute-start.6 = (f32[256,128]{1,0:T(8,128)S(1)}, f32[256,128]{1,0:T(8,128)S(1)}, u32[]{:S(2)}, u32[]{:S(2)}) collective-permute-start(f32[256,128]{1,0:T(8,128)S(1)} %get-tuple-element.33), channel_id=1, source_target_pairs={{0,96},{32,64},{64,32},{96,0},{128,224},{160,192},{192,160},{224,1... | collective-permute-start | bytes 393224 | tf_op jit(solution)/shard_map/ppermute | solution.py:485
  28.2 14.9 %collective-permute-start.7 = (f32[256,128]{1,0:T(8,128)S(1)}, f32[256,128]{1,0:T(8,128)S(1)}, u32[]{:S(2)}, u32[]{:S(2)}) collective-permute-start(f32[256,128]{1,0:T(8,128)S(1)} %get-tuple-element.34), channel_id=1, source_target_pairs={{0,128},{32,160},{64,192},{96,224},{128,0},{160,32},{192,64},{224,... | collective-permute-start | bytes 393224 | tf_op jit(solution)/shard_map/ppermute | solution.py:485
  31.4 11.7 %collective-permute-start.8 = (f32[256,128]{1,0:T(8,128)S(1)}, f32[256,128]{1,0:T(8,128)S(1)}, u32[]{:S(2)}, u32[]{:S(2)}) collective-permute-start(f32[256,128]{1,0:T(8,128)S(1)} %get-tuple-element.35), channel_id=1, source_target_pairs={{0,160},{32,128},{64,224},{96,192},{128,32},{160,0},{192,96},{224,... | collective-permute-start | bytes 393224 | tf_op jit(solution)/shard_map/ppermute | solution.py:485
  32.4 13.6 %collective-permute-start.9 = (f32[256,128]{1,0:T(8,128)S(1)}, f32[256,128]{1,0:T(8,128)S(1)}, u32[]{:S(2)}, u32[]{:S(2)}) collective-permute-start(f32[256,128]{1,0:T(8,128)S(1)} %get-tuple-element.36), channel_id=1, source_target_pairs={{0,192},{32,224},{64,128},{96,160},{128,64},{160,96},{192,0},{224,... | collective-permute-start | bytes 393224 | tf_op jit(solution)/shard_map/ppermute | solution.py:485
  36.9 9.1 %collective-permute-start.10 = (f32[256,128]{1,0:T(8,128)S(1)}, f32[256,128]{1,0:T(8,128)S(1)}, u32[]{:S(2)}, u32[]{:S(2)}) collective-permute-start(f32[256,128]{1,0:T(8,128)S(1)} %get-tuple-element.37), channel_id=1, source_target_pairs={{0,224},{32,192},{64,160},{96,128},{128,96},{160,64},{192,32},{224... | collective-permute-start | bytes 393224 | tf_op jit(solution)/shard_map/ppermute | solution.py:485
  46.1 9.0 %collective-permute-start.17 = (f32[256,128]{1,0:T(8,128)S(1)}, f32[256,128]{1,0:T(8,128)S(1)}, u32[]{:S(2)}, u32[]{:S(2)}) collective-permute-start(f32[256,128]{1,0:T(8,128)S(1)} %shard_map.134.refs_0_), channel_id=1, source_target_pairs={{0,224},{32,192},{64,160},{96,128},{128,96},{160,64},{192,32},{224... | collective-permute-start | bytes 393224 | tf_op jit(solution)/shard_map/ppermute | solution.py:485
  48.7 11.9 %collective-permute-start.16 = (f32[256,128]{1,0:T(8,128)S(1)}, f32[256,128]{1,0:T(8,128)S(1)}, u32[]{:S(2)}, u32[]{:S(2)}) collective-permute-start(f32[256,128]{1,0:T(8,128)S(1)} %shard_map.134.refs_0_), channel_id=1, source_target_pairs={{0,192},{32,224},{64,128},{96,160},{128,64},{160,96},{192,0},{224,... | collective-permute-start | bytes 393224 | tf_op jit(solution)/shard_map/ppermute | solution.py:485
  49.5 11.2 %collective-permute-start.15 = (f32[256,128]{1,0:T(8,128)S(1)}, f32[256,128]{1,0:T(8,128)S(1)}, u32[]{:S(2)}, u32[]{:S(2)}) collective-permute-start(f32[256,128]{1,0:T(8,128)S(1)} %shard_map.134.refs_0_), channel_id=1, source_target_pairs={{0,160},{32,128},{64,224},{96,192},{128,32},{160,0},{192,96},{224,... | collective-permute-start | bytes 393224 | tf_op jit(solution)/shard_map/ppermute | solution.py:485
  50.5 12.2 %collective-permute-start.14 = (f32[256,128]{1,0:T(8,128)S(1)}, f32[256,128]{1,0:T(8,128)S(1)}, u32[]{:S(2)}, u32[]{:S(2)}) collective-permute-start(f32[256,128]{1,0:T(8,128)S(1)} %shard_map.134.refs_0_), channel_id=1, source_target_pairs={{0,128},{32,160},{64,192},{96,224},{128,0},{160,32},{192,64},{224,... | collective-permute-start | bytes 393224 | tf_op jit(solution)/shard_map/ppermute | solution.py:485
  53.8 8.8 %collective-permute-start.13 = (f32[256,128]{1,0:T(8,128)S(1)}, f32[256,128]{1,0:T(8,128)S(1)}, u32[]{:S(2)}, u32[]{:S(2)}) collective-permute-start(f32[256,128]{1,0:T(8,128)S(1)} %shard_map.134.refs_0_), channel_id=1, source_target_pairs={{0,96},{32,64},{64,32},{96,0},{128,224},{160,192},{192,160},{224,1... | collective-permute-start | bytes 393224 | tf_op jit(solution)/shard_map/ppermute | solution.py:485
  55.1 9.3 %collective-permute-start.12 = (f32[256,128]{1,0:T(8,128)S(1)}, f32[256,128]{1,0:T(8,128)S(1)}, u32[]{:S(2)}, u32[]{:S(2)}) collective-permute-start(f32[256,128]{1,0:T(8,128)S(1)} %shard_map.134.refs_0_), channel_id=1, source_target_pairs={{0,64},{32,96},{64,0},{96,32},{128,192},{160,224},{192,128},{224,1... | collective-permute-start | bytes 393224 | tf_op jit(solution)/shard_map/ppermute | solution.py:485
  60.7 5.0 %collective-permute-start.11 = (f32[256,128]{1,0:T(8,128)S(1)}, f32[256,128]{1,0:T(8,128)S(1)}, u32[]{:S(2)}, u32[]{:S(2)}) collective-permute-start(f32[256,128]{1,0:T(8,128)S(1)} %shard_map.134.refs_0_), channel_id=1, source_target_pairs={{0,32},{32,0},{64,96},{96,64},{128,160},{160,128},{192,224},{224,1... | collective-permute-start | bytes 393224 | tf_op jit(solution)/shard_map/ppermute | solution.py:485
  65.7 2.7 %collective-permute-start.18 = (f32[8,256,128]{2,1,0:T(8,128)S(1)}, f32[8,256,128]{2,1,0:T(8,128)S(1)}, u32[]{:S(2)}, u32[]{:S(2)}) collective-permute-start(f32[8,256,128]{2,1,0:T(8,128)S(1)} %shard_map.135.mine), channel_id=1, source_target_pairs={{0,16},{16,0},{1,17},{17,1},{2,18},{18,2},{3,19},{19,3},{4,20},{20... | collective-permute-start | bytes 3145736 | tf_op jit(solution)/shard_map/ppermute | solution.py:490
  68.9 5.5 %collective-permute-start.19 = (f32[16,512]{1,0:T(8,128)S(1)}, f32[16,512]{1,0:T(8,128)S(1)}, u32[]{:S(2)}, u32[]{:S(2)}) collective-permute-start(f32[16,512]{1,0:T(8,128)S(1)} %shard_map.137), channel_id=1, source_target_pairs={{0,8},{8,0},{1,9},{9,1},{2,10},{10,2},{3,11},{11,3},{4,12},{12,4},... | collective-permute-start | bytes 98312 | tf_op jit(solution)/shard_map/ppermute | solution.py:471
  74.6 5.7 %collective-permute-start.20 = (f32[16,640]{1,0:T(8,128)S(1)}, f32[16,640]{1,0:T(8,128)S(1)}, u32[]{:S(2)}, u32[]{:S(2)}) collective-permute-start(f32[16,640]{1,0:T(8,128)S(1)} %get-tuple-element.40), channel_id=1, source_target_pairs={{0,1},{1,0},{2,3},{3,2},{4,5},{5,4},{6,7},{7,6},{8,9},{9,8},{10,11... | collective-permute-start | bytes 122888 | tf_op jit(solution)/shard_map/ppermute | solution.py:478
  74.7 5.6 %collective-permute-start.21 = (f32[16,640]{1,0:T(8,128)S(1)}, f32[16,640]{1,0:T(8,128)S(1)}, u32[]{:S(2)}, u32[]{:S(2)}) collective-permute-start(f32[16,640]{1,0:T(8,128)S(1)} %get-tuple-element.41), channel_id=1, source_target_pairs={{0,7},{1,2},{2,1},{3,4},{4,3},{5,6},{6,5},{7,0},{8,15},{9,10},{10,... | collective-permute-start | bytes 122888 | tf_op jit(solution)/shard_map/ppermute | solution.py:478
  78.0 2.3 %copy-start.9 = (bf16[2,48,48]{2,1,0:T(8,128)(2,1)S(1)}, bf16[2,48,48]{2,1,0:T(8,128)(2,1)}, u32[]{:S(2)}) copy-start(bf16[2,48,48]{2,1,0:T(8,128)(2,1)} %constant.23.clone.dl) | copy-start | bytes 27652
  78.1 2.3 %copy-start.10 = (bf16[2,48,48]{2,1,0:T(8,128)(2,1)S(1)}, bf16[2,48,48]{2,1,0:T(8,128)(2,1)}, u32[]{:S(2)}) copy-start(bf16[2,48,48]{2,1,0:T(8,128)(2,1)} %constant.22.clone.dh) | copy-start | bytes 27652
where the time goes:
time: 84.1 us; the launch traced here: 83.5 us
  starting transfers between devices  37.7 us (45%)
  waiting for transfers between devices  29.5 us (35%)
  Pallas kernels  14.6 us (17%)
  between operations  1.7 us (2%)
    ppermute x14, starting transfers between devices, chips_swapped(): moved[k] = lax.ppermute(parts[k], ('hour_0', 'hour_1'), pairs)  23.7 us
    ppermute x14, waiting for transfers between devices, chips_swapped(): moved[k] = lax.ppermute(parts[k], ('hour_0', 'hour_1'), pairs)  17.1 us
    pallas_call x11, Pallas kernels, call(): pl.pallas_call(kernel, out_shape=[pltpu.HBM(o, F32) if out_hbm else jax.S...  13.6 us
    ppermute x2, starting transfers between devices, lon_swapped(): lax.ppermute(to_odd, 'lon', odd)  8.25 us
    ppermute x2, waiting for transfers between devices, lat_swapped(): return lax.ppermute(strip, 'lat', [(0, 1), (1, 0)])  5.47 us
    ppermute x2, waiting for transfers between devices, cores_swapped(): return lax.ppermute(parts, 'hour_2', [(0, 1), (1, 0)])  5.29 us
    ppermute x2, starting transfers between devices, lat_swapped(): return lax.ppermute(strip, 'lat', [(0, 1), (1, 0)])  3.4 us
    ppermute x2, starting transfers between devices, lon_swapped(): lax.ppermute(to_even, 'lon', even)  2.1 us
  transfers between devices with their start and end apart: 22, of which 13 were waited for; matrix products, arithmetic and copies ran while one was open for 0% of the time, Pallas kernels for 5%

commit v1 on v0

--- a/solution.py
+++ b/solution.py
@@ -22,7 +22,6 @@
 BLOCK = TALL // 3
 PIECES = 16
 CHIPS = 8
-ORDER = (5, 7, 3, 1, 4, 2, 6)
 PIECE = ROWS // PIECES
 STRIP = 3 * RADIUS
 F32 = jnp.float32
@@ -186,10 +185,11 @@
 
 def forward_kernel(
     weight, scaling, precip, upstream, lat_in, even, odd, rh3, rl3, rh4, rl4, ch, cl,
-    slope, share, second, logs, keep, give, sx, px, side, lifted,
+    slope, share, second, logs, keep_even, keep_odd, give_even, give_odd, sx, px, side, lifted,
 ):
     lat = my_lat()
     core = lax.axis_index("hour_2")
+    far, near = lax.axis_index("hour_0"), lax.axis_index("hour_1")
     wide, narrow = 2 * RADIUS, RADIUS
     sx[wide : wide + ROWS, 0:COLS] = scaling[...]
     px[narrow : narrow + ROWS, 0:COLS] = precip[...]
@@ -220,24 +220,20 @@
                 to = slice(PIECE * j, PIECE * (j + 1))
                 second[i * (EDGE // PIECE) + q, to, :] = b[rows, lanes]
                 logs[i * (EDGE // PIECE) + q, to, :] = logb[rows, lanes]
-            for c in range(2):
-                first = slice(2 * PIECE * c, 2 * PIECE * c + PIECE)
-                other = slice(2 * PIECE * c + PIECE, 2 * PIECE * (c + 1))
-                for k, part in enumerate(parts):
-                    to = slice(EDGE * k + PIECE * j, EDGE * k + PIECE * (j + 1))
-                    x, y = part[first, lanes], part[other, lanes]
-                    keep[2 * i + c, to, :] = jnp.where(core == 0, x, y)
-                    give[2 * i + c, to, :] = jnp.where(core == 0, y, x)
-
-
-def my_chip():
-    return lax.axis_index("hour_0") * 2 + lax.axis_index("hour_1")
+            for k, part in enumerate(parts):
+                to = slice(EDGE * k + PIECE * j, EDGE * k + PIECE * (j + 1))
+                four = [part[PIECE * q : PIECE * (q + 1), lanes] for q in range(4)]
+                stay = [jnp.where(core == 0, four[2 * c], four[2 * c + 1]) for c in range(2)]
+                leave = [jnp.where(core == 0, four[2 * c + 1], four[2 * c]) for c in range(2)]
+                keep_even[i ^ far, to, :] = jnp.where(near == 0, stay[0], stay[1])
+                keep_odd[i ^ far, to, :] = jnp.where(near == 0, stay[1], stay[0])
+                give_even[i ^ far, to, :] = jnp.where(near == 0, leave[0], leave[1])
+                give_odd[i ^ far, to, :] = jnp.where(near == 0, leave[1], leave[0])
 
 
 def pair_kernel(keep, given, *outs):
-    chip = my_chip()
     for k, out in enumerate(outs):
-        out[...] = keep[chip ^ k] + given[chip ^ k]
+        out[...] = keep[k] + given[k]
 
 
 def owner_kernel(*refs):
@@ -255,24 +251,36 @@
 
 
 def gather_kernel(*refs):
-    chip = my_chip()
-    out = refs[CHIPS]
-    for k in range(CHIPS):
-        out[chip ^ k] = refs[k][...]
-
-
-def db_kernel(weight, mine, theirs, upstream, second, logs, pieces):
+    for k in range(CHIPS // 2):
+        refs[-1][k] = refs[k][...]
+
+
+def db_kernel(
+    weight, even, odd, their_even, their_odd, upstream, second, logs, pieces
+):
     core = lax.axis_index("hour_2")
-    for p in range(PIECES):
-        here = core == p % 2
-        for j in range(COLS // EDGE):
-            rows = slice(PIECE * j, PIECE * (j + 1))
-            low = slice(EDGE + PIECE * j, EDGE + PIECE * (j + 1))
-            logq = jnp.where(here, mine[p // 2, rows, :], theirs[p // 2, rows, :])
-            dlogq = jnp.where(here, mine[p // 2, low, :], theirs[p // 2, low, :])
-            own = upstream[PIECE * p : PIECE * (p + 1), EDGE * j : EDGE * (j + 1)]
-            term = PHI * own * jnp.exp(PHI * (logq - logs[p, rows, :]))
-            pieces[p, rows, :] = (weight[0] * dlogq - term) / second[p, rows, :]
+    far, near = lax.axis_index("hour_0"), lax.axis_index("hour_1")
+    for i in range(CHIPS // 2):
+        for own in range(2):
+            here = core == own
+            for j in range(COLS // EDGE):
+                rows = slice(PIECE * j, PIECE * (j + 1))
+                low = slice(EDGE + PIECE * j, EDGE + PIECE * (j + 1))
+                found = [
+                    [
+                        jnp.where(here, mine[i ^ far, part, :], theirs[i ^ far, part, :])
+                        for part in (rows, low)
+                    ]
+                    for mine, theirs in ((even, their_even), (odd, their_odd))
+                ]
+                for c in range(2):
+                    logq, dlogq = (
+                        jnp.where(near == c, same, other) for same, other in zip(*found)
+                    )
+                    p = 4 * i + 2 * c + own
+                    value = upstream[PIECE * p : PIECE * (p + 1), EDGE * j : EDGE * (j + 1)]
+                    term = PHI * value * jnp.exp(PHI * (logq - logs[p, rows, :]))
+                    pieces[p, rows, :] = (weight[0] * dlogq - term) / second[p, rows, :]
 
 
 def tile_column(pieces, j):
@@ -478,12 +486,11 @@
     return lax.ppermute(to_even, "lon", even), lax.ppermute(to_odd, "lon", odd)
 
 
-def chips_swapped(parts):
-    moved = {0: parts[0]}
-    for k in ORDER:
-        pairs = [(i, i ^ k) for i in range(CHIPS)]
-        moved[k] = lax.ppermute(parts[k], ("hour_0", "hour_1"), pairs)
-    return [moved[k] for k in range(CHIPS)]
+def chip_swapped(part, k):
+    if k == 0:
+        return part
+    pairs = [(i, i ^ k) for i in range(CHIPS)]
+    return lax.ppermute(part, ("hour_0", "hour_1"), pairs)
 
 
 def cores_swapped(parts):
@@ -501,23 +508,37 @@
     even, odd = lon_swapped(
         *call(lon_kernel, (incoming, rainfall, lat_in), ((STRIP, WIDE), (STRIP, WIDE)))
     )
-    shared = (CHIPS, 2 * EDGE, EDGE)
+    half = (CHIPS // 2, 2 * EDGE, EDGE)
     whole = (PIECES, EDGE, EDGE)
-    slope, share, second, logs, keep, give = call(
+    slope, share, second, logs, keep_even, keep_odd, give_even, give_odd = call(
         forward_kernel,
         (hour_weight, incoming, rainfall, upstream, lat_in, even, odd, *bands),
-        ((TALL, WIDE), (ROWS, COLS), whole, whole, shared, shared),
+        ((TALL, WIDE), (ROWS, COLS), whole, whole, half, half, half, half),
         scratch=((TALLER, WIDE), (TALL, WIDE), (EDGE, WIDE), (TALL, WIDE)),
         scalars=1,
         flops=4 * 10**9,
         room=14 << 20,
     )
-    one = shared[1:]
-    sums = call(pair_kernel, (keep, cores_swapped(give)), (one,) * CHIPS)
-    (owned,) = call(owner_kernel, chips_swapped(sums), (one,))
-    (mine,) = call(gather_kernel, chips_swapped([owned] * CHIPS), (shared,))
+    given_odd = cores_swapped(give_odd)
+    given_even = cores_swapped(give_even)
+    arrived = []
+    for keep, given, first in ((keep_odd, given_odd, 1), (keep_even, given_even, 0)):
+        sums = call(pair_kernel, (keep, given), (half[1:],) * (CHIPS // 2))
+        arrived += [chip_swapped(part, 2 * k + first) for k, part in enumerate(sums)]
+    (owned,) = call(owner_kernel, tuple(arrived), (half[1:],))
+
+    def collected(first, *after):
+        parts = [chip_swapped(owned, 2 * k + first) for k in range(CHIPS // 2)]
+        return call(gather_kernel, (*parts, *after), (half,))[0]
+
+    odd_part = collected(1)
+    their_odd = cores_swapped(odd_part)
+    even_part = collected(0, odd_part)
+    their_even = cores_swapped(even_part)
     (pieces,) = call(
-        db_kernel, (hour_weight, mine, cores_swapped(mine), upstream, second, logs), (whole,),
+        db_kernel,
+        (hour_weight, even_part, odd_part, their_even, their_odd, upstream, second, logs),
+        (whole,),
         scalars=1,
     )
     (to_lat,) = call(back_lat_kernel, (pieces,), ((2 * RADIUS, COLS),))

time: 84.1 us -> 82.6 us (0.982)
  starting transfers between devices: 37.7 us -> 36.3 us
    ppermute x14, starting transfers between devices: 23.7 us -> 21.8 us  [chip_swapped(): return lax.ppermute(part, ('hour_0', 'hour_1'), pairs)]
    ppermute x2 -> x4, waiting for transfers between devices: 5.29 us -> 3.55 us  [cores_swapped(): return lax.ppermute(parts, 'hour_2', [(0, 1), (1, 0)])]
    ppermute x14, waiting for transfers between devices: 17.1 us -> 18.2 us  [chip_swapped(): return lax.ppermute(part, ('hour_0', 'hour_1'), pairs)]
    ppermute x2 -> x4, starting transfers between devices: 0.19 us -> 1.18 us  [cores_swapped(): return lax.ppermute(parts, 'hour_2', [(0, 1), (1, 0)])]
    pallas_call x11 -> x13, Pallas kernels: 13.6 us -> 13.8 us  [call(): pl.pallas_call(kernel, out_shape=[pltpu.HBM(o, F32) if out_hbm else jax.S...]
  transfers between devices with their start and end apart: 22 -> 24, of which waited for: 13 -> 17; matrix products, arithmetic and copies ran while one was open for 0% -> 0% of each run, Pallas kernels for 5% -> 6%
where the time goes in v1:
time: 82.6 us; the launch traced here: 82 us
  starting transfers between devices  36.3 us (44%)
  waiting for transfers between devices  29.1 us (35%)
  Pallas kernels  14.7 us (18%)
  between operations  1.71 us (2%)
    ppermute x14, starting transfers between devices, chip_swapped(): return lax.ppermute(part, ('hour_0', 'hour_1'), pairs)  21.8 us
    ppermute x14, waiting for transfers between devices, chip_swapped(): return lax.ppermute(part, ('hour_0', 'hour_1'), pairs)  18.2 us
    pallas_call x13, Pallas kernels, call(): pl.pallas_call(kernel, out_shape=[pltpu.HBM(o, F32) if out_hbm else jax.S...  13.8 us
    ppermute x2, starting transfers between devices, lon_swapped(): lax.ppermute(to_odd, 'lon', odd)  8.26 us
    ppermute x2, waiting for transfers between devices, lat_swapped(): return lax.ppermute(strip, 'lat', [(0, 1), (1, 0)])  5.89 us
    ppermute x4, waiting for transfers between devices, cores_swapped(): return lax.ppermute(parts, 'hour_2', [(0, 1), (1, 0)])  3.55 us
    ppermute x2, starting transfers between devices, lat_swapped(): return lax.ppermute(strip, 'lat', [(0, 1), (1, 0)])  2.97 us
    ppermute x2, starting transfers between devices, lon_swapped(): lax.ppermute(to_even, 'lon', even)  2.1 us
  transfers between devices with their start and end apart: 24, of which 17 were waited for; matrix products, arithmetic and copies ran while one was open for 0% of the time, Pallas kernels for 6%

profile of v1, /device:TPU:4, one launch (start us, length us, event | category | flops | bytes accessed | tf_op | source)
XLA Modules:
  0.0 82.0 jit_solution(8420189748503490833)
XLA Ops:
  0.6 0.9 %lat_edges.1 = f32[24,512]{1,0:T(8,128)S(1)} custom-call(f32[512,512]{1,0:T(8,128)} %bitcast.5, f32[512,512]{1,0:T(8,128)} %bitcast.8), custom_call_target="tpu_custom_call" | custom-call | tf_op jit(solution)/shard_map/lat_edges/pallas_call | solution.py:165
  1.6 0.0 copy-start.2
  1.6 0.0 copy-start.3
  1.6 0.0 copy-start.4
  1.6 0.0 copy-start.5
  1.6 0.0 copy-start.6
  1.7 0.0 copy-start.7
  1.7 0.0 copy-start.8
  1.7 2.3 %collective-permute-start = (f32[24,512]{1,0:T(8,128)S(1)}, f32[24,512]{1,0:T(8,128)S(1)}, u32[]{:S(2)}, u32[]{:S(2)}) collective-permute-start(f32[24,512]{1,0:T(8,128)S(1)} %lat_edges.1), channel_id=1, source_target_pairs={{0,8},{8,0},{1,9},{9,1},{2,10},{10,2},{3,11},{11,3},{4,12},{12,4},... | collective-permute-start | bytes 147464 | tf_op jit(solution)/shard_map/ppermute | solution.py:479
  4.0 3.4 %collective-permute-done.lat_in = f32[24,512]{1,0:T(8,128)S(1)} collective-permute-done((f32[24,512]{1,0:T(8,128)S(1)}, f32[24,512]{1,0:T(8,128)S(1)}, u32[]{:S(2)}, u32[]{:S(2)}) %collective-permute-start) | collective-permute-done | bytes 49184 | tf_op jit(solution)/shard_map/ppermute | solution.py:479
  7.4 0.4 shard_map.131
  7.7 2.0 %collective-permute-start.1 = (f32[24,640]{1,0:T(8,128)S(1)}, f32[24,640]{1,0:T(8,128)S(1)}, u32[]{:S(2)}, u32[]{:S(2)}) collective-permute-start(f32[24,640]{1,0:T(8,128)S(1)} %get-tuple-element.28), channel_id=1, source_target_pairs={{0,1},{1,0},{2,3},{3,2},{4,5},{5,4},{6,7},{7,6},{8,9},{9,8},{10,11... | collective-permute-start | bytes 184328 | tf_op jit(solution)/shard_map/ppermute | solution.py:486
  9.7 4.9 %collective-permute-start.2 = (f32[24,640]{1,0:T(8,128)S(1)}, f32[24,640]{1,0:T(8,128)S(1)}, u32[]{:S(2)}, u32[]{:S(2)}) collective-permute-start(f32[24,640]{1,0:T(8,128)S(1)} %get-tuple-element.29), channel_id=1, source_target_pairs={{0,7},{1,2},{2,1},{3,4},{4,3},{5,6},{6,5},{7,0},{8,15},{9,10},{10,... | collective-permute-start | bytes 184328 | tf_op jit(solution)/shard_map/ppermute | solution.py:486
  15.3 0.0 collective-permute-done.1.even
  15.3 1.5 %collective-permute-done.2.odd = f32[24,640]{1,0:T(8,128)S(1)} collective-permute-done((f32[24,640]{1,0:T(8,128)S(1)}, f32[24,640]{1,0:T(8,128)S(1)}, u32[]{:S(2)}, u32[]{:S(2)}) %collective-permute-start.2) | collective-permute-done | bytes 61472 | tf_op jit(solution)/shard_map/ppermute | solution.py:486
  16.9 4.9 %shard_map.132 = (f32[528,640]{1,0:T(8,128)S(1)}, f32[512,512]{1,0:T(8,128)S(1)}, f32[16,128,128]{2,1,0:T(8,128)S(1)}, f32[16,128,128]{2,1,0:T(8,128)S(1)}, f32[...) custom-call(f32[1]{0:T(128)S(6)} %copy.14.weight, ...), custom_call_target="tpu_custom_call" | custom-call | flops 4000000000 | bytes 11378692 | tf_op jit(solution)/shard_map/pallas_call | solution.py:467
  21.9 0.1 collective-permute-start.3
  22.0 0.5 collective-permute-start.8
  22.5 1.4 %collective-permute-done.3.given = f32[4,256,128]{2,1,0:T(8,128)S(1)} collective-permute-done((f32[4,256,128]{2,1,0:T(8,128)S(1)}, f32[4,256,128]{2,1,0:T(8,128)S(1)}, u32[]{:S(2)}, u32[]{:S(2)}) %collective-permute-start.3) | collective-permute-done | bytes 524320 | tf_op jit(solution)/shard_map/ppermute | solution.py:497
  23.9 0.1 shard_map.133
  23.9 1.3 %collective-permute-start.4 = (f32[256,128]{1,0:T(8,128)S(1)}, f32[256,128]{1,0:T(8,128)S(1)}, u32[]{:S(2)}, u32[]{:S(2)}) collective-permute-start(f32[256,128]{1,0:T(8,128)S(1)} %get-tuple-element.32), channel_id=1, source_target_pairs={{0,32},{32,0},{64,96},{96,64},{128,160},{160,128},{192,224},{224,1... | collective-permute-start | bytes 393224 | tf_op jit(solution)/shard_map/ppermute | solution.py:493
  25.2 1.8 %collective-permute-start.5 = (f32[256,128]{1,0:T(8,128)S(1)}, f32[256,128]{1,0:T(8,128)S(1)}, u32[]{:S(2)}, u32[]{:S(2)}) collective-permute-start(f32[256,128]{1,0:T(8,128)S(1)} %get-tuple-element.33), channel_id=1, source_target_pairs={{0,96},{32,64},{64,32},{96,0},{128,224},{160,192},{192,160},{224,1... | collective-permute-start | bytes 393224 | tf_op jit(solution)/shard_map/ppermute | solution.py:493
  27.1 3.5 %collective-permute-start.6 = (f32[256,128]{1,0:T(8,128)S(1)}, f32[256,128]{1,0:T(8,128)S(1)}, u32[]{:S(2)}, u32[]{:S(2)}) collective-permute-start(f32[256,128]{1,0:T(8,128)S(1)} %get-tuple-element.34), channel_id=1, source_target_pairs={{0,160},{32,128},{64,224},{96,192},{128,32},{160,0},{192,96},{224,... | collective-permute-start | bytes 393224 | tf_op jit(solution)/shard_map/ppermute | solution.py:493
  30.6 0.5 collective-permute-start.7
  31.1 0.1 shard_map.134
  31.1 0.4 collective-permute-start.9
  31.6 0.0 collective-permute-done.4.refs_0_
  31.6 4.1 %collective-permute-start.10 = (f32[256,128]{1,0:T(8,128)S(1)}, f32[256,128]{1,0:T(8,128)S(1)}, u32[]{:S(2)}, u32[]{:S(2)}) collective-permute-start(f32[256,128]{1,0:T(8,128)S(1)} %get-tuple-element.40), channel_id=1, source_target_pairs={{0,128},{32,160},{64,192},{96,224},{128,0},{160,32},{192,64},{224,... | collective-permute-start | bytes 393224 | tf_op jit(solution)/shard_map/ppermute | solution.py:493
  35.7 0.7 collective-permute-start.11
  36.4 2.5 %collective-permute-done.6.refs_2_ = f32[256,128]{1,0:T(8,128)S(1)} collective-permute-done((f32[256,128]{1,0:T(8,128)S(1)}, f32[256,128]{1,0:T(8,128)S(1)}, u32[]{:S(2)}, u32[]{:S(2)}) %collective-permute-start.6) | collective-permute-done | bytes 131104 | tf_op jit(solution)/shard_map/ppermute | solution.py:493
  39.0 2.0 %collective-permute-done.7.refs_3_ = f32[256,128]{1,0:T(8,128)S(1)} collective-permute-done((f32[256,128]{1,0:T(8,128)S(1)}, f32[256,128]{1,0:T(8,128)S(1)}, u32[]{:S(2)}, u32[]{:S(2)}) %collective-permute-start.7) | collective-permute-done | bytes 131104 | tf_op jit(solution)/shard_map/ppermute | solution.py:493
  41.0 0.0 collective-permute-done.9.refs_5_
  41.0 2.7 %collective-permute-done.10.refs_6_ = f32[256,128]{1,0:T(8,128)S(1)} collective-permute-done((f32[256,128]{1,0:T(8,128)S(1)}, f32[256,128]{1,0:T(8,128)S(1)}, u32[]{:S(2)}, u32[]{:S(2)}) %collective-permute-start.10) | collective-permute-done | bytes 131104 | tf_op jit(solution)/shard_map/ppermute | solution.py:493
  43.6 2.7 %collective-permute-done.11.refs_7_ = f32[256,128]{1,0:T(8,128)S(1)} collective-permute-done((f32[256,128]{1,0:T(8,128)S(1)}, f32[256,128]{1,0:T(8,128)S(1)}, u32[]{:S(2)}, u32[]{:S(2)}) %collective-permute-start.11) | collective-permute-done | bytes 131104 | tf_op jit(solution)/shard_map/ppermute | solution.py:493
  46.3 0.1 shard_map.135.refs_0_
  46.4 2.0 %collective-permute-start.18 = (f32[256,128]{1,0:T(8,128)S(1)}, f32[256,128]{1,0:T(8,128)S(1)}, u32[]{:S(2)}, u32[]{:S(2)}) collective-permute-start(f32[256,128]{1,0:T(8,128)S(1)} %shard_map.135.refs_0_), channel_id=1, source_target_pairs={{0,224},{32,192},{64,160},{96,128},{128,96},{160,64},{192,32},{224... | collective-permute-start | bytes 393224 | tf_op jit(solution)/shard_map/ppermute | solution.py:493
  48.3 1.9 %collective-permute-start.17 = (f32[256,128]{1,0:T(8,128)S(1)}, f32[256,128]{1,0:T(8,128)S(1)}, u32[]{:S(2)}, u32[]{:S(2)}) collective-permute-start(f32[256,128]{1,0:T(8,128)S(1)} %shard_map.135.refs_0_), channel_id=1, source_target_pairs={{0,160},{32,128},{64,224},{96,192},{128,32},{160,0},{192,96},{224,... | collective-permute-start | bytes 393224 | tf_op jit(solution)/shard_map/ppermute | solution.py:493
  50.3 2.0 %collective-permute-start.16 = (f32[256,128]{1,0:T(8,128)S(1)}, f32[256,128]{1,0:T(8,128)S(1)}, u32[]{:S(2)}, u32[]{:S(2)}) collective-permute-start(f32[256,128]{1,0:T(8,128)S(1)} %shard_map.135.refs_0_), channel_id=1, source_target_pairs={{0,96},{32,64},{64,32},{96,0},{128,224},{160,192},{192,160},{224,1... | collective-permute-start | bytes 393224 | tf_op jit(solution)/shard_map/ppermute | solution.py:493
  52.3 0.8 %collective-permute-start.15 = (f32[256,128]{1,0:T(8,128)S(1)}, f32[256,128]{1,0:T(8,128)S(1)}, u32[]{:S(2)}, u32[]{:S(2)}) collective-permute-start(f32[256,128]{1,0:T(8,128)S(1)} %shard_map.135.refs_0_), channel_id=1, source_target_pairs={{0,32},{32,0},{64,96},{96,64},{128,160},{160,128},{192,224},{224,1... | collective-permute-start | bytes 393224 | tf_op jit(solution)/shard_map/ppermute | solution.py:493
  53.1 1.1 %collective-permute-start.14 = (f32[256,128]{1,0:T(8,128)S(1)}, f32[256,128]{1,0:T(8,128)S(1)}, u32[]{:S(2)}, u32[]{:S(2)}) collective-permute-start(f32[256,128]{1,0:T(8,128)S(1)} %shard_map.135.refs_0_), channel_id=1, source_target_pairs={{0,192},{32,224},{64,128},{96,160},{128,64},{160,96},{192,0},{224,... | collective-permute-start | bytes 393224 | tf_op jit(solution)/shard_map/ppermute | solution.py:493
  54.2 1.5 %collective-permute-done.18.refs_3_ = f32[256,128]{1,0:T(8,128)S(1)} collective-permute-done((f32[256,128]{1,0:T(8,128)S(1)}, f32[256,128]{1,0:T(8,128)S(1)}, u32[]{:S(2)}, u32[]{:S(2)}) %collective-permute-start.18) | collective-permute-done | bytes 131104 | tf_op jit(solution)/shard_map/ppermute | solution.py:493
  55.7 0.2 collective-permute-start.13
  55.8 1.6 %collective-permute-done.17.refs_2_ = f32[256,128]{1,0:T(8,128)S(1)} collective-permute-done((f32[256,128]{1,0:T(8,128)S(1)}, f32[256,128]{1,0:T(8,128)S(1)}, u32[]{:S(2)}, u32[]{:S(2)}) %collective-permute-start.17) | collective-permute-done | bytes 131104 | tf_op jit(solution)/shard_map/ppermute | solution.py:493
  57.5 1.4 %collective-permute-start.12 = (f32[256,128]{1,0:T(8,128)S(1)}, f32[256,128]{1,0:T(8,128)S(1)}, u32[]{:S(2)}, u32[]{:S(2)}) collective-permute-start(f32[256,128]{1,0:T(8,128)S(1)} %shard_map.135.refs_0_), channel_id=1, source_target_pairs={{0,64},{32,96},{64,0},{96,32},{128,192},{160,224},{192,128},{224,1... | collective-permute-start | bytes 393224 | tf_op jit(solution)/shard_map/ppermute | solution.py:493
  58.9 0.7 collective-permute-done.16.refs_1_
  59.6 1.4 %collective-permute-done.15.refs_0_ = f32[256,128]{1,0:T(8,128)S(1)} collective-permute-done((f32[256,128]{1,0:T(8,128)S(1)}, f32[256,128]{1,0:T(8,128)S(1)}, u32[]{:S(2)}, u32[]{:S(2)}) %collective-permute-start.15) | collective-permute-done | bytes 131104 | tf_op jit(solution)/shard_map/ppermute | solution.py:493
  61.1 0.5 collective-permute-done.14.refs_3_
  61.7 1.9 %collective-permute-done.13.refs_2_ = f32[256,128]{1,0:T(8,128)S(1)} collective-permute-done((f32[256,128]{1,0:T(8,128)S(1)}, f32[256,128]{1,0:T(8,128)S(1)}, u32[]{:S(2)}, u32[]{:S(2)}) %collective-permute-start.13) | collective-permute-done | bytes 131104 | tf_op jit(solution)/shard_map/ppermute | solution.py:493
  63.5 0.5 collective-permute-done.12.refs_1_
  64.1 0.1 collective-permute-start.19
  64.2 0.5 collective-permute-start.20
  64.7 1.4 %collective-permute-done.19.their_even = f32[4,256,128]{2,1,0:T(8,128)S(1)} collective-permute-done((f32[4,256,128]{2,1,0:T(8,128)S(1)}, f32[4,256,128]{2,1,0:T(8,128)S(1)}, u32[]{:S(2)}, u32[]{:S(2)}) %collective-permute-start.19) | collective-permute-done | bytes 524320 | tf_op jit(solution)/shard_map/ppermute | solution.py:497
  66.1 0.7 collective-permute-done.20.their_odd
  66.9 0.5 shard_map.138.pieces
  67.4 0.7 collective-permute-start.21
  68.1 2.3 %shard_map.141 = (f32[512,512]{1,0:T(8,128)S(1)}, f32[528,640]{1,0:T(8,128)S(1)}, f32[48,640]{1,0:T(8,128)S(1)}, f32[48,640]{1,0:T(8,128)S(1)}) custom-call(f32[16,128,128]{2,1,0:T(8,128)S(1)} %shard_map.138.pieces, f32[528,640]{1,0:T(8,128)S(1)} %get-tuple-element.46.slope, f32[512,512]{1,0:T(8,128)S(1)} %get-tuple-element.47.share, ...), custom_call_target="tpu_custom_call" | custom-call | flops 2000000000 | bytes 7413760 | tf_op jit(solution)/shard_map/pallas_call | solution.py:467
  70.4 2.5 %collective-permute-done.21.lat_in = f32[16,512]{1,0:T(8,128)S(1)} collective-permute-done((f32[16,512]{1,0:T(8,128)S(1)}, f32[16,512]{1,0:T(8,128)S(1)}, u32[]{:S(2)}, u32[]{:S(2)}) %collective-permute-start.21) | collective-permute-done | bytes 32800 | tf_op jit(solution)/shard_map/ppermute | solution.py:479
  72.9 0.2 shard_map.140
  73.1 0.1 collective-permute-start.22
  73.2 3.3 %collective-permute-start.23 = (f32[16,640]{1,0:T(8,128)S(1)}, f32[16,640]{1,0:T(8,128)S(1)}, u32[]{:S(2)}, u32[]{:S(2)}) collective-permute-start(f32[16,640]{1,0:T(8,128)S(1)} %get-tuple-element.45), channel_id=1, source_target_pairs={{0,7},{1,2},{2,1},{3,4},{4,3},{5,6},{6,5},{7,0},{8,15},{9,10},{10,... | collective-permute-start | bytes 122888 | tf_op jit(solution)/shard_map/ppermute | solution.py:486
  76.5 2.3 %shard_map.142.scaling_part = f32[512,512]{1,0:T(8,128)S(1)} custom-call(f32[528,640]{1,0:T(8,128)S(1)} %get-tuple-element.51.sloped, bf16[128,144]{1,0:T(8,128)(2,1)S(1)} %copy-done.8, bf16[128,144]{1,0:T(8,128)(2,1)S(1)} %copy-done.7, bf16[512,256]{1,0:T(8,128)(2,1)S(1)} %copy-done.4, bf16[512,256]{1,0:T(8,128)(2,1)S(1)} %copy-done.3), custom_call_target="tpu_custom_call" | custom-call | flops 2000000000 | bytes 3596288 | tf_op jit(solution)/shard_map/pallas_call | solution.py:467
  78.8 0.0 collective-permute-done.22.even
  78.8 0.0 collective-permute-done.23.odd
  78.9 2.9 %shard_map.143 = (f32[512,512]{1,0:T(8,128)}, f32[512,512]{1,0:T(8,128)}) custom-call(f32[16,512]{1,0:T(8,128)S(1)} %collective-permute-done.21.lat_in, f32[16,640]{1,0:T(8,128)S(1)} %collective-permute-done.22.even, f32[16,640]{1,0:T(8,128)S(1)} %collective-permute-done.23.odd, f32[48,640]{1,0:T(8,128)S(1)} %get-tuple-element.48.slope_edge, ...), custom_call_target="tpu_custom_call" | custom-call | flops 1000000000 | bytes 4591616 | tf_op jit(solution)/shard_map/pallas_call | solution.py:467
  (20 shorter events, 0.1 us)
Async XLA Ops:
  0.6 6.7 %copy-start = (f32[1,512,512]{2,1,0:T(8,128)S(1)}, f32[1,512,512]{2,1,0:T(8,128)}, u32[]{:S(2)}) copy-start(f32[1,512,512]{2,1,0:T(8,128)} %param.13) | copy-start | bytes 3145732
  0.6 6.7 %copy-start.1 = (f32[1,512,512]{2,1,0:T(8,128)S(1)}, f32[1,512,512]{2,1,0:T(8,128)}, u32[]{:S(2)}) copy-start(f32[1,512,512]{2,1,0:T(8,128)} %param.12) | copy-start | bytes 3145732
  1.6 15.3 %copy-start.2 = (f32[1,512,512]{2,1,0:T(8,128)S(1)}, f32[1,512,512]{2,1,0:T(8,128)}, u32[]{:S(2)}) copy-start(f32[1,512,512]{2,1,0:T(8,128)} %param.15) | copy-start | bytes 3145732
  1.6 15.3 %copy-start.3 = (bf16[512,256]{1,0:T(8,128)(2,1)S(1)}, bf16[512,256]{1,0:T(8,128)(2,1)}, u32[]{:S(2)}) copy-start(bf16[512,256]{1,0:T(8,128)(2,1)} %constant.21.clone.cl) | copy-start | bytes 786436
  1.6 15.3 %copy-start.4 = (bf16[512,256]{1,0:T(8,128)(2,1)S(1)}, bf16[512,256]{1,0:T(8,128)(2,1)}, u32[]{:S(2)}) copy-start(bf16[512,256]{1,0:T(8,128)(2,1)} %constant.20.clone.ch) | copy-start | bytes 786436
  1.6 15.3 %copy-start.5 = (bf16[176,192]{1,0:T(8,128)(2,1)S(1)}, bf16[176,192]{1,0:T(8,128)(2,1)}, u32[]{:S(2)}) copy-start(bf16[176,192]{1,0:T(8,128)(2,1)} %constant.17.clone.rl3) | copy-start | bytes 202756
  1.6 15.3 %copy-start.6 = (bf16[176,192]{1,0:T(8,128)(2,1)S(1)}, bf16[176,192]{1,0:T(8,128)(2,1)}, u32[]{:S(2)}) copy-start(bf16[176,192]{1,0:T(8,128)(2,1)} %constant.16.clone.rh3) | copy-start | bytes 202756
  1.7 15.3 %copy-start.7 = (bf16[128,144]{1,0:T(8,128)(2,1)S(1)}, bf16[128,144]{1,0:T(8,128)(2,1)}, u32[]{:S(2)}) copy-start(bf16[128,144]{1,0:T(8,128)(2,1)} %constant.19.clone.rl4) | copy-start | bytes 110596
  1.7 15.3 %copy-start.8 = (bf16[128,144]{1,0:T(8,128)(2,1)S(1)}, bf16[128,144]{1,0:T(8,128)(2,1)}, u32[]{:S(2)}) copy-start(bf16[128,144]{1,0:T(8,128)(2,1)} %constant.18.clone.rh4) | copy-start | bytes 110596
  1.7 5.7 %collective-permute-start = (f32[24,512]{1,0:T(8,128)S(1)}, f32[24,512]{1,0:T(8,128)S(1)}, u32[]{:S(2)}, u32[]{:S(2)}) collective-permute-start(f32[24,512]{1,0:T(8,128)S(1)} %lat_edges.1), channel_id=1, source_target_pairs={{0,8},{8,0},{1,9},{9,1},{2,10},{10,2},{3,11},{11,3},{4,12},{12,4},... | collective-permute-start | bytes 147464 | tf_op jit(solution)/shard_map/ppermute | solution.py:479
  7.7 7.6 %collective-permute-start.1 = (f32[24,640]{1,0:T(8,128)S(1)}, f32[24,640]{1,0:T(8,128)S(1)}, u32[]{:S(2)}, u32[]{:S(2)}) collective-permute-start(f32[24,640]{1,0:T(8,128)S(1)} %get-tuple-element.28), channel_id=1, source_target_pairs={{0,1},{1,0},{2,3},{3,2},{4,5},{5,4},{6,7},{7,6},{8,9},{9,8},{10,11... | collective-permute-start | bytes 184328 | tf_op jit(solution)/shard_map/ppermute | solution.py:486
  9.7 7.1 %collective-permute-start.2 = (f32[24,640]{1,0:T(8,128)S(1)}, f32[24,640]{1,0:T(8,128)S(1)}, u32[]{:S(2)}, u32[]{:S(2)}) collective-permute-start(f32[24,640]{1,0:T(8,128)S(1)} %get-tuple-element.29), channel_id=1, source_target_pairs={{0,7},{1,2},{2,1},{3,4},{4,3},{5,6},{6,5},{7,0},{8,15},{9,10},{10,... | collective-permute-start | bytes 184328 | tf_op jit(solution)/shard_map/ppermute | solution.py:486
  21.9 2.0 %collective-permute-start.3 = (f32[4,256,128]{2,1,0:T(8,128)S(1)}, f32[4,256,128]{2,1,0:T(8,128)S(1)}, u32[]{:S(2)}, u32[]{:S(2)}) collective-permute-start(f32[4,256,128]{2,1,0:T(8,128)S(1)} %get-tuple-element.31), channel_id=1, source_target_pairs={{0,16},{16,0},{1,17},{17,1},{2,18},{18,2},{3,19},{19,3},{4,20},{20... | collective-permute-start | bytes 1572872 | tf_op jit(solution)/shard_map/ppermute | solution.py:497
  22.0 9.1 %collective-permute-start.8 = (f32[4,256,128]{2,1,0:T(8,128)S(1)}, f32[4,256,128]{2,1,0:T(8,128)S(1)}, u32[]{:S(2)}, u32[]{:S(2)}) collective-permute-start(f32[4,256,128]{2,1,0:T(8,128)S(1)} %get-tuple-element.37), channel_id=1, source_target_pairs={{0,16},{16,0},{1,17},{17,1},{2,18},{18,2},{3,19},{19,3},{4,20},{20... | collective-permute-start | bytes 1572872 | tf_op jit(solution)/shard_map/ppermute | solution.py:497
  23.9 7.7 %collective-permute-start.4 = (f32[256,128]{1,0:T(8,128)S(1)}, f32[256,128]{1,0:T(8,128)S(1)}, u32[]{:S(2)}, u32[]{:S(2)}) collective-permute-start(f32[256,128]{1,0:T(8,128)S(1)} %get-tuple-element.32), channel_id=1, source_target_pairs={{0,32},{32,0},{64,96},{96,64},{128,160},{160,128},{192,224},{224,1... | collective-permute-start | bytes 393224 | tf_op jit(solution)/shard_map/ppermute | solution.py:493
  25.2 10.5 %collective-permute-start.5 = (f32[256,128]{1,0:T(8,128)S(1)}, f32[256,128]{1,0:T(8,128)S(1)}, u32[]{:S(2)}, u32[]{:S(2)}) collective-permute-start(f32[256,128]{1,0:T(8,128)S(1)} %get-tuple-element.33), channel_id=1, source_target_pairs={{0,96},{32,64},{64,32},{96,0},{128,224},{160,192},{192,160},{224,1... | collective-permute-start | bytes 393224 | tf_op jit(solution)/shard_map/ppermute | solution.py:493
  27.1 11.9 %collective-permute-start.6 = (f32[256,128]{1,0:T(8,128)S(1)}, f32[256,128]{1,0:T(8,128)S(1)}, u32[]{:S(2)}, u32[]{:S(2)}) collective-permute-start(f32[256,128]{1,0:T(8,128)S(1)} %get-tuple-element.34), channel_id=1, source_target_pairs={{0,160},{32,128},{64,224},{96,192},{128,32},{160,0},{192,96},{224,... | collective-permute-start | bytes 393224 | tf_op jit(solution)/shard_map/ppermute | solution.py:493
  30.6 10.4 %collective-permute-start.7 = (f32[256,128]{1,0:T(8,128)S(1)}, f32[256,128]{1,0:T(8,128)S(1)}, u32[]{:S(2)}, u32[]{:S(2)}) collective-permute-start(f32[256,128]{1,0:T(8,128)S(1)} %get-tuple-element.35), channel_id=1, source_target_pairs={{0,224},{32,192},{64,160},{96,128},{128,96},{160,64},{192,32},{224... | collective-permute-start | bytes 393224 | tf_op jit(solution)/shard_map/ppermute | solution.py:493
  31.1 9.8 %collective-permute-start.9 = (f32[256,128]{1,0:T(8,128)S(1)}, f32[256,128]{1,0:T(8,128)S(1)}, u32[]{:S(2)}, u32[]{:S(2)}) collective-permute-start(f32[256,128]{1,0:T(8,128)S(1)} %get-tuple-element.39), channel_id=1, source_target_pairs={{0,64},{32,96},{64,0},{96,32},{128,192},{160,224},{192,128},{224,1... | collective-permute-start | bytes 393224 | tf_op jit(solution)/shard_map/ppermute | solution.py:493
  31.6 12.0 %collective-permute-start.10 = (f32[256,128]{1,0:T(8,128)S(1)}, f32[256,128]{1,0:T(8,128)S(1)}, u32[]{:S(2)}, u32[]{:S(2)}) collective-permute-start(f32[256,128]{1,0:T(8,128)S(1)} %get-tuple-element.40), channel_id=1, source_target_pairs={{0,128},{32,160},{64,192},{96,224},{128,0},{160,32},{192,64},{224,... | collective-permute-start | bytes 393224 | tf_op jit(solution)/shard_map/ppermute | solution.py:493
  35.7 10.6 %collective-permute-start.11 = (f32[256,128]{1,0:T(8,128)S(1)}, f32[256,128]{1,0:T(8,128)S(1)}, u32[]{:S(2)}, u32[]{:S(2)}) collective-permute-start(f32[256,128]{1,0:T(8,128)S(1)} %get-tuple-element.41), channel_id=1, source_target_pairs={{0,192},{32,224},{64,128},{96,160},{128,64},{160,96},{192,0},{224,... | collective-permute-start | bytes 393224 | tf_op jit(solution)/shard_map/ppermute | solution.py:493
  46.4 9.3 %collective-permute-start.18 = (f32[256,128]{1,0:T(8,128)S(1)}, f32[256,128]{1,0:T(8,128)S(1)}, u32[]{:S(2)}, u32[]{:S(2)}) collective-permute-start(f32[256,128]{1,0:T(8,128)S(1)} %shard_map.135.refs_0_), channel_id=1, source_target_pairs={{0,224},{32,192},{64,160},{96,128},{128,96},{160,64},{192,32},{224... | collective-permute-start | bytes 393224 | tf_op jit(solution)/shard_map/ppermute | solution.py:493
  48.3 9.1 %collective-permute-start.17 = (f32[256,128]{1,0:T(8,128)S(1)}, f32[256,128]{1,0:T(8,128)S(1)}, u32[]{:S(2)}, u32[]{:S(2)}) collective-permute-start(f32[256,128]{1,0:T(8,128)S(1)} %shard_map.135.refs_0_), channel_id=1, source_target_pairs={{0,160},{32,128},{64,224},{96,192},{128,32},{160,0},{192,96},{224,... | collective-permute-start | bytes 393224 | tf_op jit(solution)/shard_map/ppermute | solution.py:493
  50.3 9.4 %collective-permute-start.16 = (f32[256,128]{1,0:T(8,128)S(1)}, f32[256,128]{1,0:T(8,128)S(1)}, u32[]{:S(2)}, u32[]{:S(2)}) collective-permute-start(f32[256,128]{1,0:T(8,128)S(1)} %shard_map.135.refs_0_), channel_id=1, source_target_pairs={{0,96},{32,64},{64,32},{96,0},{128,224},{160,192},{192,160},{224,1... | collective-permute-start | bytes 393224 | tf_op jit(solution)/shard_map/ppermute | solution.py:493
  52.3 8.8 %collective-permute-start.15 = (f32[256,128]{1,0:T(8,128)S(1)}, f32[256,128]{1,0:T(8,128)S(1)}, u32[]{:S(2)}, u32[]{:S(2)}) collective-permute-start(f32[256,128]{1,0:T(8,128)S(1)} %shard_map.135.refs_0_), channel_id=1, source_target_pairs={{0,32},{32,0},{64,96},{96,64},{128,160},{160,128},{192,224},{224,1... | collective-permute-start | bytes 393224 | tf_op jit(solution)/shard_map/ppermute | solution.py:493
  53.1 8.6 %collective-permute-start.14 = (f32[256,128]{1,0:T(8,128)S(1)}, f32[256,128]{1,0:T(8,128)S(1)}, u32[]{:S(2)}, u32[]{:S(2)}) collective-permute-start(f32[256,128]{1,0:T(8,128)S(1)} %shard_map.135.refs_0_), channel_id=1, source_target_pairs={{0,192},{32,224},{64,128},{96,160},{128,64},{160,96},{192,0},{224,... | collective-permute-start | bytes 393224 | tf_op jit(solution)/shard_map/ppermute | solution.py:493
  55.7 7.9 %collective-permute-start.13 = (f32[256,128]{1,0:T(8,128)S(1)}, f32[256,128]{1,0:T(8,128)S(1)}, u32[]{:S(2)}, u32[]{:S(2)}) collective-permute-start(f32[256,128]{1,0:T(8,128)S(1)} %shard_map.135.refs_0_), channel_id=1, source_target_pairs={{0,128},{32,160},{64,192},{96,224},{128,0},{160,32},{192,64},{224,... | collective-permute-start | bytes 393224 | tf_op jit(solution)/shard_map/ppermute | solution.py:493
  57.5 6.6 %collective-permute-start.12 = (f32[256,128]{1,0:T(8,128)S(1)}, f32[256,128]{1,0:T(8,128)S(1)}, u32[]{:S(2)}, u32[]{:S(2)}) collective-permute-start(f32[256,128]{1,0:T(8,128)S(1)} %shard_map.135.refs_0_), channel_id=1, source_target_pairs={{0,64},{32,96},{64,0},{96,32},{128,192},{160,224},{192,128},{224,1... | collective-permute-start | bytes 393224 | tf_op jit(solution)/shard_map/ppermute | solution.py:493
  64.1 2.0 %collective-permute-start.19 = (f32[4,256,128]{2,1,0:T(8,128)S(1)}, f32[4,256,128]{2,1,0:T(8,128)S(1)}, u32[]{:S(2)}, u32[]{:S(2)}) collective-permute-start(f32[4,256,128]{2,1,0:T(8,128)S(1)} %shard_map.137.even), channel_id=1, source_target_pairs={{0,16},{16,0},{1,17},{17,1},{2,18},{18,2},{3,19},{19,3},{4,20},{20... | collective-permute-start | bytes 1572872 | tf_op jit(solution)/shard_map/ppermute | solution.py:497
  64.2 2.6 %collective-permute-start.20 = (f32[4,256,128]{2,1,0:T(8,128)S(1)}, f32[4,256,128]{2,1,0:T(8,128)S(1)}, u32[]{:S(2)}, u32[]{:S(2)}) collective-permute-start(f32[4,256,128]{2,1,0:T(8,128)S(1)} %shard_map.136.refs_4_.odd), channel_id=1, source_target_pairs={{0,16},{16,0},{1,17},{17,1},{2,18},{18,2},{3,19},{19,3},{4,20},{20... | collective-permute-start | bytes 1572872 | tf_op jit(solution)/shard_map/ppermute | solution.py:497
  67.4 5.5 %collective-permute-start.21 = (f32[16,512]{1,0:T(8,128)S(1)}, f32[16,512]{1,0:T(8,128)S(1)}, u32[]{:S(2)}, u32[]{:S(2)}) collective-permute-start(f32[16,512]{1,0:T(8,128)S(1)} %shard_map.139), channel_id=1, source_target_pairs={{0,8},{8,0},{1,9},{9,1},{2,10},{10,2},{3,11},{11,3},{4,12},{12,4},... | collective-permute-start | bytes 98312 | tf_op jit(solution)/shard_map/ppermute | solution.py:479
  73.1 5.7 %collective-permute-start.22 = (f32[16,640]{1,0:T(8,128)S(1)}, f32[16,640]{1,0:T(8,128)S(1)}, u32[]{:S(2)}, u32[]{:S(2)}) collective-permute-start(f32[16,640]{1,0:T(8,128)S(1)} %get-tuple-element.44), channel_id=1, source_target_pairs={{0,1},{1,0},{2,3},{3,2},{4,5},{5,4},{6,7},{7,6},{8,9},{9,8},{10,11... | collective-permute-start | bytes 122888 | tf_op jit(solution)/shard_map/ppermute | solution.py:486
  73.2 5.6 %collective-permute-start.23 = (f32[16,640]{1,0:T(8,128)S(1)}, f32[16,640]{1,0:T(8,128)S(1)}, u32[]{:S(2)}, u32[]{:S(2)}) collective-permute-start(f32[16,640]{1,0:T(8,128)S(1)} %get-tuple-element.45), channel_id=1, source_target_pairs={{0,7},{1,2},{2,1},{3,4},{4,3},{5,6},{6,5},{7,0},{8,15},{9,10},{10,... | collective-permute-start | bytes 122888 | tf_op jit(solution)/shard_map/ppermute | solution.py:486
  76.5 2.3 %copy-start.9 = (bf16[2,48,48]{2,1,0:T(8,128)(2,1)S(1)}, bf16[2,48,48]{2,1,0:T(8,128)(2,1)}, u32[]{:S(2)}) copy-start(bf16[2,48,48]{2,1,0:T(8,128)(2,1)} %constant.23.clone.dl) | copy-start | bytes 27652
  76.5 2.3 %copy-start.10 = (bf16[2,48,48]{2,1,0:T(8,128)(2,1)S(1)}, bf16[2,48,48]{2,1,0:T(8,128)(2,1)}, u32[]{:S(2)}) copy-start(bf16[2,48,48]{2,1,0:T(8,128)(2,1)} %constant.22.clone.dh) | copy-start | bytes 27652

commit v2 on v1

--- a/solution.py
+++ b/solution.py
@@ -44,7 +44,7 @@
 def row_band(size):
     outer = np.arange(size)[:, None]
     inner = np.arange(size + 2 * RADIUS)[None, :]
-    return halves(taps_of((inner - outer - RADIUS).astype(np.float64)))
+    return jnp.concatenate(halves(taps_of((inner - outer - RADIUS).astype(np.float64))), axis=0)
 
 
 def edge_bands():
@@ -74,16 +74,20 @@
     return jnp.dot(a, b, preferred_element_type=F32)
 
 
-def rows_pass(x, high, low):
+def rows_pass(x, both):
     xh, xl = split(x)
-    return dot(high[...], xh) + (dot(low[...], xh) + dot(high[...], xl))
+    rows = both.shape[0] // 2
+    twice = dot(both[...], xh)
+    return twice[0:rows] + (twice[rows:] + dot(both[0:rows, :], xl))
 
 
 def cols_piece(rh, rl, ch, cl, spans, count):
     total = None
     for lo, hi, at in spans:
         high, low = ch[at : at + hi - lo, 0:count], cl[at : at + hi - lo, 0:count]
-        part = dot(rh[:, lo:hi], high) + (dot(rl[:, lo:hi], high) + dot(rh[:, lo:hi], low))
+        rows = rh.shape[0]
+        twice = dot(jnp.concatenate([rh[:, lo:hi], rl[:, lo:hi]], axis=0), high)
+        part = twice[0:rows] + (twice[rows:] + dot(rh[:, lo:hi], low))
         total = part if total is None else total + part
     return total
 
@@ -184,12 +188,9 @@
 
 
 def forward_kernel(
-    weight, scaling, precip, upstream, lat_in, even, odd, rh3, rl3, rh4, rl4, ch, cl,
-    slope, share, second, logs, keep_even, keep_odd, give_even, give_odd, sx, px, side, lifted,
+    scaling, precip, lat_in, even, odd, both3, ch, cl, slope, share, lifted, sx, px, side
 ):
     lat = my_lat()
-    core = lax.axis_index("hour_2")
-    far, near = lax.axis_index("hour_0"), lax.axis_index("hour_1")
     wide, narrow = 2 * RADIUS, RADIUS
     sx[wide : wide + ROWS, 0:COLS] = scaling[...]
     px[narrow : narrow + ROWS, 0:COLS] = precip[...]
@@ -197,7 +198,7 @@
     fill_edges(px, narrow, lat_in[wide:STRIP, :], even[wide:STRIP, :], odd[wide:STRIP, :], side)
     for i in range(3):
         at = BLOCK * i
-        r = rows_pass(sx[at : at + BLOCK + 2 * RADIUS, :], rh3, rl3)
+        r = rows_pass(sx[at : at + BLOCK + 2 * RADIUS, :], both3)
         a = cols_pass(r, ch, cl, True)
         rain = px[at : at + BLOCK, :]
         inside = valid_part(at, BLOCK, lat)
@@ -207,28 +208,36 @@
         lo, hi = max(at, RADIUS), min(at + BLOCK, RADIUS + ROWS)
         here = slice(lo - RADIUS, hi - RADIUS)
         share[here, :] = PHI * u[lo - at : hi - at, 0:COLS] / rain[lo - at : hi - at, 0:COLS]
-    for i in range(4):
-        at = EDGE * i
-        r = rows_pass(lifted[at : at + EDGE + 2 * RADIUS, :], rh4, rl4)
+
+
+def half_start(flip):
+    near = lax.axis_index("hour_1")
+    return pl.multiple_of(((1 - near) if flip else near) * (ROWS // 2), ROWS // 2)
+
+
+def log_kernel(flip, weight, lifted, upstream, both4, ch, cl, second, logs, keep, give):
+    core, far = lax.axis_index("hour_2"), lax.axis_index("hour_0")
+    for i in range(2):
+        at = half_start(flip) + EDGE * i
+        r = rows_pass(lifted[pl.ds(at, EDGE + 2 * RADIUS), :], both4)
         b = cols_pass(r, ch, cl, False)
         logb = jnp.log(b)
-        parts = (weight[0] * logb, upstream[at : at + EDGE, :] * jnp.exp(-PHI * logb))
+        parts = (
+            weight[0] * logb, upstream[pl.ds(at, EDGE), :] * jnp.exp(-PHI * logb)
+        )
         for j in range(COLS // EDGE):
             lanes = slice(EDGE * j, EDGE * (j + 1))
-            for q in range(EDGE // PIECE):
-                rows = slice(PIECE * q, PIECE * (q + 1))
+            four = [slice(PIECE * q, PIECE * (q + 1)) for q in range(4)]
+            for q, rows in enumerate(four):
                 to = slice(PIECE * j, PIECE * (j + 1))
-                second[i * (EDGE // PIECE) + q, to, :] = b[rows, lanes]
-                logs[i * (EDGE // PIECE) + q, to, :] = logb[rows, lanes]
+                second[4 * i + q, to, :] = b[rows, lanes]
+                logs[4 * i + q, to, :] = logb[rows, lanes]
             for k, part in enumerate(parts):
                 to = slice(EDGE * k + PIECE * j, EDGE * k + PIECE * (j + 1))
-                four = [part[PIECE * q : PIECE * (q + 1), lanes] for q in range(4)]
-                stay = [jnp.where(core == 0, four[2 * c], four[2 * c + 1]) for c in range(2)]
-                leave = [jnp.where(core == 0, four[2 * c + 1], four[2 * c]) for c in range(2)]
-                keep_even[i ^ far, to, :] = jnp.where(near == 0, stay[0], stay[1])
-                keep_odd[i ^ far, to, :] = jnp.where(near == 0, stay[1], stay[0])
-                give_even[i ^ far, to, :] = jnp.where(near == 0, leave[0], leave[1])
-                give_odd[i ^ far, to, :] = jnp.where(near == 0, leave[1], leave[0])
+                for c in range(2):
+                    x, y = part[four[2 * c], lanes], part[four[2 * c + 1], lanes]
+                    keep[(2 * i + c) ^ far, to, :] = jnp.where(core == 0, x, y)
+                    give[(2 * i + c) ^ far, to, :] = jnp.where(core == 0, y, x)
 
 
 def pair_kernel(keep, given, *outs):
@@ -256,31 +265,26 @@
 
 
 def db_kernel(
-    weight, even, odd, their_even, their_odd, upstream, second, logs, pieces
+    weight, even, odd, their_even, their_odd, upstream, second_even, second_odd, logs_even,
+    logs_odd, pieces,
 ):
-    core = lax.axis_index("hour_2")
-    far, near = lax.axis_index("hour_0"), lax.axis_index("hour_1")
-    for i in range(CHIPS // 2):
-        for own in range(2):
-            here = core == own
+    core, far = lax.axis_index("hour_2"), lax.axis_index("hour_0")
+    for flip, mine, theirs, second, logs in (
+        (False, even, their_even, second_even, logs_even),
+        (True, odd, their_odd, second_odd, logs_odd),
+    ):
+        start = half_start(flip)
+        first = start // PIECE
+        for n in range(PIECES // 2):
+            here, slot = core == n % 2, (n // 2) ^ far
             for j in range(COLS // EDGE):
                 rows = slice(PIECE * j, PIECE * (j + 1))
                 low = slice(EDGE + PIECE * j, EDGE + PIECE * (j + 1))
-                found = [
-                    [
-                        jnp.where(here, mine[i ^ far, part, :], theirs[i ^ far, part, :])
-                        for part in (rows, low)
-                    ]
-                    for mine, theirs in ((even, their_even), (odd, their_odd))
-                ]
-                for c in range(2):
-                    logq, dlogq = (
-                        jnp.where(near == c, same, other) for same, other in zip(*found)
-                    )
-                    p = 4 * i + 2 * c + own
-                    value = upstream[PIECE * p : PIECE * (p + 1), EDGE * j : EDGE * (j + 1)]
-                    term = PHI * value * jnp.exp(PHI * (logq - logs[p, rows, :]))
-                    pieces[p, rows, :] = (weight[0] * dlogq - term) / second[p, rows, :]
+                logq = jnp.where(here, mine[slot, rows, :], theirs[slot, rows, :])
+                dlogq = jnp.where(here, mine[slot, low, :], theirs[slot, low, :])
+                value = upstream[pl.ds(start + PIECE * n, PIECE), EDGE * j : EDGE * (j + 1)]
+                term = PHI * value * jnp.exp(PHI * (logq - logs[n, rows, :]))
+                pieces[first + n, rows, :] = (weight[0] * dlogq - term) / second[n, rows, :]
 
 
 def tile_column(pieces, j):
@@ -333,7 +337,7 @@
 
 
 def back_first_kernel(
-    pieces, slope, share, rh3, rl3, ch, cl, grad_precip, sloped, slope_edge, share_edge, dx
+    pieces, slope, share, both3, ch, cl, grad_precip, sloped, slope_edge, share_edge, dx
 ):
     coefficient_strips(slope, share, slope_edge, share_edge)
     wide = 2 * RADIUS
@@ -346,7 +350,7 @@
             ]
     for i in range(3):
         at = BLOCK * i
-        rh, rl = split(rows_pass(dx[at : at + BLOCK + 2 * RADIUS, :], rh3, rl3))
+        rh, rl = split(rows_pass(dx[at : at + BLOCK + 2 * RADIUS, :], both3))
         du = jnp.concatenate(
             [
                 cols_piece(rh, rl, ch, cl, ((0, 384, 128),), 256),
@@ -361,10 +365,10 @@
         grad_precip[here, :] = share[here, :] * du[lo - at : hi - at, 0:COLS]
 
 
-def back_second_kernel(sloped, rh4, rl4, ch, cl, grad_scaling):
+def back_second_kernel(sloped, both4, ch, cl, grad_scaling):
     for i in range(4):
         at = EDGE * i
-        r = rows_pass(sloped[at : at + EDGE + 2 * RADIUS, :], rh4, rl4)
+        r = rows_pass(sloped[at : at + EDGE + 2 * RADIUS, :], both4)
         grad_scaling[at : at + EDGE, :] = cols_pass(r, ch, cl, False)
 
 
@@ -502,24 +506,35 @@
     incoming = scaling[0]
     upstream = cotangent[0]
     band3, band4, around = row_band(BLOCK), row_band(EDGE), col_band()
-    bands = (*band3, *band4, *around)
     to_lat = lat_strip(incoming, rainfall)
     lat_in = lat_swapped(to_lat)
     even, odd = lon_swapped(
         *call(lon_kernel, (incoming, rainfall, lat_in), ((STRIP, WIDE), (STRIP, WIDE)))
     )
     half = (CHIPS // 2, 2 * EDGE, EDGE)
-    whole = (PIECES, EDGE, EDGE)
-    slope, share, second, logs, keep_even, keep_odd, give_even, give_odd = call(
+    whole, part = (PIECES, EDGE, EDGE), (PIECES // 2, EDGE, EDGE)
+    slope, share, lifted = call(
         forward_kernel,
-        (hour_weight, incoming, rainfall, upstream, lat_in, even, odd, *bands),
-        ((TALL, WIDE), (ROWS, COLS), whole, whole, half, half, half, half),
-        scratch=((TALLER, WIDE), (TALL, WIDE), (EDGE, WIDE), (TALL, WIDE)),
-        scalars=1,
-        flops=4 * 10**9,
+        (incoming, rainfall, lat_in, even, odd, band3, *around),
+        ((TALL, WIDE), (ROWS, COLS), (TALL, WIDE)),
+        scratch=((TALLER, WIDE), (TALL, WIDE), (EDGE, WIDE)),
+        flops=2 * 10**9,
         room=14 << 20,
     )
+
+    def logged(flip, *after):
+        return call(
+            lambda *refs: log_kernel(flip, *refs[: 6], *refs[6 + len(after) :]),
+            (hour_weight, lifted, upstream, band4, *around, *after),
+            (part, part, half, half),
+            scalars=1,
+            flops=10**9,
+            room=14 << 20,
+        )
+
+    second_odd, logs_odd, keep_odd, give_odd = logged(True)
     given_odd = cores_swapped(give_odd)
+    second_even, logs_even, keep_even, give_even = logged(False, keep_odd)
     given_even = cores_swapped(give_even)
     arrived = []
     for keep, given, first in ((keep_odd, given_odd, 1), (keep_even, given_even, 0)):
@@ -537,7 +552,10 @@
     their_even = cores_swapped(even_part)
     (pieces,) = call(
         db_kernel,
-        (hour_weight, even_part, odd_part, their_even, their_odd, upstream, second, logs),
+        (
+            hour_weight, even_part, odd_part, their_even, their_odd, upstream, second_even,
+            second_odd, logs_even, logs_odd,
+        ),
         (whole,),
         scalars=1,
     )
@@ -548,14 +566,14 @@
     )
     precip_part, sloped, slope_edge, share_edge = call(
         back_first_kernel,
-        (pieces, slope, share, *band3, *around),
+        (pieces, slope, share, band3, *around),
         ((ROWS, COLS), (TALL, WIDE), (48, WIDE), (48, WIDE)),
         scratch=((TALLER, COLS),),
         flops=2 * 10**9,
         room=14 << 20,
     )
     (scaling_part,) = call(
-        back_second_kernel, (sloped, *band4, *around), ((ROWS, COLS),),
+        back_second_kernel, (sloped, band4, *around), ((ROWS, COLS),),
         flops=2 * 10**9, room=14 << 20,
     )
     grad_precip, grad_scaling = call(

time: 82.6 us -> 81.6 us (0.988)
  waiting for transfers between devices: 29.1 us -> 27.9 us
    ppermute x4, waiting for transfers between devices: 3.55 us -> 2.18 us  [cores_swapped(): return lax.ppermute(parts, 'hour_2', [(0, 1), (1, 0)])]
    pallas_call x13 -> x15, Pallas kernels: 13.8 us -> 14.2 us  [call(): pl.pallas_call(kernel, out_shape=[pltpu.HBM(o, F32) if out_hbm else jax.S...]
  transfers between devices with their start and end apart: 24 -> 24, of which waited for: 17 -> 16; matrix products, arithmetic and copies ran while one was open for 0% -> 0% of each run, Pallas kernels for 6% -> 7%
where the time goes in v2:
time: 81.6 us; the launch traced here: 81.2 us
  starting transfers between devices  36.4 us (45%)
  waiting for transfers between devices  27.9 us (34%)
  Pallas kernels  15.1 us (19%)
  between operations  1.69 us (2%)
    ppermute x14, starting transfers between devices, chip_swapped(): return lax.ppermute(part, ('hour_0', 'hour_1'), pairs)  21.8 us
    ppermute x14, waiting for transfers between devices, chip_swapped(): return lax.ppermute(part, ('hour_0', 'hour_1'), pairs)  18.1 us
    pallas_call x15, Pallas kernels, call(): pl.pallas_call(kernel, out_shape=[pltpu.HBM(o, F32) if out_hbm else jax.S...  14.2 us
    ppermute x2, starting transfers between devices, lon_swapped(): lax.ppermute(to_odd, 'lon', odd)  8.26 us
    ppermute x2, waiting for transfers between devices, lat_swapped(): return lax.ppermute(strip, 'lat', [(0, 1), (1, 0)])  6.1 us
    ppermute x2, starting transfers between devices, lat_swapped(): return lax.ppermute(strip, 'lat', [(0, 1), (1, 0)])  2.98 us
    ppermute x4, waiting for transfers between devices, cores_swapped(): return lax.ppermute(parts, 'hour_2', [(0, 1), (1, 0)])  2.18 us
    ppermute x2, starting transfers between devices, lon_swapped(): lax.ppermute(to_even, 'lon', even)  2.1 us
  transfers between devices with their start and end apart: 24, of which 16 were waited for; matrix products, arithmetic and copies ran while one was open for 0% of the time, Pallas kernels for 7%

profile of v2, /device:TPU:4, one launch (start us, length us, event | category | flops | bytes accessed | tf_op | source)
XLA Modules:
  0.0 81.2 jit_solution(12962987094363898869)
XLA Ops:
  0.6 0.9 %lat_edges.1 = f32[24,512]{1,0:T(8,128)S(1)} custom-call(f32[512,512]{1,0:T(8,128)} %bitcast.5, f32[512,512]{1,0:T(8,128)} %bitcast.8), custom_call_target="tpu_custom_call" | custom-call | tf_op jit(solution)/shard_map/lat_edges/pallas_call | solution.py:169
  1.6 0.0 copy-start.3
  1.6 0.0 copy-start.4
  1.6 0.0 copy-start.5
  1.6 2.3 %collective-permute-start = (f32[24,512]{1,0:T(8,128)S(1)}, f32[24,512]{1,0:T(8,128)S(1)}, u32[]{:S(2)}, u32[]{:S(2)}) collective-permute-start(f32[24,512]{1,0:T(8,128)S(1)} %lat_edges.1), channel_id=1, source_target_pairs={{0,8},{8,0},{1,9},{9,1},{2,10},{10,2},{3,11},{11,3},{4,12},{12,4},... | collective-permute-start | bytes 147464 | tf_op jit(solution)/shard_map/ppermute | solution.py:483
  3.9 3.4 %collective-permute-done.lat_in = f32[24,512]{1,0:T(8,128)S(1)} collective-permute-done((f32[24,512]{1,0:T(8,128)S(1)}, f32[24,512]{1,0:T(8,128)S(1)}, u32[]{:S(2)}, u32[]{:S(2)}) %collective-permute-start) | collective-permute-done | bytes 49184 | tf_op jit(solution)/shard_map/ppermute | solution.py:483
  7.3 0.4 shard_map.131
  7.7 2.0 %collective-permute-start.1 = (f32[24,640]{1,0:T(8,128)S(1)}, f32[24,640]{1,0:T(8,128)S(1)}, u32[]{:S(2)}, u32[]{:S(2)}) collective-permute-start(f32[24,640]{1,0:T(8,128)S(1)} %get-tuple-element.31), channel_id=1, source_target_pairs={{0,1},{1,0},{2,3},{3,2},{4,5},{5,4},{6,7},{7,6},{8,9},{9,8},{10,11... | collective-permute-start | bytes 184328 | tf_op jit(solution)/shard_map/ppermute | solution.py:490
  9.7 4.9 %collective-permute-start.2 = (f32[24,640]{1,0:T(8,128)S(1)}, f32[24,640]{1,0:T(8,128)S(1)}, u32[]{:S(2)}, u32[]{:S(2)}) collective-permute-start(f32[24,640]{1,0:T(8,128)S(1)} %get-tuple-element.32), channel_id=1, source_target_pairs={{0,7},{1,2},{2,1},{3,4},{4,3},{5,6},{6,5},{7,0},{8,15},{9,10},{10,... | collective-permute-start | bytes 184328 | tf_op jit(solution)/shard_map/ppermute | solution.py:490
  15.3 0.0 copy-start.2
  15.3 0.0 copy-start.6
  15.3 0.0 collective-permute-done.1.even
  15.3 1.5 %collective-permute-done.2.odd = f32[24,640]{1,0:T(8,128)S(1)} collective-permute-done((f32[24,640]{1,0:T(8,128)S(1)}, f32[24,640]{1,0:T(8,128)S(1)}, u32[]{:S(2)}, u32[]{:S(2)}) %collective-permute-start.2) | collective-permute-done | bytes 61472 | tf_op jit(solution)/shard_map/ppermute | solution.py:490
  16.8 2.9 %shard_map.132 = (f32[528,640]{1,0:T(8,128)S(1)}, f32[512,512]{1,0:T(8,128)S(1)}, f32[528,640]{1,0:T(8,128)S(1)}) custom-call(f32[512,512]{1,0:T(8,128)S(1)} %bitcast.7, f32[512,512]{1,0:T(8,128)S(1)} %bitcast.10, f32[24,512]{1,0:T(8,128)S(1)} %collective-permute-done.lat_in, f32[24,640]{1,0:T(8,128)S(1)} %collective-permute-done.1.even, ...), custom_call_target="tpu_custom_call" | custom-call | flops 2000000000 | bytes 7340032 | tf_op jit(solution)/shard_map/pallas_call | solution.py:471
  19.8 1.3 %shard_map.133 = (f32[8,128,128]{2,1,0:T(8,128)S(1)}, f32[8,128,128]{2,1,0:T(8,128)S(1)}, f32[4,256,128]{2,1,0:T(8,128)S(1)}, f32[4,256,128]{2,1,0:T(8,128)S(1)}) custom-call(f32[1]{0:T(128)S(6)} %copy.14.refs_0_.weight, f32[528,640]{1,0:T(8,128)S(1)} %get-tuple-element.33.refs_1_, f32[512,512]{1,0:T(8,128)S(1)} %bitcast.11, bf16[256,144]{1,0:T(8,128)(2,1)S(1)} %copy-done.6, ...), custom_call_target="tpu_custom_call" | custom-call | flops 1000000000 | bytes 5693444 | tf_op jit(solution)/shard_map/pallas_call | solution.py:471
  21.1 0.1 collective-permute-start.3
  21.2 1.3 %shard_map.135 = (f32[8,128,128]{2,1,0:T(8,128)S(1)}, f32[8,128,128]{2,1,0:T(8,128)S(1)}, f32[4,256,128]{2,1,0:T(8,128)S(1)}, f32[4,256,128]{2,1,0:T(8,128)S(1)}) custom-call(f32[1]{0:T(128)S(6)} %copy.14.refs_0_.weight, f32[528,640]{1,0:T(8,128)S(1)} %get-tuple-element.33.refs_1_, f32[512,512]{1,0:T(8,128)S(1)} %bitcast.12, bf16[256,144]{1,0:T(8,128)(2,1)S(1)} %copy-done.6, ...), custom_call_target="tpu_custom_call" | custom-call | flops 1000000000 | bytes 6217732 | tf_op jit(solution)/shard_map/pallas_call | solution.py:471
  22.5 0.6 collective-permute-start.8
  23.1 0.0 collective-permute-done.3.given
  23.1 0.1 shard_map.134
  23.1 1.3 %collective-permute-start.4 = (f32[256,128]{1,0:T(8,128)S(1)}, f32[256,128]{1,0:T(8,128)S(1)}, u32[]{:S(2)}, u32[]{:S(2)}) collective-permute-start(f32[256,128]{1,0:T(8,128)S(1)} %get-tuple-element.36), channel_id=1, source_target_pairs={{0,32},{32,0},{64,96},{96,64},{128,160},{160,128},{192,224},{224,1... | collective-permute-start | bytes 393224 | tf_op jit(solution)/shard_map/ppermute | solution.py:497
  24.4 1.8 %collective-permute-start.5 = (f32[256,128]{1,0:T(8,128)S(1)}, f32[256,128]{1,0:T(8,128)S(1)}, u32[]{:S(2)}, u32[]{:S(2)}) collective-permute-start(f32[256,128]{1,0:T(8,128)S(1)} %get-tuple-element.37), channel_id=1, source_target_pairs={{0,96},{32,64},{64,32},{96,0},{128,224},{160,192},{192,160},{224,1... | collective-permute-start | bytes 393224 | tf_op jit(solution)/shard_map/ppermute | solution.py:497
  26.3 3.5 %collective-permute-start.6 = (f32[256,128]{1,0:T(8,128)S(1)}, f32[256,128]{1,0:T(8,128)S(1)}, u32[]{:S(2)}, u32[]{:S(2)}) collective-permute-start(f32[256,128]{1,0:T(8,128)S(1)} %get-tuple-element.38), channel_id=1, source_target_pairs={{0,160},{32,128},{64,224},{96,192},{128,32},{160,0},{192,96},{224,... | collective-permute-start | bytes 393224 | tf_op jit(solution)/shard_map/ppermute | solution.py:497
  29.8 0.5 collective-permute-start.7
  30.3 0.0 collective-permute-done.8.given
  30.3 0.1 shard_map.136
  30.3 0.5 collective-permute-start.9
  30.8 0.0 collective-permute-done.4.refs_0_
  30.8 4.1 %collective-permute-start.10 = (f32[256,128]{1,0:T(8,128)S(1)}, f32[256,128]{1,0:T(8,128)S(1)}, u32[]{:S(2)}, u32[]{:S(2)}) collective-permute-start(f32[256,128]{1,0:T(8,128)S(1)} %get-tuple-element.44), channel_id=1, source_target_pairs={{0,128},{32,160},{64,192},{96,224},{128,0},{160,32},{192,64},{224,... | collective-permute-start | bytes 393224 | tf_op jit(solution)/shard_map/ppermute | solution.py:497
  34.9 0.0 collective-permute-done.5.refs_1_
  34.9 0.7 collective-permute-start.11
  35.6 2.5 %collective-permute-done.6.refs_2_ = f32[256,128]{1,0:T(8,128)S(1)} collective-permute-done((f32[256,128]{1,0:T(8,128)S(1)}, f32[256,128]{1,0:T(8,128)S(1)}, u32[]{:S(2)}, u32[]{:S(2)}) %collective-permute-start.6) | collective-permute-done | bytes 131104 | tf_op jit(solution)/shard_map/ppermute | solution.py:497
  38.2 2.0 %collective-permute-done.7.refs_3_ = f32[256,128]{1,0:T(8,128)S(1)} collective-permute-done((f32[256,128]{1,0:T(8,128)S(1)}, f32[256,128]{1,0:T(8,128)S(1)}, u32[]{:S(2)}, u32[]{:S(2)}) %collective-permute-start.7) | collective-permute-done | bytes 131104 | tf_op jit(solution)/shard_map/ppermute | solution.py:497
  40.2 2.7 %collective-permute-done.10.refs_6_ = f32[256,128]{1,0:T(8,128)S(1)} collective-permute-done((f32[256,128]{1,0:T(8,128)S(1)}, f32[256,128]{1,0:T(8,128)S(1)}, u32[]{:S(2)}, u32[]{:S(2)}) %collective-permute-start.10) | collective-permute-done | bytes 131104 | tf_op jit(solution)/shard_map/ppermute | solution.py:497
  42.8 2.7 %collective-permute-done.11.refs_7_ = f32[256,128]{1,0:T(8,128)S(1)} collective-permute-done((f32[256,128]{1,0:T(8,128)S(1)}, f32[256,128]{1,0:T(8,128)S(1)}, u32[]{:S(2)}, u32[]{:S(2)}) %collective-permute-start.11) | collective-permute-done | bytes 131104 | tf_op jit(solution)/shard_map/ppermute | solution.py:497
  45.5 0.1 shard_map.137.refs_0_
  45.6 2.0 %collective-permute-start.18 = (f32[256,128]{1,0:T(8,128)S(1)}, f32[256,128]{1,0:T(8,128)S(1)}, u32[]{:S(2)}, u32[]{:S(2)}) collective-permute-start(f32[256,128]{1,0:T(8,128)S(1)} %shard_map.137.refs_0_), channel_id=1, source_target_pairs={{0,224},{32,192},{64,160},{96,128},{128,96},{160,64},{192,32},{224... | collective-permute-start | bytes 393224 | tf_op jit(solution)/shard_map/ppermute | solution.py:497
  47.6 1.9 %collective-permute-start.17 = (f32[256,128]{1,0:T(8,128)S(1)}, f32[256,128]{1,0:T(8,128)S(1)}, u32[]{:S(2)}, u32[]{:S(2)}) collective-permute-start(f32[256,128]{1,0:T(8,128)S(1)} %shard_map.137.refs_0_), channel_id=1, source_target_pairs={{0,160},{32,128},{64,224},{96,192},{128,32},{160,0},{192,96},{224,... | collective-permute-start | bytes 393224 | tf_op jit(solution)/shard_map/ppermute | solution.py:497
  49.5 2.0 %collective-permute-start.16 = (f32[256,128]{1,0:T(8,128)S(1)}, f32[256,128]{1,0:T(8,128)S(1)}, u32[]{:S(2)}, u32[]{:S(2)}) collective-permute-start(f32[256,128]{1,0:T(8,128)S(1)} %shard_map.137.refs_0_), channel_id=1, source_target_pairs={{0,96},{32,64},{64,32},{96,0},{128,224},{160,192},{192,160},{224,1... | collective-permute-start | bytes 393224 | tf_op jit(solution)/shard_map/ppermute | solution.py:497
  51.5 0.8 %collective-permute-start.15 = (f32[256,128]{1,0:T(8,128)S(1)}, f32[256,128]{1,0:T(8,128)S(1)}, u32[]{:S(2)}, u32[]{:S(2)}) collective-permute-start(f32[256,128]{1,0:T(8,128)S(1)} %shard_map.137.refs_0_), channel_id=1, source_target_pairs={{0,32},{32,0},{64,96},{96,64},{128,160},{160,128},{192,224},{224,1... | collective-permute-start | bytes 393224 | tf_op jit(solution)/shard_map/ppermute | solution.py:497
  52.3 1.1 %collective-permute-start.14 = (f32[256,128]{1,0:T(8,128)S(1)}, f32[256,128]{1,0:T(8,128)S(1)}, u32[]{:S(2)}, u32[]{:S(2)}) collective-permute-start(f32[256,128]{1,0:T(8,128)S(1)} %shard_map.137.refs_0_), channel_id=1, source_target_pairs={{0,192},{32,224},{64,128},{96,160},{128,64},{160,96},{192,0},{224,... | collective-permute-start | bytes 393224 | tf_op jit(solution)/shard_map/ppermute | solution.py:497
  53.4 1.5 %collective-permute-done.18.refs_3_ = f32[256,128]{1,0:T(8,128)S(1)} collective-permute-done((f32[256,128]{1,0:T(8,128)S(1)}, f32[256,128]{1,0:T(8,128)S(1)}, u32[]{:S(2)}, u32[]{:S(2)}) %collective-permute-start.18) | collective-permute-done | bytes 131104 | tf_op jit(solution)/shard_map/ppermute | solution.py:497
  54.9 0.2 collective-permute-start.13
  55.0 1.6 %collective-permute-done.17.refs_2_ = f32[256,128]{1,0:T(8,128)S(1)} collective-permute-done((f32[256,128]{1,0:T(8,128)S(1)}, f32[256,128]{1,0:T(8,128)S(1)}, u32[]{:S(2)}, u32[]{:S(2)}) %collective-permute-start.17) | collective-permute-done | bytes 131104 | tf_op jit(solution)/shard_map/ppermute | solution.py:497
  56.7 1.4 %collective-permute-start.12 = (f32[256,128]{1,0:T(8,128)S(1)}, f32[256,128]{1,0:T(8,128)S(1)}, u32[]{:S(2)}, u32[]{:S(2)}) collective-permute-start(f32[256,128]{1,0:T(8,128)S(1)} %shard_map.137.refs_0_), channel_id=1, source_target_pairs={{0,64},{32,96},{64,0},{96,32},{128,192},{160,224},{192,128},{224,1... | collective-permute-start | bytes 393224 | tf_op jit(solution)/shard_map/ppermute | solution.py:497
  58.1 0.7 collective-permute-done.16.refs_1_
  58.8 1.4 %collective-permute-done.15.refs_0_ = f32[256,128]{1,0:T(8,128)S(1)} collective-permute-done((f32[256,128]{1,0:T(8,128)S(1)}, f32[256,128]{1,0:T(8,128)S(1)}, u32[]{:S(2)}, u32[]{:S(2)}) %collective-permute-start.15) | collective-permute-done | bytes 131104 | tf_op jit(solution)/shard_map/ppermute | solution.py:497
  60.3 0.6 collective-permute-done.14.refs_3_
  60.9 1.9 %collective-permute-done.13.refs_2_ = f32[256,128]{1,0:T(8,128)S(1)} collective-permute-done((f32[256,128]{1,0:T(8,128)S(1)}, f32[256,128]{1,0:T(8,128)S(1)}, u32[]{:S(2)}, u32[]{:S(2)}) %collective-permute-start.13) | collective-permute-done | bytes 131104 | tf_op jit(solution)/shard_map/ppermute | solution.py:497
  62.8 0.5 collective-permute-done.12.refs_1_
  63.3 0.1 collective-permute-start.19
  63.4 0.5 collective-permute-start.20
  63.9 1.4 %collective-permute-done.19.their_even = f32[4,256,128]{2,1,0:T(8,128)S(1)} collective-permute-done((f32[4,256,128]{2,1,0:T(8,128)S(1)}, f32[4,256,128]{2,1,0:T(8,128)S(1)}, u32[]{:S(2)}, u32[]{:S(2)}) %collective-permute-start.19) | collective-permute-done | bytes 524320 | tf_op jit(solution)/shard_map/ppermute | solution.py:501
  65.3 0.7 collective-permute-done.20.their_odd
  66.1 0.6 shard_map.140.pieces
  66.7 0.7 collective-permute-start.21
  67.4 2.1 %shard_map.143 = (f32[512,512]{1,0:T(8,128)S(1)}, f32[528,640]{1,0:T(8,128)S(1)}, f32[48,640]{1,0:T(8,128)S(1)}, f32[48,640]{1,0:T(8,128)S(1)}) custom-call(f32[16,128,128]{2,1,0:T(8,128)S(1)} %shard_map.140.pieces, f32[528,640]{1,0:T(8,128)S(1)} %get-tuple-element.52.slope, f32[512,512]{1,0:T(8,128)S(1)} %get-tuple-element.53.share, ...), custom_call_target="tpu_custom_call" | custom-call | flops 2000000000 | bytes 7413760 | tf_op jit(solution)/shard_map/pallas_call | solution.py:471
  69.5 2.7 %collective-permute-done.21.lat_in = f32[16,512]{1,0:T(8,128)S(1)} collective-permute-done((f32[16,512]{1,0:T(8,128)S(1)}, f32[16,512]{1,0:T(8,128)S(1)}, u32[]{:S(2)}, u32[]{:S(2)}) %collective-permute-start.21) | collective-permute-done | bytes 32800 | tf_op jit(solution)/shard_map/ppermute | solution.py:483
  72.2 0.2 shard_map.142
  72.4 0.1 collective-permute-start.22
  72.5 3.3 %collective-permute-start.23 = (f32[16,640]{1,0:T(8,128)S(1)}, f32[16,640]{1,0:T(8,128)S(1)}, u32[]{:S(2)}, u32[]{:S(2)}) collective-permute-start(f32[16,640]{1,0:T(8,128)S(1)} %get-tuple-element.51), channel_id=1, source_target_pairs={{0,7},{1,2},{2,1},{3,4},{4,3},{5,6},{6,5},{7,0},{8,15},{9,10},{10,... | collective-permute-start | bytes 122888 | tf_op jit(solution)/shard_map/ppermute | solution.py:490
  75.8 2.2 %shard_map.144.scaling_part = f32[512,512]{1,0:T(8,128)S(1)} custom-call(f32[528,640]{1,0:T(8,128)S(1)} %get-tuple-element.57.sloped, bf16[256,144]{1,0:T(8,128)(2,1)S(1)} %copy-done.6, bf16[512,256]{1,0:T(8,128)(2,1)S(1)} %copy-done.4, bf16[512,256]{1,0:T(8,128)(2,1)S(1)} %copy-done.3), custom_call_target="tpu_custom_call" | custom-call | flops 2000000000 | bytes 3596288 | tf_op jit(solution)/shard_map/pallas_call | solution.py:471
  78.1 0.0 collective-permute-done.22.even
  78.1 2.9 %shard_map.145 = (f32[512,512]{1,0:T(8,128)}, f32[512,512]{1,0:T(8,128)}) custom-call(f32[16,512]{1,0:T(8,128)S(1)} %collective-permute-done.21.lat_in, f32[16,640]{1,0:T(8,128)S(1)} %collective-permute-done.22.even, f32[16,640]{1,0:T(8,128)S(1)} %collective-permute-done.23.odd, f32[48,640]{1,0:T(8,128)S(1)} %get-tuple-element.54.slope_edge, ...), custom_call_target="tpu_custom_call" | custom-call | flops 1000000000 | bytes 4591616 | tf_op jit(solution)/shard_map/pallas_call | solution.py:471
  (18 shorter events, 0.1 us)
Async XLA Ops:
  0.6 6.7 %copy-start = (f32[1,512,512]{2,1,0:T(8,128)S(1)}, f32[1,512,512]{2,1,0:T(8,128)}, u32[]{:S(2)}) copy-start(f32[1,512,512]{2,1,0:T(8,128)} %param.13) | copy-start | bytes 3145732
  0.6 6.7 %copy-start.1 = (f32[1,512,512]{2,1,0:T(8,128)S(1)}, f32[1,512,512]{2,1,0:T(8,128)}, u32[]{:S(2)}) copy-start(f32[1,512,512]{2,1,0:T(8,128)} %param.12) | copy-start | bytes 3145732
  1.6 15.2 %copy-start.3 = (bf16[512,256]{1,0:T(8,128)(2,1)S(1)}, bf16[512,256]{1,0:T(8,128)(2,1)}, u32[]{:S(2)}) copy-start(bf16[512,256]{1,0:T(8,128)(2,1)} %constant.21.clone.cl.refs_5_) | copy-start | bytes 786436
  1.6 15.2 %copy-start.4 = (bf16[512,256]{1,0:T(8,128)(2,1)S(1)}, bf16[512,256]{1,0:T(8,128)(2,1)}, u32[]{:S(2)}) copy-start(bf16[512,256]{1,0:T(8,128)(2,1)} %constant.20.clone.ch.refs_4_) | copy-start | bytes 786436
  1.6 15.2 %copy-start.5 = (bf16[352,192]{1,0:T(8,128)(2,1)S(1)}, bf16[352,192]{1,0:T(8,128)(2,1)}, u32[]{:S(2)}) copy-start(bf16[352,192]{1,0:T(8,128)(2,1)} %constant.28.both3) | copy-start | bytes 405508
  1.6 5.7 %collective-permute-start = (f32[24,512]{1,0:T(8,128)S(1)}, f32[24,512]{1,0:T(8,128)S(1)}, u32[]{:S(2)}, u32[]{:S(2)}) collective-permute-start(f32[24,512]{1,0:T(8,128)S(1)} %lat_edges.1), channel_id=1, source_target_pairs={{0,8},{8,0},{1,9},{9,1},{2,10},{10,2},{3,11},{11,3},{4,12},{12,4},... | collective-permute-start | bytes 147464 | tf_op jit(solution)/shard_map/ppermute | solution.py:483
  7.7 7.6 %collective-permute-start.1 = (f32[24,640]{1,0:T(8,128)S(1)}, f32[24,640]{1,0:T(8,128)S(1)}, u32[]{:S(2)}, u32[]{:S(2)}) collective-permute-start(f32[24,640]{1,0:T(8,128)S(1)} %get-tuple-element.31), channel_id=1, source_target_pairs={{0,1},{1,0},{2,3},{3,2},{4,5},{5,4},{6,7},{7,6},{8,9},{9,8},{10,11... | collective-permute-start | bytes 184328 | tf_op jit(solution)/shard_map/ppermute | solution.py:490
  9.7 7.1 %collective-permute-start.2 = (f32[24,640]{1,0:T(8,128)S(1)}, f32[24,640]{1,0:T(8,128)S(1)}, u32[]{:S(2)}, u32[]{:S(2)}) collective-permute-start(f32[24,640]{1,0:T(8,128)S(1)} %get-tuple-element.32), channel_id=1, source_target_pairs={{0,7},{1,2},{2,1},{3,4},{4,3},{5,6},{6,5},{7,0},{8,15},{9,10},{10,... | collective-permute-start | bytes 184328 | tf_op jit(solution)/shard_map/ppermute | solution.py:490
  15.3 4.5 %copy-start.2 = (f32[1,512,512]{2,1,0:T(8,128)S(1)}, f32[1,512,512]{2,1,0:T(8,128)}, u32[]{:S(2)}) copy-start(f32[1,512,512]{2,1,0:T(8,128)} %param.15) | copy-start | bytes 3145732
  15.3 4.5 %copy-start.6 = (bf16[256,144]{1,0:T(8,128)(2,1)S(1)}, bf16[256,144]{1,0:T(8,128)(2,1)}, u32[]{:S(2)}) copy-start(bf16[256,144]{1,0:T(8,128)(2,1)} %constant.29.refs_3_.both4) | copy-start | bytes 221188
  21.1 2.0 %collective-permute-start.3 = (f32[4,256,128]{2,1,0:T(8,128)S(1)}, f32[4,256,128]{2,1,0:T(8,128)S(1)}, u32[]{:S(2)}, u32[]{:S(2)}) collective-permute-start(f32[4,256,128]{2,1,0:T(8,128)S(1)} %get-tuple-element.35), channel_id=1, source_target_pairs={{0,16},{16,0},{1,17},{17,1},{2,18},{18,2},{3,19},{19,3},{4,20},{20... | collective-permute-start | bytes 1572872 | tf_op jit(solution)/shard_map/ppermute | solution.py:501
  22.5 7.8 %collective-permute-start.8 = (f32[4,256,128]{2,1,0:T(8,128)S(1)}, f32[4,256,128]{2,1,0:T(8,128)S(1)}, u32[]{:S(2)}, u32[]{:S(2)}) collective-permute-start(f32[4,256,128]{2,1,0:T(8,128)S(1)} %get-tuple-element.41), channel_id=1, source_target_pairs={{0,16},{16,0},{1,17},{17,1},{2,18},{18,2},{3,19},{19,3},{4,20},{20... | collective-permute-start | bytes 1572872 | tf_op jit(solution)/shard_map/ppermute | solution.py:501
  23.1 7.7 %collective-permute-start.4 = (f32[256,128]{1,0:T(8,128)S(1)}, f32[256,128]{1,0:T(8,128)S(1)}, u32[]{:S(2)}, u32[]{:S(2)}) collective-permute-start(f32[256,128]{1,0:T(8,128)S(1)} %get-tuple-element.36), channel_id=1, source_target_pairs={{0,32},{32,0},{64,96},{96,64},{128,160},{160,128},{192,224},{224,1... | collective-permute-start | bytes 393224 | tf_op jit(solution)/shard_map/ppermute | solution.py:497
  24.4 10.5 %collective-permute-start.5 = (f32[256,128]{1,0:T(8,128)S(1)}, f32[256,128]{1,0:T(8,128)S(1)}, u32[]{:S(2)}, u32[]{:S(2)}) collective-permute-start(f32[256,128]{1,0:T(8,128)S(1)} %get-tuple-element.37), channel_id=1, source_target_pairs={{0,96},{32,64},{64,32},{96,0},{128,224},{160,192},{192,160},{224,1... | collective-permute-start | bytes 393224 | tf_op jit(solution)/shard_map/ppermute | solution.py:497
  26.3 11.9 %collective-permute-start.6 = (f32[256,128]{1,0:T(8,128)S(1)}, f32[256,128]{1,0:T(8,128)S(1)}, u32[]{:S(2)}, u32[]{:S(2)}) collective-permute-start(f32[256,128]{1,0:T(8,128)S(1)} %get-tuple-element.38), channel_id=1, source_target_pairs={{0,160},{32,128},{64,224},{96,192},{128,32},{160,0},{192,96},{224,... | collective-permute-start | bytes 393224 | tf_op jit(solution)/shard_map/ppermute | solution.py:497
  29.8 10.4 %collective-permute-start.7 = (f32[256,128]{1,0:T(8,128)S(1)}, f32[256,128]{1,0:T(8,128)S(1)}, u32[]{:S(2)}, u32[]{:S(2)}) collective-permute-start(f32[256,128]{1,0:T(8,128)S(1)} %get-tuple-element.39), channel_id=1, source_target_pairs={{0,224},{32,192},{64,160},{96,128},{128,96},{160,64},{192,32},{224... | collective-permute-start | bytes 393224 | tf_op jit(solution)/shard_map/ppermute | solution.py:497
  30.3 9.8 %collective-permute-start.9 = (f32[256,128]{1,0:T(8,128)S(1)}, f32[256,128]{1,0:T(8,128)S(1)}, u32[]{:S(2)}, u32[]{:S(2)}) collective-permute-start(f32[256,128]{1,0:T(8,128)S(1)} %get-tuple-element.43), channel_id=1, source_target_pairs={{0,64},{32,96},{64,0},{96,32},{128,192},{160,224},{192,128},{224,1... | collective-permute-start | bytes 393224 | tf_op jit(solution)/shard_map/ppermute | solution.py:497
  30.8 12.0 %collective-permute-start.10 = (f32[256,128]{1,0:T(8,128)S(1)}, f32[256,128]{1,0:T(8,128)S(1)}, u32[]{:S(2)}, u32[]{:S(2)}) collective-permute-start(f32[256,128]{1,0:T(8,128)S(1)} %get-tuple-element.44), channel_id=1, source_target_pairs={{0,128},{32,160},{64,192},{96,224},{128,0},{160,32},{192,64},{224,... | collective-permute-start | bytes 393224 | tf_op jit(solution)/shard_map/ppermute | solution.py:497
  34.9 10.6 %collective-permute-start.11 = (f32[256,128]{1,0:T(8,128)S(1)}, f32[256,128]{1,0:T(8,128)S(1)}, u32[]{:S(2)}, u32[]{:S(2)}) collective-permute-start(f32[256,128]{1,0:T(8,128)S(1)} %get-tuple-element.45), channel_id=1, source_target_pairs={{0,192},{32,224},{64,128},{96,160},{128,64},{160,96},{192,0},{224,... | collective-permute-start | bytes 393224 | tf_op jit(solution)/shard_map/ppermute | solution.py:497
  45.6 9.3 %collective-permute-start.18 = (f32[256,128]{1,0:T(8,128)S(1)}, f32[256,128]{1,0:T(8,128)S(1)}, u32[]{:S(2)}, u32[]{:S(2)}) collective-permute-start(f32[256,128]{1,0:T(8,128)S(1)} %shard_map.137.refs_0_), channel_id=1, source_target_pairs={{0,224},{32,192},{64,160},{96,128},{128,96},{160,64},{192,32},{224... | collective-permute-start | bytes 393224 | tf_op jit(solution)/shard_map/ppermute | solution.py:497
  47.6 9.1 %collective-permute-start.17 = (f32[256,128]{1,0:T(8,128)S(1)}, f32[256,128]{1,0:T(8,128)S(1)}, u32[]{:S(2)}, u32[]{:S(2)}) collective-permute-start(f32[256,128]{1,0:T(8,128)S(1)} %shard_map.137.refs_0_), channel_id=1, source_target_pairs={{0,160},{32,128},{64,224},{96,192},{128,32},{160,0},{192,96},{224,... | collective-permute-start | bytes 393224 | tf_op jit(solution)/shard_map/ppermute | solution.py:497
  49.5 9.4 %collective-permute-start.16 = (f32[256,128]{1,0:T(8,128)S(1)}, f32[256,128]{1,0:T(8,128)S(1)}, u32[]{:S(2)}, u32[]{:S(2)}) collective-permute-start(f32[256,128]{1,0:T(8,128)S(1)} %shard_map.137.refs_0_), channel_id=1, source_target_pairs={{0,96},{32,64},{64,32},{96,0},{128,224},{160,192},{192,160},{224,1... | collective-permute-start | bytes 393224 | tf_op jit(solution)/shard_map/ppermute | solution.py:497
  51.5 8.8 %collective-permute-start.15 = (f32[256,128]{1,0:T(8,128)S(1)}, f32[256,128]{1,0:T(8,128)S(1)}, u32[]{:S(2)}, u32[]{:S(2)}) collective-permute-start(f32[256,128]{1,0:T(8,128)S(1)} %shard_map.137.refs_0_), channel_id=1, source_target_pairs={{0,32},{32,0},{64,96},{96,64},{128,160},{160,128},{192,224},{224,1... | collective-permute-start | bytes 393224 | tf_op jit(solution)/shard_map/ppermute | solution.py:497
  52.3 8.6 %collective-permute-start.14 = (f32[256,128]{1,0:T(8,128)S(1)}, f32[256,128]{1,0:T(8,128)S(1)}, u32[]{:S(2)}, u32[]{:S(2)}) collective-permute-start(f32[256,128]{1,0:T(8,128)S(1)} %shard_map.137.refs_0_), channel_id=1, source_target_pairs={{0,192},{32,224},{64,128},{96,160},{128,64},{160,96},{192,0},{224,... | collective-permute-start | bytes 393224 | tf_op jit(solution)/shard_map/ppermute | solution.py:497
  54.9 7.9 %collective-permute-start.13 = (f32[256,128]{1,0:T(8,128)S(1)}, f32[256,128]{1,0:T(8,128)S(1)}, u32[]{:S(2)}, u32[]{:S(2)}) collective-permute-start(f32[256,128]{1,0:T(8,128)S(1)} %shard_map.137.refs_0_), channel_id=1, source_target_pairs={{0,128},{32,160},{64,192},{96,224},{128,0},{160,32},{192,64},{224,... | collective-permute-start | bytes 393224 | tf_op jit(solution)/shard_map/ppermute | solution.py:497
  56.7 6.6 %collective-permute-start.12 = (f32[256,128]{1,0:T(8,128)S(1)}, f32[256,128]{1,0:T(8,128)S(1)}, u32[]{:S(2)}, u32[]{:S(2)}) collective-permute-start(f32[256,128]{1,0:T(8,128)S(1)} %shard_map.137.refs_0_), channel_id=1, source_target_pairs={{0,64},{32,96},{64,0},{96,32},{128,192},{160,224},{192,128},{224,1... | collective-permute-start | bytes 393224 | tf_op jit(solution)/shard_map/ppermute | solution.py:497
  63.3 2.0 %collective-permute-start.19 = (f32[4,256,128]{2,1,0:T(8,128)S(1)}, f32[4,256,128]{2,1,0:T(8,128)S(1)}, u32[]{:S(2)}, u32[]{:S(2)}) collective-permute-start(f32[4,256,128]{2,1,0:T(8,128)S(1)} %shard_map.139.even), channel_id=1, source_target_pairs={{0,16},{16,0},{1,17},{17,1},{2,18},{18,2},{3,19},{19,3},{4,20},{20... | collective-permute-start | bytes 1572872 | tf_op jit(solution)/shard_map/ppermute | solution.py:501
  63.4 2.6 %collective-permute-start.20 = (f32[4,256,128]{2,1,0:T(8,128)S(1)}, f32[4,256,128]{2,1,0:T(8,128)S(1)}, u32[]{:S(2)}, u32[]{:S(2)}) collective-permute-start(f32[4,256,128]{2,1,0:T(8,128)S(1)} %shard_map.138.refs_4_.odd), channel_id=1, source_target_pairs={{0,16},{16,0},{1,17},{17,1},{2,18},{18,2},{3,19},{19,3},{4,20},{20... | collective-permute-start | bytes 1572872 | tf_op jit(solution)/shard_map/ppermute | solution.py:501
  66.7 5.5 %collective-permute-start.21 = (f32[16,512]{1,0:T(8,128)S(1)}, f32[16,512]{1,0:T(8,128)S(1)}, u32[]{:S(2)}, u32[]{:S(2)}) collective-permute-start(f32[16,512]{1,0:T(8,128)S(1)} %shard_map.141), channel_id=1, source_target_pairs={{0,8},{8,0},{1,9},{9,1},{2,10},{10,2},{3,11},{11,3},{4,12},{12,4},... | collective-permute-start | bytes 98312 | tf_op jit(solution)/shard_map/ppermute | solution.py:483
  72.4 5.7 %collective-permute-start.22 = (f32[16,640]{1,0:T(8,128)S(1)}, f32[16,640]{1,0:T(8,128)S(1)}, u32[]{:S(2)}, u32[]{:S(2)}) collective-permute-start(f32[16,640]{1,0:T(8,128)S(1)} %get-tuple-element.50), channel_id=1, source_target_pairs={{0,1},{1,0},{2,3},{3,2},{4,5},{5,4},{6,7},{7,6},{8,9},{9,8},{10,11... | collective-permute-start | bytes 122888 | tf_op jit(solution)/shard_map/ppermute | solution.py:490
  72.5 5.6 %collective-permute-start.23 = (f32[16,640]{1,0:T(8,128)S(1)}, f32[16,640]{1,0:T(8,128)S(1)}, u32[]{:S(2)}, u32[]{:S(2)}) collective-permute-start(f32[16,640]{1,0:T(8,128)S(1)} %get-tuple-element.51), channel_id=1, source_target_pairs={{0,7},{1,2},{2,1},{3,4},{4,3},{5,6},{6,5},{7,0},{8,15},{9,10},{10,... | collective-permute-start | bytes 122888 | tf_op jit(solution)/shard_map/ppermute | solution.py:490
  75.8 2.3 %copy-start.7 = (bf16[2,48,48]{2,1,0:T(8,128)(2,1)S(1)}, bf16[2,48,48]{2,1,0:T(8,128)(2,1)}, u32[]{:S(2)}) copy-start(bf16[2,48,48]{2,1,0:T(8,128)(2,1)} %constant.23.clone.dl) | copy-start | bytes 27652
  75.8 2.3 %copy-start.8 = (bf16[2,48,48]{2,1,0:T(8,128)(2,1)S(1)}, bf16[2,48,48]{2,1,0:T(8,128)(2,1)}, u32[]{:S(2)}) copy-start(bf16[2,48,48]{2,1,0:T(8,128)(2,1)} %constant.22.clone.dh) | copy-start | bytes 27652

commit v3 on v2

--- a/solution.py
+++ b/solution.py
@@ -188,7 +188,7 @@
 
 
 def forward_kernel(
-    scaling, precip, lat_in, even, odd, both3, ch, cl, slope, share, lifted, sx, px, side
+    scaling, precip, lat_in, even, odd, both3, ch, cl, first, lifted, sx, px, side
 ):
     lat = my_lat()
     wide, narrow = 2 * RADIUS, RADIUS
@@ -200,14 +200,10 @@
         at = BLOCK * i
         r = rows_pass(sx[at : at + BLOCK + 2 * RADIUS, :], both3)
         a = cols_pass(r, ch, cl, True)
-        rain = px[at : at + BLOCK, :]
-        inside = valid_part(at, BLOCK, lat)
-        u = jnp.where(inside, jnp.exp(PHI * jnp.log(rain / a)), 0.0)
-        lifted[at : at + BLOCK, :] = u
-        slope[at : at + BLOCK, :] = jnp.where(inside, -PHI * u / a, 0.0)
-        lo, hi = max(at, RADIUS), min(at + BLOCK, RADIUS + ROWS)
-        here = slice(lo - RADIUS, hi - RADIUS)
-        share[here, :] = PHI * u[lo - at : hi - at, 0:COLS] / rain[lo - at : hi - at, 0:COLS]
+        first[at : at + BLOCK, :] = a
+        lifted[at : at + BLOCK, :] = jnp.where(
+            valid_part(at, BLOCK, lat), jnp.exp(PHI * jnp.log(px[at : at + BLOCK, :] / a)), 0.0
+        )
 
 
 def half_start(flip):
@@ -215,7 +211,7 @@
     return pl.multiple_of(((1 - near) if flip else near) * (ROWS // 2), ROWS // 2)
 
 
-def log_kernel(flip, weight, lifted, upstream, both4, ch, cl, second, logs, keep, give):
+def log_kernel(flip, weight, lifted, upstream, both4, ch, cl, second, scaled, keep, give):
     core, far = lax.axis_index("hour_2"), lax.axis_index("hour_0")
     for i in range(2):
         at = half_start(flip) + EDGE * i
@@ -231,7 +227,7 @@
             for q, rows in enumerate(four):
                 to = slice(PIECE * j, PIECE * (j + 1))
                 second[4 * i + q, to, :] = b[rows, lanes]
-                logs[4 * i + q, to, :] = logb[rows, lanes]
+                scaled[4 * i + q, to, :] = parts[1][rows, lanes]
             for k, part in enumerate(parts):
                 to = slice(EDGE * k + PIECE * j, EDGE * k + PIECE * (j + 1))
                 for c in range(2):
@@ -254,9 +250,9 @@
             x = x + part[start : start + EDGE, :]
         return x
 
-    logq = total(0)
-    out[0:EDGE, :] = logq
-    out[EDGE : 2 * EDGE, :] = PHI * jnp.exp(PHI * logq) * total(EDGE)
+    level = jnp.exp(PHI * total(0))
+    out[0:EDGE, :] = level
+    out[EDGE : 2 * EDGE, :] = PHI * level * total(EDGE)
 
 
 def gather_kernel(*refs):
@@ -265,26 +261,21 @@
 
 
 def db_kernel(
-    weight, even, odd, their_even, their_odd, upstream, second_even, second_odd, logs_even,
-    logs_odd, pieces,
+    even, odd, their_even, their_odd, rise_even, rise_odd, fall_even, fall_odd, pieces
 ):
     core, far = lax.axis_index("hour_2"), lax.axis_index("hour_0")
-    for flip, mine, theirs, second, logs in (
-        (False, even, their_even, second_even, logs_even),
-        (True, odd, their_odd, second_odd, logs_odd),
+    for flip, mine, theirs, rise, fall in (
+        (False, even, their_even, rise_even, fall_even),
+        (True, odd, their_odd, rise_odd, fall_odd),
     ):
-        start = half_start(flip)
-        first = start // PIECE
+        first = half_start(flip) // PIECE
         for n in range(PIECES // 2):
             here, slot = core == n % 2, (n // 2) ^ far
-            for j in range(COLS // EDGE):
-                rows = slice(PIECE * j, PIECE * (j + 1))
-                low = slice(EDGE + PIECE * j, EDGE + PIECE * (j + 1))
-                logq = jnp.where(here, mine[slot, rows, :], theirs[slot, rows, :])
-                dlogq = jnp.where(here, mine[slot, low, :], theirs[slot, low, :])
-                value = upstream[pl.ds(start + PIECE * n, PIECE), EDGE * j : EDGE * (j + 1)]
-                term = PHI * value * jnp.exp(PHI * (logq - logs[n, rows, :]))
-                pieces[first + n, rows, :] = (weight[0] * dlogq - term) / second[n, rows, :]
+            level = jnp.where(here, mine[slot, 0:EDGE, :], theirs[slot, 0:EDGE, :])
+            dlogq = jnp.where(
+                here, mine[slot, EDGE : 2 * EDGE, :], theirs[slot, EDGE : 2 * EDGE, :]
+            )
+            pieces[first + n] = rise[n] * dlogq - fall[n] * level
 
 
 def tile_column(pieces, j):
@@ -336,10 +327,30 @@
     share_edge[32:40, 0:COLS] = tile[EDGE - RADIUS : EDGE]
 
 
+def prepare_kernel(
+    weight, first, lifted, precip, second_even, second_odd, scaled_even, scaled_odd,
+    slope, share, slope_edge, share_edge, rise_even, rise_odd, fall_even, fall_odd,
+):
+    lat = my_lat()
+    for i in range(3):
+        rows = slice(BLOCK * i, BLOCK * (i + 1))
+        slope[rows, :] = jnp.where(
+            valid_part(BLOCK * i, BLOCK, lat), -PHI * lifted[rows, :] / first[rows, :], 0.0
+        )
+    share[...] = PHI * lifted[RADIUS : RADIUS + ROWS, 0:COLS] / precip[...]
+    coefficient_strips(slope, share, slope_edge, share_edge)
+    for second, scaled, rise, fall in (
+        (second_even, scaled_even, rise_even, fall_even),
+        (second_odd, scaled_odd, rise_odd, fall_odd),
+    ):
+        inverse = 1.0 / second[...]
+        rise[...] = weight[0] * inverse
+        fall[...] = PHI * scaled[...] * inverse
+
+
 def back_first_kernel(
-    pieces, slope, share, both3, ch, cl, grad_precip, sloped, slope_edge, share_edge, dx
+    pieces, slope, share, both3, ch, cl, grad_precip, sloped, dx
 ):
-    coefficient_strips(slope, share, slope_edge, share_edge)
     wide = 2 * RADIUS
     dx[0:wide, :] = jnp.zeros((wide, COLS), F32)
     dx[wide + ROWS : TALLER, :] = jnp.zeros((wide, COLS), F32)
@@ -513,10 +524,10 @@
     )
     half = (CHIPS // 2, 2 * EDGE, EDGE)
     whole, part = (PIECES, EDGE, EDGE), (PIECES // 2, EDGE, EDGE)
-    slope, share, lifted = call(
+    smooth, lifted = call(
         forward_kernel,
         (incoming, rainfall, lat_in, even, odd, band3, *around),
-        ((TALL, WIDE), (ROWS, COLS), (TALL, WIDE)),
+        ((TALL, WIDE), (TALL, WIDE)),
         scratch=((TALLER, WIDE), (TALL, WIDE), (EDGE, WIDE)),
         flops=2 * 10**9,
         room=14 << 20,
@@ -532,14 +543,24 @@
             room=14 << 20,
         )
 
-    second_odd, logs_odd, keep_odd, give_odd = logged(True)
+    second_odd, scaled_odd, keep_odd, give_odd = logged(True)
     given_odd = cores_swapped(give_odd)
-    second_even, logs_even, keep_even, give_even = logged(False, keep_odd)
+    second_even, scaled_even, keep_even, give_even = logged(False, keep_odd)
     given_even = cores_swapped(give_even)
     arrived = []
     for keep, given, first in ((keep_odd, given_odd, 1), (keep_even, given_even, 0)):
         sums = call(pair_kernel, (keep, given), (half[1:],) * (CHIPS // 2))
         arrived += [chip_swapped(part, 2 * k + first) for k, part in enumerate(sums)]
+    slope, share, slope_edge, share_edge, *factors = call(
+        prepare_kernel,
+        (
+            hour_weight, smooth, lifted, rainfall, second_even, second_odd, scaled_even,
+            scaled_odd,
+        ),
+        ((TALL, WIDE), (ROWS, COLS), (48, WIDE), (48, WIDE), part, part, part, part),
+        scalars=1,
+        room=14 << 20,
+    )
     (owned,) = call(owner_kernel, tuple(arrived), (half[1:],))
 
     def collected(first, *after):
@@ -550,24 +571,16 @@
     their_odd = cores_swapped(odd_part)
     even_part = collected(0, odd_part)
     their_even = cores_swapped(even_part)
-    (pieces,) = call(
-        db_kernel,
-        (
-            hour_weight, even_part, odd_part, their_even, their_odd, upstream, second_even,
-            second_odd, logs_even, logs_odd,
-        ),
-        (whole,),
-        scalars=1,
-    )
+    (pieces,) = call(db_kernel, (even_part, odd_part, their_even, their_odd, *factors), (whole,))
     (to_lat,) = call(back_lat_kernel, (pieces,), ((2 * RADIUS, COLS),))
     lat_in = lat_swapped(to_lat)
     even, odd = lon_swapped(
         *call(back_lon_kernel, (pieces, lat_in), ((2 * RADIUS, WIDE), (2 * RADIUS, WIDE)))
     )
-    precip_part, sloped, slope_edge, share_edge = call(
+    precip_part, sloped = call(
         back_first_kernel,
         (pieces, slope, share, band3, *around),
-        ((ROWS, COLS), (TALL, WIDE), (48, WIDE), (48, WIDE)),
+        ((ROWS, COLS), (TALL, WIDE)),
         scratch=((TALLER, COLS),),
         flops=2 * 10**9,
         room=14 << 20,

time: 81.6 us -> 81.1 us (level)
    pallas_call x15 -> x16, Pallas kernels: 14.2 us -> 14.6 us  [call(): pl.pallas_call(kernel, out_shape=[pltpu.HBM(o, F32) if out_hbm else jax.S...]
  transfers between devices with their start and end apart: 24 -> 24, of which waited for: 16 -> 16; matrix products, arithmetic and copies ran while one was open for 0% -> 0% of each run, Pallas kernels for 7% -> 8%
where the time goes in v3:
time: 81.1 us; the launch traced here: 80.7 us
  starting transfers between devices  36.2 us (45%)
  waiting for transfers between devices  27.2 us (34%)
  Pallas kernels  15.5 us (19%)
  between operations  1.7 us (2%)
    ppermute x14, starting transfers between devices, chip_swapped(): return lax.ppermute(part, ('hour_0', 'hour_1'), pairs)  21.6 us
    ppermute x14, waiting for transfers between devices, chip_swapped(): return lax.ppermute(part, ('hour_0', 'hour_1'), pairs)  18.2 us
    pallas_call x16, Pallas kernels, call(): pl.pallas_call(kernel, out_shape=[pltpu.HBM(o, F32) if out_hbm else jax.S...  14.6 us
    ppermute x2, starting transfers between devices, lon_swapped(): lax.ppermute(to_odd, 'lon', odd)  8.26 us
    ppermute x2, waiting for transfers between devices, lat_swapped(): return lax.ppermute(strip, 'lat', [(0, 1), (1, 0)])  6.13 us
    ppermute x2, starting transfers between devices, lat_swapped(): return lax.ppermute(strip, 'lat', [(0, 1), (1, 0)])  2.98 us
    ppermute x2, starting transfers between devices, lon_swapped(): lax.ppermute(to_even, 'lon', even)  2.1 us
  transfers between devices with their start and end apart: 24, of which 16 were waited for; matrix products, arithmetic and copies ran while one was open for 0% of the time, Pallas kernels for 8%

profile of v3, /device:TPU:4, one launch (start us, length us, event | category | flops | bytes accessed | tf_op | source)
XLA Modules:
  0.0 80.7 jit_solution(10682671287729395162)
XLA Ops:
  0.6 0.9 %lat_edges.1 = f32[24,512]{1,0:T(8,128)S(1)} custom-call(f32[512,512]{1,0:T(8,128)} %bitcast.9, f32[512,512]{1,0:T(8,128)} %bitcast.5), custom_call_target="tpu_custom_call" | custom-call | tf_op jit(solution)/shard_map/lat_edges/pallas_call | solution.py:169
  1.6 0.0 copy-start.3
  1.6 0.0 copy-start.4
  1.6 0.0 copy-start.5
  1.6 2.3 %collective-permute-start = (f32[24,512]{1,0:T(8,128)S(1)}, f32[24,512]{1,0:T(8,128)S(1)}, u32[]{:S(2)}, u32[]{:S(2)}) collective-permute-start(f32[24,512]{1,0:T(8,128)S(1)} %lat_edges.1), channel_id=1, source_target_pairs={{0,8},{8,0},{1,9},{9,1},{2,10},{10,2},{3,11},{11,3},{4,12},{12,4},... | collective-permute-start | bytes 147464 | tf_op jit(solution)/shard_map/ppermute | solution.py:494
  3.9 3.4 %collective-permute-done.lat_in = f32[24,512]{1,0:T(8,128)S(1)} collective-permute-done((f32[24,512]{1,0:T(8,128)S(1)}, f32[24,512]{1,0:T(8,128)S(1)}, u32[]{:S(2)}, u32[]{:S(2)}) %collective-permute-start) | collective-permute-done | bytes 49184 | tf_op jit(solution)/shard_map/ppermute | solution.py:494
  7.3 0.4 shard_map.131
  7.7 2.0 %collective-permute-start.1 = (f32[24,640]{1,0:T(8,128)S(1)}, f32[24,640]{1,0:T(8,128)S(1)}, u32[]{:S(2)}, u32[]{:S(2)}) collective-permute-start(f32[24,640]{1,0:T(8,128)S(1)} %get-tuple-element.36), channel_id=1, source_target_pairs={{0,1},{1,0},{2,3},{3,2},{4,5},{5,4},{6,7},{7,6},{8,9},{9,8},{10,11... | collective-permute-start | bytes 184328 | tf_op jit(solution)/shard_map/ppermute | solution.py:501
  9.7 4.9 %collective-permute-start.2 = (f32[24,640]{1,0:T(8,128)S(1)}, f32[24,640]{1,0:T(8,128)S(1)}, u32[]{:S(2)}, u32[]{:S(2)}) collective-permute-start(f32[24,640]{1,0:T(8,128)S(1)} %get-tuple-element.37), channel_id=1, source_target_pairs={{0,7},{1,2},{2,1},{3,4},{4,3},{5,6},{6,5},{7,0},{8,15},{9,10},{10,... | collective-permute-start | bytes 184328 | tf_op jit(solution)/shard_map/ppermute | solution.py:501
  15.3 0.0 copy-start.2
  15.3 0.0 copy-start.6
  15.3 0.0 collective-permute-done.1.even
  15.3 1.5 %collective-permute-done.2.odd = f32[24,640]{1,0:T(8,128)S(1)} collective-permute-done((f32[24,640]{1,0:T(8,128)S(1)}, f32[24,640]{1,0:T(8,128)S(1)}, u32[]{:S(2)}, u32[]{:S(2)}) %collective-permute-start.2) | collective-permute-done | bytes 61472 | tf_op jit(solution)/shard_map/ppermute | solution.py:501
  16.8 2.8 %shard_map.132 = (f32[528,640]{1,0:T(8,128)S(1)}, f32[528,640]{1,0:T(8,128)S(1)}) custom-call(f32[512,512]{1,0:T(8,128)S(1)} %bitcast.11, f32[512,512]{1,0:T(8,128)S(1)} %bitcast.7, f32[24,512]{1,0:T(8,128)S(1)} %collective-permute-done.lat_in, f32[24,640]{1,0:T(8,128)S(1)} %collective-permute-done.1.even, f32[24,640]{1,0:T(8,128)S(1)} %collective-permute-done.2.odd, ...), custom_call_target="tpu_custom_call" | custom-call | flops 2000000000 | bytes 6291456 | tf_op jit(solution)/shard_map/pallas_call | solution.py:482
  19.7 1.3 %shard_map.133 = (f32[8,128,128]{2,1,0:T(8,128)S(1)}, f32[8,128,128]{2,1,0:T(8,128)S(1)}, f32[4,256,128]{2,1,0:T(8,128)S(1)}, f32[4,256,128]{2,1,0:T(8,128)S(1)}) custom-call(f32[1]{0:T(128)S(6)} %copy.14.refs_0_.weight, f32[528,640]{1,0:T(8,128)S(1)} %get-tuple-element.38.refs_1_.lifted, f32[512,512]{1,0:T(8,128)S(1)} %bitcast.12, ...), custom_call_target="tpu_custom_call" | custom-call | flops 1000000000 | bytes 5693444 | tf_op jit(solution)/shard_map/pallas_call | solution.py:482
  21.0 0.1 collective-permute-start.3
  21.1 1.3 %shard_map.135 = (f32[8,128,128]{2,1,0:T(8,128)S(1)}, f32[8,128,128]{2,1,0:T(8,128)S(1)}, f32[4,256,128]{2,1,0:T(8,128)S(1)}, f32[4,256,128]{2,1,0:T(8,128)S(1)}) custom-call(f32[1]{0:T(128)S(6)} %copy.14.refs_0_.weight, f32[528,640]{1,0:T(8,128)S(1)} %get-tuple-element.38.refs_1_.lifted, f32[512,512]{1,0:T(8,128)S(1)} %bitcast.13, ...), custom_call_target="tpu_custom_call" | custom-call | flops 1000000000 | bytes 6217732 | tf_op jit(solution)/shard_map/pallas_call | solution.py:482
  22.4 0.6 collective-permute-start.8
  23.0 0.0 collective-permute-done.3.given
  23.0 0.1 shard_map.134
  23.1 1.3 %collective-permute-start.4 = (f32[256,128]{1,0:T(8,128)S(1)}, f32[256,128]{1,0:T(8,128)S(1)}, u32[]{:S(2)}, u32[]{:S(2)}) collective-permute-start(f32[256,128]{1,0:T(8,128)S(1)} %get-tuple-element.41), channel_id=1, source_target_pairs={{0,32},{32,0},{64,96},{96,64},{128,160},{160,128},{192,224},{224,1... | collective-permute-start | bytes 393224 | tf_op jit(solution)/shard_map/ppermute | solution.py:508
  24.3 1.8 %collective-permute-start.5 = (f32[256,128]{1,0:T(8,128)S(1)}, f32[256,128]{1,0:T(8,128)S(1)}, u32[]{:S(2)}, u32[]{:S(2)}) collective-permute-start(f32[256,128]{1,0:T(8,128)S(1)} %get-tuple-element.42), channel_id=1, source_target_pairs={{0,96},{32,64},{64,32},{96,0},{128,224},{160,192},{192,160},{224,1... | collective-permute-start | bytes 393224 | tf_op jit(solution)/shard_map/ppermute | solution.py:508
  26.2 3.5 %collective-permute-start.6 = (f32[256,128]{1,0:T(8,128)S(1)}, f32[256,128]{1,0:T(8,128)S(1)}, u32[]{:S(2)}, u32[]{:S(2)}) collective-permute-start(f32[256,128]{1,0:T(8,128)S(1)} %get-tuple-element.43), channel_id=1, source_target_pairs={{0,160},{32,128},{64,224},{96,192},{128,32},{160,0},{192,96},{224,... | collective-permute-start | bytes 393224 | tf_op jit(solution)/shard_map/ppermute | solution.py:508
  29.7 0.5 collective-permute-start.7
  30.2 0.0 collective-permute-done.8.given
  30.2 0.1 shard_map.136
  30.3 0.4 collective-permute-start.9
  30.7 0.0 collective-permute-done.4.refs_0_
  30.7 4.1 %collective-permute-start.10 = (f32[256,128]{1,0:T(8,128)S(1)}, f32[256,128]{1,0:T(8,128)S(1)}, u32[]{:S(2)}, u32[]{:S(2)}) collective-permute-start(f32[256,128]{1,0:T(8,128)S(1)} %get-tuple-element.49), channel_id=1, source_target_pairs={{0,128},{32,160},{64,192},{96,224},{128,0},{160,32},{192,64},{224,... | collective-permute-start | bytes 393224 | tf_op jit(solution)/shard_map/ppermute | solution.py:508
  34.8 0.7 collective-permute-start.11
  35.6 2.5 %collective-permute-done.6.refs_2_ = f32[256,128]{1,0:T(8,128)S(1)} collective-permute-done((f32[256,128]{1,0:T(8,128)S(1)}, f32[256,128]{1,0:T(8,128)S(1)}, u32[]{:S(2)}, u32[]{:S(2)}) %collective-permute-start.6) | collective-permute-done | bytes 131104 | tf_op jit(solution)/shard_map/ppermute | solution.py:508
  38.1 2.0 %collective-permute-done.7.refs_3_ = f32[256,128]{1,0:T(8,128)S(1)} collective-permute-done((f32[256,128]{1,0:T(8,128)S(1)}, f32[256,128]{1,0:T(8,128)S(1)}, u32[]{:S(2)}, u32[]{:S(2)}) %collective-permute-start.7) | collective-permute-done | bytes 131104 | tf_op jit(solution)/shard_map/ppermute | solution.py:508
  40.1 2.7 %collective-permute-done.10.refs_6_ = f32[256,128]{1,0:T(8,128)S(1)} collective-permute-done((f32[256,128]{1,0:T(8,128)S(1)}, f32[256,128]{1,0:T(8,128)S(1)}, u32[]{:S(2)}, u32[]{:S(2)}) %collective-permute-start.10) | collective-permute-done | bytes 131104 | tf_op jit(solution)/shard_map/ppermute | solution.py:508
  42.7 2.7 %collective-permute-done.11.refs_7_ = f32[256,128]{1,0:T(8,128)S(1)} collective-permute-done((f32[256,128]{1,0:T(8,128)S(1)}, f32[256,128]{1,0:T(8,128)S(1)}, u32[]{:S(2)}, u32[]{:S(2)}) %collective-permute-start.11) | collective-permute-done | bytes 131104 | tf_op jit(solution)/shard_map/ppermute | solution.py:508
  45.5 0.1 shard_map.137.refs_0_
  45.5 1.8 %collective-permute-start.18 = (f32[256,128]{1,0:T(8,128)S(1)}, f32[256,128]{1,0:T(8,128)S(1)}, u32[]{:S(2)}, u32[]{:S(2)}) collective-permute-start(f32[256,128]{1,0:T(8,128)S(1)} %shard_map.137.refs_0_), channel_id=1, source_target_pairs={{0,224},{32,192},{64,160},{96,128},{128,96},{160,64},{192,32},{224... | collective-permute-start | bytes 393224 | tf_op jit(solution)/shard_map/ppermute | solution.py:508
  47.3 1.9 %collective-permute-start.17 = (f32[256,128]{1,0:T(8,128)S(1)}, f32[256,128]{1,0:T(8,128)S(1)}, u32[]{:S(2)}, u32[]{:S(2)}) collective-permute-start(f32[256,128]{1,0:T(8,128)S(1)} %shard_map.137.refs_0_), channel_id=1, source_target_pairs={{0,160},{32,128},{64,224},{96,192},{128,32},{160,0},{192,96},{224,... | collective-permute-start | bytes 393224 | tf_op jit(solution)/shard_map/ppermute | solution.py:508
  49.2 2.0 %collective-permute-start.16 = (f32[256,128]{1,0:T(8,128)S(1)}, f32[256,128]{1,0:T(8,128)S(1)}, u32[]{:S(2)}, u32[]{:S(2)}) collective-permute-start(f32[256,128]{1,0:T(8,128)S(1)} %shard_map.137.refs_0_), channel_id=1, source_target_pairs={{0,96},{32,64},{64,32},{96,0},{128,224},{160,192},{192,160},{224,1... | collective-permute-start | bytes 393224 | tf_op jit(solution)/shard_map/ppermute | solution.py:508
  51.2 0.8 %collective-permute-start.15 = (f32[256,128]{1,0:T(8,128)S(1)}, f32[256,128]{1,0:T(8,128)S(1)}, u32[]{:S(2)}, u32[]{:S(2)}) collective-permute-start(f32[256,128]{1,0:T(8,128)S(1)} %shard_map.137.refs_0_), channel_id=1, source_target_pairs={{0,32},{32,0},{64,96},{96,64},{128,160},{160,128},{192,224},{224,1... | collective-permute-start | bytes 393224 | tf_op jit(solution)/shard_map/ppermute | solution.py:508
  52.1 1.1 %collective-permute-start.14 = (f32[256,128]{1,0:T(8,128)S(1)}, f32[256,128]{1,0:T(8,128)S(1)}, u32[]{:S(2)}, u32[]{:S(2)}) collective-permute-start(f32[256,128]{1,0:T(8,128)S(1)} %shard_map.137.refs_0_), channel_id=1, source_target_pairs={{0,192},{32,224},{64,128},{96,160},{128,64},{160,96},{192,0},{224,... | collective-permute-start | bytes 393224 | tf_op jit(solution)/shard_map/ppermute | solution.py:508
  53.1 1.5 %collective-permute-done.18.refs_3_ = f32[256,128]{1,0:T(8,128)S(1)} collective-permute-done((f32[256,128]{1,0:T(8,128)S(1)}, f32[256,128]{1,0:T(8,128)S(1)}, u32[]{:S(2)}, u32[]{:S(2)}) %collective-permute-start.18) | collective-permute-done | bytes 131104 | tf_op jit(solution)/shard_map/ppermute | solution.py:508
  54.6 0.2 collective-permute-start.13
  54.8 1.6 %collective-permute-done.17.refs_2_ = f32[256,128]{1,0:T(8,128)S(1)} collective-permute-done((f32[256,128]{1,0:T(8,128)S(1)}, f32[256,128]{1,0:T(8,128)S(1)}, u32[]{:S(2)}, u32[]{:S(2)}) %collective-permute-start.17) | collective-permute-done | bytes 131104 | tf_op jit(solution)/shard_map/ppermute | solution.py:508
  56.4 1.4 %collective-permute-start.12 = (f32[256,128]{1,0:T(8,128)S(1)}, f32[256,128]{1,0:T(8,128)S(1)}, u32[]{:S(2)}, u32[]{:S(2)}) collective-permute-start(f32[256,128]{1,0:T(8,128)S(1)} %shard_map.137.refs_0_), channel_id=1, source_target_pairs={{0,64},{32,96},{64,0},{96,32},{128,192},{160,224},{192,128},{224,1... | collective-permute-start | bytes 393224 | tf_op jit(solution)/shard_map/ppermute | solution.py:508
  57.8 0.7 collective-permute-done.16.refs_1_
  58.6 1.4 %collective-permute-done.15.refs_0_ = f32[256,128]{1,0:T(8,128)S(1)} collective-permute-done((f32[256,128]{1,0:T(8,128)S(1)}, f32[256,128]{1,0:T(8,128)S(1)}, u32[]{:S(2)}, u32[]{:S(2)}) %collective-permute-start.15) | collective-permute-done | bytes 131104 | tf_op jit(solution)/shard_map/ppermute | solution.py:508
  60.1 0.5 collective-permute-done.14.refs_3_
  60.6 1.9 %collective-permute-done.13.refs_2_ = f32[256,128]{1,0:T(8,128)S(1)} collective-permute-done((f32[256,128]{1,0:T(8,128)S(1)}, f32[256,128]{1,0:T(8,128)S(1)}, u32[]{:S(2)}, u32[]{:S(2)}) %collective-permute-start.13) | collective-permute-done | bytes 131104 | tf_op jit(solution)/shard_map/ppermute | solution.py:508
  62.5 0.5 collective-permute-done.12.refs_1_
  63.1 0.1 collective-permute-start.19
  63.2 0.5 collective-permute-start.20
  63.7 0.7 shard_map.140
  64.4 0.7 collective-permute-done.19.their_even
  65.1 0.7 collective-permute-done.20.their_odd
  65.8 0.3 shard_map.141.pieces
  66.2 0.7 collective-permute-start.21
  66.8 2.1 %shard_map.144 = (f32[512,512]{1,0:T(8,128)S(1)}, f32[528,640]{1,0:T(8,128)S(1)}) custom-call(f32[16,128,128]{2,1,0:T(8,128)S(1)} %shard_map.141.pieces, f32[528,640]{1,0:T(8,128)S(1)} %get-tuple-element.64.slope, f32[512,512]{1,0:T(8,128)S(1)} %get-tuple-element.65.share, bf16[352,192]{1,0:T(8,128)(2,1)S(1)} %copy-done.5, bf16[512,256]{1,0:T(8,128)(2,1)S(1)} %copy-done.4, ...), custom_call_target="tpu_custom_call" | custom-call | flops 2000000000 | bytes 7168000 | tf_op jit(solution)/shard_map/pallas_call | solution.py:482
  68.9 2.8 %collective-permute-done.21.lat_in = f32[16,512]{1,0:T(8,128)S(1)} collective-permute-done((f32[16,512]{1,0:T(8,128)S(1)}, f32[16,512]{1,0:T(8,128)S(1)}, u32[]{:S(2)}, u32[]{:S(2)}) %collective-permute-start.21) | collective-permute-done | bytes 32800 | tf_op jit(solution)/shard_map/ppermute | solution.py:494
  71.7 0.2 shard_map.143
  71.9 0.1 collective-permute-start.22
  72.0 3.3 %collective-permute-start.23 = (f32[16,640]{1,0:T(8,128)S(1)}, f32[16,640]{1,0:T(8,128)S(1)}, u32[]{:S(2)}, u32[]{:S(2)}) collective-permute-start(f32[16,640]{1,0:T(8,128)S(1)} %get-tuple-element.61), channel_id=1, source_target_pairs={{0,7},{1,2},{2,1},{3,4},{4,3},{5,6},{6,5},{7,0},{8,15},{9,10},{10,... | collective-permute-start | bytes 122888 | tf_op jit(solution)/shard_map/ppermute | solution.py:501
  75.3 2.2 %shard_map.145.scaling_part = f32[512,512]{1,0:T(8,128)S(1)} custom-call(f32[528,640]{1,0:T(8,128)S(1)} %get-tuple-element.67.sloped, bf16[256,144]{1,0:T(8,128)(2,1)S(1)} %copy-done.6, bf16[512,256]{1,0:T(8,128)(2,1)S(1)} %copy-done.4, bf16[512,256]{1,0:T(8,128)(2,1)S(1)} %copy-done.3), custom_call_target="tpu_custom_call" | custom-call | flops 2000000000 | bytes 3596288 | tf_op jit(solution)/shard_map/pallas_call | solution.py:482
  77.6 0.0 collective-permute-done.22.even
  77.6 2.9 %shard_map.146 = (f32[512,512]{1,0:T(8,128)}, f32[512,512]{1,0:T(8,128)}) custom-call(f32[16,512]{1,0:T(8,128)S(1)} %collective-permute-done.21.lat_in, f32[16,640]{1,0:T(8,128)S(1)} %collective-permute-done.22.even, f32[16,640]{1,0:T(8,128)S(1)} %collective-permute-done.23.odd, f32[48,640]{1,0:T(8,128)S(1)} %get-tuple-element.62.slope_edge, ...), custom_call_target="tpu_custom_call" | custom-call | flops 1000000000 | bytes 4591616 | tf_op jit(solution)/shard_map/pallas_call | solution.py:482
  (19 shorter events, 0.1 us)
Async XLA Ops:
  0.6 6.7 %copy-start.1 = (f32[1,512,512]{2,1,0:T(8,128)S(1)}, f32[1,512,512]{2,1,0:T(8,128)}, u32[]{:S(2)}) copy-start(f32[1,512,512]{2,1,0:T(8,128)} %param.13) | copy-start | bytes 3145732
  0.6 6.7 %copy-start = (f32[1,512,512]{2,1,0:T(8,128)S(1)}, f32[1,512,512]{2,1,0:T(8,128)}, u32[]{:S(2)}) copy-start(f32[1,512,512]{2,1,0:T(8,128)} %param.12) | copy-start | bytes 3145732
  1.6 15.2 %copy-start.3 = (bf16[512,256]{1,0:T(8,128)(2,1)S(1)}, bf16[512,256]{1,0:T(8,128)(2,1)}, u32[]{:S(2)}) copy-start(bf16[512,256]{1,0:T(8,128)(2,1)} %constant.21.clone.cl.refs_5_) | copy-start | bytes 786436
  1.6 15.2 %copy-start.4 = (bf16[512,256]{1,0:T(8,128)(2,1)S(1)}, bf16[512,256]{1,0:T(8,128)(2,1)}, u32[]{:S(2)}) copy-start(bf16[512,256]{1,0:T(8,128)(2,1)} %constant.20.clone.ch.refs_4_) | copy-start | bytes 786436
  1.6 15.2 %copy-start.5 = (bf16[352,192]{1,0:T(8,128)(2,1)S(1)}, bf16[352,192]{1,0:T(8,128)(2,1)}, u32[]{:S(2)}) copy-start(bf16[352,192]{1,0:T(8,128)(2,1)} %constant.28.both3) | copy-start | bytes 405508
  1.6 5.7 %collective-permute-start = (f32[24,512]{1,0:T(8,128)S(1)}, f32[24,512]{1,0:T(8,128)S(1)}, u32[]{:S(2)}, u32[]{:S(2)}) collective-permute-start(f32[24,512]{1,0:T(8,128)S(1)} %lat_edges.1), channel_id=1, source_target_pairs={{0,8},{8,0},{1,9},{9,1},{2,10},{10,2},{3,11},{11,3},{4,12},{12,4},... | collective-permute-start | bytes 147464 | tf_op jit(solution)/shard_map/ppermute | solution.py:494
  7.7 7.6 %collective-permute-start.1 = (f32[24,640]{1,0:T(8,128)S(1)}, f32[24,640]{1,0:T(8,128)S(1)}, u32[]{:S(2)}, u32[]{:S(2)}) collective-permute-start(f32[24,640]{1,0:T(8,128)S(1)} %get-tuple-element.36), channel_id=1, source_target_pairs={{0,1},{1,0},{2,3},{3,2},{4,5},{5,4},{6,7},{7,6},{8,9},{9,8},{10,11... | collective-permute-start | bytes 184328 | tf_op jit(solution)/shard_map/ppermute | solution.py:501
  9.7 7.1 %collective-permute-start.2 = (f32[24,640]{1,0:T(8,128)S(1)}, f32[24,640]{1,0:T(8,128)S(1)}, u32[]{:S(2)}, u32[]{:S(2)}) collective-permute-start(f32[24,640]{1,0:T(8,128)S(1)} %get-tuple-element.37), channel_id=1, source_target_pairs={{0,7},{1,2},{2,1},{3,4},{4,3},{5,6},{6,5},{7,0},{8,15},{9,10},{10,... | collective-permute-start | bytes 184328 | tf_op jit(solution)/shard_map/ppermute | solution.py:501
  15.3 4.4 %copy-start.2 = (f32[1,512,512]{2,1,0:T(8,128)S(1)}, f32[1,512,512]{2,1,0:T(8,128)}, u32[]{:S(2)}) copy-start(f32[1,512,512]{2,1,0:T(8,128)} %param.15) | copy-start | bytes 3145732
  15.3 4.4 %copy-start.6 = (bf16[256,144]{1,0:T(8,128)(2,1)S(1)}, bf16[256,144]{1,0:T(8,128)(2,1)}, u32[]{:S(2)}) copy-start(bf16[256,144]{1,0:T(8,128)(2,1)} %constant.29.refs_3_.both4) | copy-start | bytes 221188
  21.0 2.0 %collective-permute-start.3 = (f32[4,256,128]{2,1,0:T(8,128)S(1)}, f32[4,256,128]{2,1,0:T(8,128)S(1)}, u32[]{:S(2)}, u32[]{:S(2)}) collective-permute-start(f32[4,256,128]{2,1,0:T(8,128)S(1)} %get-tuple-element.40), channel_id=1, source_target_pairs={{0,16},{16,0},{1,17},{17,1},{2,18},{18,2},{3,19},{19,3},{4,20},{20... | collective-permute-start | bytes 1572872 | tf_op jit(solution)/shard_map/ppermute | solution.py:512
  22.4 7.8 %collective-permute-start.8 = (f32[4,256,128]{2,1,0:T(8,128)S(1)}, f32[4,256,128]{2,1,0:T(8,128)S(1)}, u32[]{:S(2)}, u32[]{:S(2)}) collective-permute-start(f32[4,256,128]{2,1,0:T(8,128)S(1)} %get-tuple-element.46), channel_id=1, source_target_pairs={{0,16},{16,0},{1,17},{17,1},{2,18},{18,2},{3,19},{19,3},{4,20},{20... | collective-permute-start | bytes 1572872 | tf_op jit(solution)/shard_map/ppermute | solution.py:512
  23.1 7.7 %collective-permute-start.4 = (f32[256,128]{1,0:T(8,128)S(1)}, f32[256,128]{1,0:T(8,128)S(1)}, u32[]{:S(2)}, u32[]{:S(2)}) collective-permute-start(f32[256,128]{1,0:T(8,128)S(1)} %get-tuple-element.41), channel_id=1, source_target_pairs={{0,32},{32,0},{64,96},{96,64},{128,160},{160,128},{192,224},{224,1... | collective-permute-start | bytes 393224 | tf_op jit(solution)/shard_map/ppermute | solution.py:508
  24.3 10.5 %collective-permute-start.5 = (f32[256,128]{1,0:T(8,128)S(1)}, f32[256,128]{1,0:T(8,128)S(1)}, u32[]{:S(2)}, u32[]{:S(2)}) collective-permute-start(f32[256,128]{1,0:T(8,128)S(1)} %get-tuple-element.42), channel_id=1, source_target_pairs={{0,96},{32,64},{64,32},{96,0},{128,224},{160,192},{192,160},{224,1... | collective-permute-start | bytes 393224 | tf_op jit(solution)/shard_map/ppermute | solution.py:508
  26.2 11.9 %collective-permute-start.6 = (f32[256,128]{1,0:T(8,128)S(1)}, f32[256,128]{1,0:T(8,128)S(1)}, u32[]{:S(2)}, u32[]{:S(2)}) collective-permute-start(f32[256,128]{1,0:T(8,128)S(1)} %get-tuple-element.43), channel_id=1, source_target_pairs={{0,160},{32,128},{64,224},{96,192},{128,32},{160,0},{192,96},{224,... | collective-permute-start | bytes 393224 | tf_op jit(solution)/shard_map/ppermute | solution.py:508
  29.7 10.4 %collective-permute-start.7 = (f32[256,128]{1,0:T(8,128)S(1)}, f32[256,128]{1,0:T(8,128)S(1)}, u32[]{:S(2)}, u32[]{:S(2)}) collective-permute-start(f32[256,128]{1,0:T(8,128)S(1)} %get-tuple-element.44), channel_id=1, source_target_pairs={{0,224},{32,192},{64,160},{96,128},{128,96},{160,64},{192,32},{224... | collective-permute-start | bytes 393224 | tf_op jit(solution)/shard_map/ppermute | solution.py:508
  30.3 9.8 %collective-permute-start.9 = (f32[256,128]{1,0:T(8,128)S(1)}, f32[256,128]{1,0:T(8,128)S(1)}, u32[]{:S(2)}, u32[]{:S(2)}) collective-permute-start(f32[256,128]{1,0:T(8,128)S(1)} %get-tuple-element.48), channel_id=1, source_target_pairs={{0,64},{32,96},{64,0},{96,32},{128,192},{160,224},{192,128},{224,1... | collective-permute-start | bytes 393224 | tf_op jit(solution)/shard_map/ppermute | solution.py:508
  30.7 12.0 %collective-permute-start.10 = (f32[256,128]{1,0:T(8,128)S(1)}, f32[256,128]{1,0:T(8,128)S(1)}, u32[]{:S(2)}, u32[]{:S(2)}) collective-permute-start(f32[256,128]{1,0:T(8,128)S(1)} %get-tuple-element.49), channel_id=1, source_target_pairs={{0,128},{32,160},{64,192},{96,224},{128,0},{160,32},{192,64},{224,... | collective-permute-start | bytes 393224 | tf_op jit(solution)/shard_map/ppermute | solution.py:508
  34.8 10.6 %collective-permute-start.11 = (f32[256,128]{1,0:T(8,128)S(1)}, f32[256,128]{1,0:T(8,128)S(1)}, u32[]{:S(2)}, u32[]{:S(2)}) collective-permute-start(f32[256,128]{1,0:T(8,128)S(1)} %get-tuple-element.50), channel_id=1, source_target_pairs={{0,192},{32,224},{64,128},{96,160},{128,64},{160,96},{192,0},{224,... | collective-permute-start | bytes 393224 | tf_op jit(solution)/shard_map/ppermute | solution.py:508
  45.5 9.1 %collective-permute-start.18 = (f32[256,128]{1,0:T(8,128)S(1)}, f32[256,128]{1,0:T(8,128)S(1)}, u32[]{:S(2)}, u32[]{:S(2)}) collective-permute-start(f32[256,128]{1,0:T(8,128)S(1)} %shard_map.137.refs_0_), channel_id=1, source_target_pairs={{0,224},{32,192},{64,160},{96,128},{128,96},{160,64},{192,32},{224... | collective-permute-start | bytes 393224 | tf_op jit(solution)/shard_map/ppermute | solution.py:508
  47.3 9.1 %collective-permute-start.17 = (f32[256,128]{1,0:T(8,128)S(1)}, f32[256,128]{1,0:T(8,128)S(1)}, u32[]{:S(2)}, u32[]{:S(2)}) collective-permute-start(f32[256,128]{1,0:T(8,128)S(1)} %shard_map.137.refs_0_), channel_id=1, source_target_pairs={{0,160},{32,128},{64,224},{96,192},{128,32},{160,0},{192,96},{224,... | collective-permute-start | bytes 393224 | tf_op jit(solution)/shard_map/ppermute | solution.py:508
  49.2 9.4 %collective-permute-start.16 = (f32[256,128]{1,0:T(8,128)S(1)}, f32[256,128]{1,0:T(8,128)S(1)}, u32[]{:S(2)}, u32[]{:S(2)}) collective-permute-start(f32[256,128]{1,0:T(8,128)S(1)} %shard_map.137.refs_0_), channel_id=1, source_target_pairs={{0,96},{32,64},{64,32},{96,0},{128,224},{160,192},{192,160},{224,1... | collective-permute-start | bytes 393224 | tf_op jit(solution)/shard_map/ppermute | solution.py:508
  51.2 8.8 %collective-permute-start.15 = (f32[256,128]{1,0:T(8,128)S(1)}, f32[256,128]{1,0:T(8,128)S(1)}, u32[]{:S(2)}, u32[]{:S(2)}) collective-permute-start(f32[256,128]{1,0:T(8,128)S(1)} %shard_map.137.refs_0_), channel_id=1, source_target_pairs={{0,32},{32,0},{64,96},{96,64},{128,160},{160,128},{192,224},{224,1... | collective-permute-start | bytes 393224 | tf_op jit(solution)/shard_map/ppermute | solution.py:508
  52.1 8.6 %collective-permute-start.14 = (f32[256,128]{1,0:T(8,128)S(1)}, f32[256,128]{1,0:T(8,128)S(1)}, u32[]{:S(2)}, u32[]{:S(2)}) collective-permute-start(f32[256,128]{1,0:T(8,128)S(1)} %shard_map.137.refs_0_), channel_id=1, source_target_pairs={{0,192},{32,224},{64,128},{96,160},{128,64},{160,96},{192,0},{224,... | collective-permute-start | bytes 393224 | tf_op jit(solution)/shard_map/ppermute | solution.py:508
  54.6 7.9 %collective-permute-start.13 = (f32[256,128]{1,0:T(8,128)S(1)}, f32[256,128]{1,0:T(8,128)S(1)}, u32[]{:S(2)}, u32[]{:S(2)}) collective-permute-start(f32[256,128]{1,0:T(8,128)S(1)} %shard_map.137.refs_0_), channel_id=1, source_target_pairs={{0,128},{32,160},{64,192},{96,224},{128,0},{160,32},{192,64},{224,... | collective-permute-start | bytes 393224 | tf_op jit(solution)/shard_map/ppermute | solution.py:508
  56.4 6.6 %collective-permute-start.12 = (f32[256,128]{1,0:T(8,128)S(1)}, f32[256,128]{1,0:T(8,128)S(1)}, u32[]{:S(2)}, u32[]{:S(2)}) collective-permute-start(f32[256,128]{1,0:T(8,128)S(1)} %shard_map.137.refs_0_), channel_id=1, source_target_pairs={{0,64},{32,96},{64,0},{96,32},{128,192},{160,224},{192,128},{224,1... | collective-permute-start | bytes 393224 | tf_op jit(solution)/shard_map/ppermute | solution.py:508
  63.1 2.0 %collective-permute-start.19 = (f32[4,256,128]{2,1,0:T(8,128)S(1)}, f32[4,256,128]{2,1,0:T(8,128)S(1)}, u32[]{:S(2)}, u32[]{:S(2)}) collective-permute-start(f32[4,256,128]{2,1,0:T(8,128)S(1)} %shard_map.139.even), channel_id=1, source_target_pairs={{0,16},{16,0},{1,17},{17,1},{2,18},{18,2},{3,19},{19,3},{4,20},{20... | collective-permute-start | bytes 1572872 | tf_op jit(solution)/shard_map/ppermute | solution.py:512
  63.2 2.6 %collective-permute-start.20 = (f32[4,256,128]{2,1,0:T(8,128)S(1)}, f32[4,256,128]{2,1,0:T(8,128)S(1)}, u32[]{:S(2)}, u32[]{:S(2)}) collective-permute-start(f32[4,256,128]{2,1,0:T(8,128)S(1)} %shard_map.138.refs_4_.odd), channel_id=1, source_target_pairs={{0,16},{16,0},{1,17},{17,1},{2,18},{18,2},{3,19},{19,3},{4,20},{20... | collective-permute-start | bytes 1572872 | tf_op jit(solution)/shard_map/ppermute | solution.py:512
  66.2 5.5 %collective-permute-start.21 = (f32[16,512]{1,0:T(8,128)S(1)}, f32[16,512]{1,0:T(8,128)S(1)}, u32[]{:S(2)}, u32[]{:S(2)}) collective-permute-start(f32[16,512]{1,0:T(8,128)S(1)} %shard_map.142), channel_id=1, source_target_pairs={{0,8},{8,0},{1,9},{9,1},{2,10},{10,2},{3,11},{11,3},{4,12},{12,4},... | collective-permute-start | bytes 98312 | tf_op jit(solution)/shard_map/ppermute | solution.py:494
  71.9 5.7 %collective-permute-start.22 = (f32[16,640]{1,0:T(8,128)S(1)}, f32[16,640]{1,0:T(8,128)S(1)}, u32[]{:S(2)}, u32[]{:S(2)}) collective-permute-start(f32[16,640]{1,0:T(8,128)S(1)} %get-tuple-element.60), channel_id=1, source_target_pairs={{0,1},{1,0},{2,3},{3,2},{4,5},{5,4},{6,7},{7,6},{8,9},{9,8},{10,11... | collective-permute-start | bytes 122888 | tf_op jit(solution)/shard_map/ppermute | solution.py:501
  72.0 5.6 %collective-permute-start.23 = (f32[16,640]{1,0:T(8,128)S(1)}, f32[16,640]{1,0:T(8,128)S(1)}, u32[]{:S(2)}, u32[]{:S(2)}) collective-permute-start(f32[16,640]{1,0:T(8,128)S(1)} %get-tuple-element.61), channel_id=1, source_target_pairs={{0,7},{1,2},{2,1},{3,4},{4,3},{5,6},{6,5},{7,0},{8,15},{9,10},{10,... | collective-permute-start | bytes 122888 | tf_op jit(solution)/shard_map/ppermute | solution.py:501
  75.3 2.3 %copy-start.7 = (bf16[2,48,48]{2,1,0:T(8,128)(2,1)S(1)}, bf16[2,48,48]{2,1,0:T(8,128)(2,1)}, u32[]{:S(2)}) copy-start(bf16[2,48,48]{2,1,0:T(8,128)(2,1)} %constant.23.clone.dl) | copy-start | bytes 27652
  75.3 2.3 %copy-start.8 = (bf16[2,48,48]{2,1,0:T(8,128)(2,1)S(1)}, bf16[2,48,48]{2,1,0:T(8,128)(2,1)}, u32[]{:S(2)}) copy-start(bf16[2,48,48]{2,1,0:T(8,128)(2,1)} %constant.22.clone.dh) | copy-start | bytes 27652
